TPU v7x, 256 devices: a whole 4x4x8 slice. The times are simulated.
256 devices in a mesh: leaf: 64 (over z, y, core), cols: 4 (over x).
Axes of the slice: x: 4, y: 4, z: 8, core: 2. Of those that a mesh axis runs over, the one named last changes fastest.
Arguments:
- points: bfloat16 [262144, 64], P('leaf', 'cols'), may hold values from -6 to 6
- weights: bfloat16 [262144, 1024], P('leaf', 'cols'), may hold values from -6 to 6
- leaf_basis: bfloat16 [65536, 1024], P('leaf'), may hold values from -0.1875 to 0.1875
- dev_transfer: bfloat16 [16384, 1024], P('leaf'), may hold values from -0.1875 to 0.1875
- group_transfer: bfloat16 [4096, 1024], P('leaf'), may hold values from -0.1875 to 0.1875
- leaf_skeleton: int32 [256, 256], P('leaf'), may hold values from 0 to 1023, as said below
- dev_skeleton: int32 [64, 256], P('leaf'), may hold values from 0 to 1023, as said below
- group_skeleton: int32 [16, 256], replicated, may hold values from 0 to 1023, as said below
- near_list: int32 [256, 3], P('leaf'), may hold values from 0 to 255, as said below
- near_count: int32 [256], P('leaf'), may hold values from 1 to 3
Outputs:
- potentials: float32 [262144, 1024], P('leaf', 'cols')
Inputs may be any that keep to these rules, and one draw needn't show every extreme that they name: `leaf_skeleton`: each row holds 256 distinct point numbers within the leaf. `dev_skeleton`: each row holds 256 distinct numbers into the 1024 skeleton points of the node's children, in child order. `group_skeleton`: each row holds 256 distinct numbers into the 1024 skeleton points of the node's children, in child order. `near_list`: row l names leaves of the first-level node holding leaf l and of the first-level nodes just before and after it; its first entry is l itself and its first near_count[l] entries are distinct; later entries are leaf numbers that are not used.
All inputs are finite; a program needn't handle non-finite values.
Results may differ from a plain program's by a relative error of at most 0.005.
Values may be sent and summed in bfloat16 or wider, within the bound.
No kernel may reach another device: no remote copies, remote signals or barrier semaphores. Data moves between devices by JAX's collectives and lax.ppermute only.
A program may use at most 128 MiB of HBM per device.

v0:
```python
import functools

import jax
import jax.numpy as jnp
from jax import lax
from jax.experimental import pallas as pl
from jax.experimental.pallas import tpu as pltpu
from jax.sharding import PartitionSpec as P

LEAF = 1024
RANK = 256
SHARPNESS = 2.0
LOG2E = 1.4426950408889634
BF = jnp.bfloat16
F32 = jnp.float32


VMEM = pl.BlockSpec(memory_space=pltpu.VMEM)
SMEM = pl.BlockSpec(memory_space=pltpu.SMEM)


def mm(a, b):
    return lax.dot_general(a, b, (((1,), (0,)), ((), ())), preferred_element_type=F32)


def mm_nt(a, b):
    return lax.dot_general(a, b, (((1,), (1,)), ((), ())), preferred_element_type=F32)


def mm_tn(a, b):
    return lax.dot_general(a, b, (((0,), (0,)), ((), ())), preferred_element_type=F32)


def call(body, outs, in_specs, scratch=(), flops=0, exps=0, nbytes=0, vmem=8):
    return pl.pallas_call(
        body,
        out_shape=[jax.ShapeDtypeStruct(s, d) for s, d in outs],
        in_specs=in_specs,
        out_specs=[VMEM] * len(outs),
        scratch_shapes=list(scratch),
        cost_estimate=pl.CostEstimate(flops=flops, transcendentals=exps, bytes_accessed=nbytes),
        compiler_params=pltpu.CompilerParams(vmem_limit_bytes=vmem * 1024 * 1024),
    )


def one_hot(index_row, rows):
    numbers = lax.broadcasted_iota(jnp.int32, (rows, index_row.shape[1]), 0)
    return jnp.where(numbers == index_row, 1.0, 0.0).astype(BF)


def tails(coords_t):
    wide = coords_t.astype(F32)
    half = -0.5 * jnp.sum(wide * wide, axis=0, keepdims=True)
    high = half.astype(BF).astype(F32)
    rest = half - high
    mid = rest.astype(BF).astype(F32)
    low = rest - mid
    row = lax.broadcasted_iota(jnp.int32, (16, coords_t.shape[1]), 0)

    def pieces(base, ones):
        out = jnp.where((row >= ones) & (row < ones + 3), 1.0, 0.0)
        out = jnp.where(row == base, high, out)
        out = jnp.where(row == base + 1, mid, out)
        return jnp.where(row == base + 2, low, out)

    return pieces(3, 0), pieces(0, 3)


def right_form(coords_t):
    _, tail = tails(coords_t)
    n = coords_t.shape[1]
    return jnp.concatenate([coords_t, tail.astype(BF), jnp.zeros((48, n), BF)], axis=0)


def left_form(coords_t):
    tail, _ = tails(coords_t)
    n = coords_t.shape[1]
    wide = jnp.concatenate([coords_t.astype(F32), tail, jnp.zeros((48, n), F32)], axis=0)
    return wide.T.astype(BF)


def kernel_block(left, right, dim):
    scale = 2.0 * SHARPNESS / dim * LOG2E
    return jnp.exp2(mm(left, right) * scale).astype(BF)


def column_share(position):
    return (position % 4) ^ (2 * (position // 4 % 2))


def skel_body(weights, basis, transfer, leaf_skel, nodes, weights_in, basis_in, transfer_in, sems):
    def copies(leaf):
        rows = pl.ds(leaf * LEAF, LEAF)
        ranks = pl.ds(leaf * RANK, RANK)
        return (
            pltpu.make_async_copy(basis.at[ranks], basis_in.at[ranks], sems.at[leaf]),
            pltpu.make_async_copy(weights.at[rows], weights_in.at[rows], sems.at[4 + leaf]),
        )

    whole = pltpu.make_async_copy(transfer, transfer_in, sems.at[8])
    for leaf in range(4):
        for copy in copies(leaf):
            copy.start()
        if leaf == 0:
            whole.start()
    total = None
    for leaf in range(4):
        rows = slice(leaf * RANK, (leaf + 1) * RANK)
        for copy in copies(leaf):
            copy.wait()
        skel = mm(basis_in[rows, :], weights_in[leaf * LEAF : (leaf + 1) * LEAF, :]).astype(BF)
        leaf_skel[rows, :] = skel
        if leaf == 0:
            whole.wait()
        part = mm(transfer_in[:, rows], skel)
        total = part if total is None else total + part
    nodes[...] = total.T.astype(BF)


def select_body(
    p0, p1, p2, p3, leaf_skeleton, dev_skeleton, group_skeleton, nodes, coords, leaf_coords, k0, k1, k2, k3
):
    position = lax.axis_index("leaf")
    member, group, share = position % 4, position // 4, column_share(position)
    for n, part in enumerate((p0, p1, p2, p3)):
        coords[pl.ds(n * 16, 16), :] = part[...]
    for leaf in range(4):
        hot = one_hot(leaf_skeleton[pl.ds(leaf, 1), :], LEAF)
        picked = mm(coords[:, leaf * LEAF : (leaf + 1) * LEAF], hot)
        leaf_coords[:, leaf * RANK : (leaf + 1) * RANK] = picked.astype(BF)
    node_coords = mm(leaf_coords[...], one_hot(dev_skeleton[...], 4 * RANK)).astype(BF)
    chosen = group_skeleton[pl.ds(group, 1), :] - member * RANK
    group_coords = mm(node_coords, one_hot(chosen, RANK)).astype(BF)
    for flip, out in enumerate((k0, k1, k2, k3)):
        start = pl.multiple_of((share ^ flip) * 64, 64)
        out[0:64, :] = nodes[pl.ds(start, 64), :]
        out[64:128, :] = node_coords
        out[128:192, :] = group_coords


def forms_body(coords, left, right):
    for leaf in range(4):
        cols = slice(leaf * LEAF, (leaf + 1) * LEAF)
        value = coords[:, cols]
        left[cols, :] = left_form(value)
        right[:, cols] = right_form(value)


def leaf_field_body(dim, coords, leaf_skel, field):
    picked = [coords[:, leaf * RANK : (leaf + 1) * RANK] for leaf in range(4)]
    lefts = [left_form(value) for value in picked]
    rights = [right_form(value) for value in picked]
    for i in range(4):
        total = None
        for j in range(4):
            if i != j:
                part = mm(kernel_block(lefts[i], rights[j], dim), leaf_skel[j * RANK : (j + 1) * RANK, :])
                total = part if total is None else total + part
        field[i * RANK : (i + 1) * RANK, :] = total


def near_tile(out, left, right, weights, leaf, source, opening, dim, first=0):
    cols = pl.ds(pl.multiple_of(source * LEAF, LEAF), LEAF)
    for chunk in range(4):
        rows = pl.ds(pl.multiple_of(leaf * LEAF + chunk * 256, 256), 256)
        out_rows = pl.ds(pl.multiple_of((leaf - first) * LEAF + chunk * 256, 256), 256)
        block = kernel_block(left[rows, :], right[:, cols], dim)
        part = mm(block, weights[cols, :])
        if opening:
            out[out_rows, :] = part
        else:
            out[out_rows, :] += part


def near_own_body(dim, first, near_list, near_count, left, right, weights, out):
    base = lax.axis_index("leaf") * 4

    def leaf_step(leaf, carry):
        near_tile(out, left, right, weights, leaf, leaf, True, dim, first)

        def slot_step(slot, carry):
            source = near_list[leaf, slot] - base
            active = (slot < near_count[leaf]) & (source >= 0) & (source < 4)

            @pl.when(active)
            def _():
                near_tile(out, left, right, weights, leaf, source, False, dim, first)

            return carry

        return lax.fori_loop(1, 3, slot_step, carry)

    lax.fori_loop(first, first + out.shape[0] // LEAF, leaf_step, 0)


def near_far_body(dim, near_list, near_count, left, before, after, w_up, w_down, w_late, start_a, start_b, out, right):
    position = lax.axis_index("leaf")
    base = position * 4
    low = position % 2 == 0
    up_late = low & (position % 8 != 0)
    down_late = jnp.logical_not(low) & (position % 8 != 7)
    for leaf in range(4):
        cols = slice(leaf * LEAF, (leaf + 1) * LEAF)
        right[0, :, cols] = right_form(before[:, cols])
        right[1, :, cols] = right_form(after[:, cols])
    half = start_a.shape[0]
    out[:half, :] = start_a[...]
    out[half:, :] = start_b[...]

    def leaf_step(leaf, carry):
        def slot_step(slot, carry):
            source = near_list[leaf, slot] - base
            active = slot < near_count[leaf]
            behind = active & (source < 0) & (source >= -4)
            ahead = active & (source >= 4) & (source < 8)

            @pl.when(behind & up_late)
            def _():
                near_tile(out, left, right.at[0], w_late, leaf, source + 4, False, dim)

            @pl.when(behind & jnp.logical_not(up_late))
            def _():
                near_tile(out, left, right.at[0], w_up, leaf, source + 4, False, dim)

            @pl.when(ahead & down_late)
            def _():
                near_tile(out, left, right.at[1], w_late, leaf, source - 4, False, dim)

            @pl.when(ahead & jnp.logical_not(down_late))
            def _():
                near_tile(out, left, right.at[1], w_down, leaf, source - 4, False, dim)

            return carry

        return lax.fori_loop(1, 3, slot_step, carry)

    lax.fori_loop(0, 4, leaf_step, 0)


def group_body(r0, r1, r2, r3, g0, g1, g2, g3, packed, transfer):
    member = lax.axis_index("leaf") % 4
    for flip, part in enumerate((g0, g1, g2, g3)):
        rows = pl.ds(pl.multiple_of((member ^ flip) * 64, 64), 64)
        transfer[rows, :] = part[...]
    total, coords = None, None
    for flip, part in enumerate((r0, r1, r2, r3)):
        cols = pl.ds(pl.multiple_of((member ^ flip) * RANK, RANK), RANK)
        value = mm_nt(part[0:64, :], transfer[:, cols])
        picked = part[128:192, :].astype(F32)
        total = value if total is None else total + value
        coords = picked if coords is None else coords + picked
    packed[0:64, :] = total.astype(BF)
    packed[64:128, :] = coords.astype(BF)


def top_body(dim, own, other, s1, s2, s3, s4, s5, s6, s7, r0, r1, r2, r3, transfer, *outs):
    member = lax.axis_index("leaf") % 4
    own_left = left_form(own[64:128, :])
    top = None
    blocks = [(other, 0)] + [(ref, row) for ref in (s1, s2, s3, s4, s5, s6, s7) for row in (0, 128)]
    for ref, row in blocks:
        block = kernel_block(own_left, right_form(ref[row + 64 : row + 128, :]), dim)
        part = mm_nt(ref[row : row + 64, :], block)
        top = part if top is None else top + part
    top = top.astype(BF)
    nodes = (r0, r1, r2, r3)
    lefts = [left_form(node[64:128, :]) for node in nodes]
    rights = [right_form(node[64:128, :]) for node in nodes]
    for i in range(4):
        cols = pl.ds(pl.multiple_of((member ^ i) * RANK, RANK), RANK)
        total = mm(top, transfer[:, cols])
        for j in range(4):
            if i != j:
                total = total + mm(nodes[j][0:64, :], kernel_block(lefts[j], rights[i], dim))
        outs[i][...] = total.astype(BF)


def finish_body(t0, t1, t2, t3, transfer, basis, field, near, out, total):
    leaf = pl.program_id(0)
    share = column_share(lax.axis_index("leaf"))

    @pl.when(leaf == 0)
    def _():
        for flip, part in enumerate((t0, t1, t2, t3)):
            rows = pl.ds(pl.multiple_of((share ^ flip) * 64, 64), 64)
            total[rows, :] = part[...]
        node_total = total[...].astype(F32).T.astype(BF)
        total[...] = node_total

    ranks = pl.ds(pl.multiple_of(leaf * RANK, RANK), RANK)
    rows = pl.ds(pl.multiple_of(leaf * LEAF, LEAF), LEAF)
    leaf_total = (field[ranks, :] + mm_tn(transfer[:, ranks], total[...])).astype(BF)
    out[...] = near[rows, :] + mm_tn(basis[ranks, :], leaf_total)


def per_device(
    points,
    weights,
    leaf_basis,
    dev_transfer,
    group_transfer,
    leaf_skeleton,
    dev_skeleton,
    group_skeleton,
    near_list,
    near_count,
):
    count = lax.axis_size("leaf")
    cols_count = lax.axis_size("cols")
    dim = points.shape[1] * cols_count
    width = weights.shape[1]
    rows = points.shape[0]

    def moved(value, pairs, axis="leaf"):
        return lax.ppermute(value, axis, pairs)

    def flipped(value, flip):
        return moved(value, [(i, i ^ flip) for i in range(count)])

    def shifted(value, step):
        pairs = [(i, (i + step) % cols_count) for i in range(cols_count)]
        return moved(value, pairs, "cols")

    def raised(value, step):
        return moved(value, [(i, (i + 8 * step) % count) for i in range(count)])

    up = [(i, i + 1) for i in range(count - 1)]
    down = [(j, i) for i, j in up]
    shard = points.T
    parts = [shard] + [shifted(shard, step) for step in (1, 2, 3)]
    transfer_1 = flipped(group_transfer, 1)
    transfer_2 = flipped(group_transfer, 2)
    transfer_3 = flipped(transfer_2, 1)
    transfers = [group_transfer, transfer_1, transfer_2, transfer_3]
    is_late = lambda pair: pair[1] % 8 != (0 if pair[0] < pair[1] else 7) and pair[1] % 2 == (pair[0] > pair[1])
    w_up = moved(weights, [pair for pair in up if not is_late(pair)])
    w_down = moved(weights, [pair for pair in down if not is_late(pair)])
    w_late = moved(weights, [pair for pair in up + down if is_late(pair)])

    leaf_skel, nodes = call(
        skel_body,
        [((4 * RANK, width), BF), ((width, RANK), BF)],
        [pl.BlockSpec(memory_space=pl.ANY)] * 3,
        scratch=[
            pltpu.VMEM((rows, width), BF),
            pltpu.VMEM((4 * RANK, LEAF), BF),
            pltpu.VMEM((RANK, 4 * RANK), BF),
            pltpu.SemaphoreType.DMA((9,)),
        ],
        flops=2 * 5 * RANK * LEAF * width,
        nbytes=5 * 1024 * 1024,
        vmem=58,
    )(weights, leaf_basis, dev_transfer)
    coords, leaf_coords, *packs = call(
        select_body,
        [((dim, rows), BF), ((dim, 4 * RANK), BF)] + [((192, RANK), BF)] * 4,
        [VMEM] * 8,
        flops=2 * 64 * RANK * 5 * LEAF * 4,
        nbytes=1024 * 1024,
    )(*parts, leaf_skeleton, dev_skeleton, group_skeleton, nodes)
    family = [packs[0]] + [flipped(packs[flip], flip) for flip in (1, 2, 3)]

    group_skel, full_transfer = call(
        group_body,
        [((128, RANK), BF), ((RANK, 4 * RANK), BF)],
        [VMEM] * 8,
        flops=2 * 64 * RANK * LEAF * 4,
        nbytes=1024 * 1024,
    )(*family, *transfers)
    other = moved(group_skel, [(i, i // 8 * 8 + (3 - i % 8 // 2) * 2 + i % 2) for i in range(count)])
    pair = jnp.concatenate([group_skel, other], axis=0)
    ring_u1, ring_d1 = raised(pair, 1), raised(pair, -1)
    ring_u2, ring_d2 = raised(ring_u1, 1), raised(ring_d1, -1)
    ring_u3, ring_d3 = raised(ring_u2, 1), raised(ring_d2, -1)
    ring_u4 = raised(ring_u3, 1)
    rings = (ring_u1, ring_d1, ring_u2, ring_d2, ring_u3, ring_d3, ring_u4)

    left, right = call(
        forms_body,
        [((rows, 128), BF), ((128, rows), BF)],
        [VMEM],
        flops=rows * 1024,
        nbytes=rows * 128 * 8,
        vmem=10,
    )(coords)
    before = moved(coords, up)
    after_coords = moved(coords, down)

    (leaf_field,) = call(
        functools.partial(leaf_field_body, dim),
        [((4 * RANK, width), F32)],
        [VMEM] * 2,
        flops=2 * 4 * RANK * 4 * RANK * 512,
        exps=4 * RANK * 4 * RANK,
        nbytes=2 * 1024 * 1024,
        vmem=12,
    )(leaf_coords, leaf_skel)

    tile_flops = 2 * LEAF * LEAF * 512
    near_parts = []
    for first in (0, 2):
        near_parts += call(
            functools.partial(near_own_body, dim, first),
            [((rows // 2, width), F32)],
            [SMEM, SMEM, VMEM, VMEM, VMEM],
            flops=5 * tile_flops // 2,
            exps=5 * LEAF * LEAF // 2,
            nbytes=6 * 1024 * 1024,
            vmem=16,
        )(near_list, near_count, left, right, weights)

    totals = call(
        functools.partial(top_body, dim),
        [((64, RANK), BF)] * 4,
        [VMEM] * 14,
        flops=2 * LEAF * LEAF * 512 * 2,
        exps=2 * LEAF * LEAF,
        nbytes=2 * 1024 * 1024,
        vmem=12,
    )(group_skel, other, *rings, *family, full_transfer)
    returned = [totals[0]] + [flipped(totals[flip], flip) for flip in (1, 2, 3)]

    (near_sum,) = call(
        functools.partial(near_far_body, dim),
        [((rows, width), F32)],
        [SMEM, SMEM] + [VMEM] * 8,
        scratch=[pltpu.VMEM((2, 128, rows), BF)],
        flops=7 * tile_flops,
        exps=7 * LEAF * LEAF,
        nbytes=12 * 1024 * 1024,
        vmem=24,
    )(near_list, near_count, left, before, after_coords, w_up, w_down, w_late, *near_parts)

    return pl.pallas_call(
        finish_body,
        grid=(4,),
        out_shape=jax.ShapeDtypeStruct((rows, width), F32),
        in_specs=[VMEM] * 8,
        out_specs=pl.BlockSpec((LEAF, width), lambda i: (i, 0)),
        scratch_shapes=[pltpu.VMEM((width, RANK), BF)],
        compiler_params=pltpu.CompilerParams(vmem_limit_bytes=12 * 1024 * 1024),
        cost_estimate=pl.CostEstimate(
            flops=2 * 5 * RANK * LEAF * width, transcendentals=0, bytes_accessed=10 * 1024 * 1024
        ),
        name="finish",
    )(*returned, dev_transfer, leaf_basis, leaf_field, near_sum)


def solution(mesh):
    in_specs = (
        P("leaf", "cols"),
        P("leaf", "cols"),
        P("leaf", None),
        P("leaf", None),
        P("leaf", None),
        P("leaf", None),
        P("leaf", None),
        P(),
        P("leaf", None),
        P("leaf"),
    )
    out_specs = P("leaf", "cols")
    return jax.shard_map(per_device, mesh=mesh, in_specs=in_specs, out_specs=out_specs, check_vma=False)
```

profile of v0, /device:TPU:97, one launch (start us, length us, event | category | flops | bytes accessed | tf_op | source)
XLA Modules:
  0.0 111.3 jit_solution(12207812532192678533)
XLA Ops:
  0.0 1.3 %collective-permute-start.22 = (bf16[4096,256]{1,0:T(8,128)(2,1)}, bf16[4096,256]{1,0:T(8,128)(2,1)S(1)}, u32[]{:S(2)}, u32[]{:S(2)}) collective-permute-start(bf16[4096,256]{1,0:T(8,128)(2,1)} %weights.5), channel_id=1, source_target_pairs={{0,4},{8,12},{16,20},{24,28},{28,32},{32,36},{40,44},{48,52},{56,6... | collective-permute-start | bytes 6291464 | tf_op jit(solution)/shard_map/ppermute | solution.py:315
  1.3 3.3 %collective-permute-start.23 = (bf16[4096,256]{1,0:T(8,128)(2,1)}, bf16[4096,256]{1,0:T(8,128)(2,1)S(1)}, u32[]{:S(2)}, u32[]{:S(2)}) collective-permute-start(bf16[4096,256]{1,0:T(8,128)(2,1)} %weights.5), channel_id=1, source_target_pairs={{4,0},{12,8},{20,16},{28,24},{32,28},{36,32},{44,40},{52,48},{60,5... | collective-permute-start | bytes 6291464 | tf_op jit(solution)/shard_map/ppermute | solution.py:315
  4.6 2.3 %collective-permute-start.24 = (bf16[4096,256]{1,0:T(8,128)(2,1)}, bf16[4096,256]{1,0:T(8,128)(2,1)}, u32[]{:S(2)}, u32[]{:S(2)}) collective-permute-start(bf16[4096,256]{1,0:T(8,128)(2,1)} %weights.5), channel_id=1, source_target_pairs={{4,8},{12,16},{20,24},{36,40},{44,48},{52,56},{68,72},{76,80},{84,... | collective-permute-start | bytes 6291464 | tf_op jit(solution)/shard_map/ppermute | solution.py:315
  7.0 1.3 %collective-permute-start = (bf16[16,4096]{1,0:T(8,128)(2,1)}, bf16[16,4096]{1,0:T(8,128)(2,1)S(1)}, u32[]{:S(2)}, u32[]{:S(2)}) collective-permute-start(bf16[16,4096]{1,0:T(8,128)(2,1)} %bitcast.1), channel_id=1, source_target_pairs={{0,1},{1,2},{2,3},{3,0},{4,5},{5,6},{6,7},{7,4},{8,9},{9,10},{10,1... | collective-permute-start | bytes 393224 | tf_op jit(solution)/shard_map/ppermute | solution.py:315
  8.3 2.5 %collective-permute-start.1 = (bf16[16,4096]{1,0:T(8,128)(2,1)}, bf16[16,4096]{1,0:T(8,128)(2,1)S(1)}, u32[]{:S(2)}, u32[]{:S(2)}) collective-permute-start(bf16[16,4096]{1,0:T(8,128)(2,1)} %bitcast.2), channel_id=1, source_target_pairs={{0,2},{1,3},{2,0},{3,1},{4,6},{5,7},{6,4},{7,5},{8,10},{9,11},{10,... | collective-permute-start | bytes 393224 | tf_op jit(solution)/shard_map/ppermute | solution.py:315
  10.7 1.9 %collective-permute-done.p1 = bf16[16,4096]{1,0:T(8,128)(2,1)S(1)} collective-permute-done((bf16[16,4096]{1,0:T(8,128)(2,1)}, bf16[16,4096]{1,0:T(8,128)(2,1)S(1)}, u32[]{:S(2)}, u32[]{:S(2)}) %collective-permute-start) | collective-permute-done | bytes 131104 | tf_op jit(solution)/shard_map/ppermute | solution.py:315
  12.6 1.3 %collective-permute-start.2 = (bf16[16,4096]{1,0:T(8,128)(2,1)}, bf16[16,4096]{1,0:T(8,128)(2,1)S(1)}, u32[]{:S(2)}, u32[]{:S(2)}) collective-permute-start(bf16[16,4096]{1,0:T(8,128)(2,1)} %bitcast.3), channel_id=1, source_target_pairs={{0,3},{1,0},{2,1},{3,2},{4,7},{5,4},{6,5},{7,6},{8,11},{9,8},{10,9... | collective-permute-start | bytes 393224 | tf_op jit(solution)/shard_map/ppermute | solution.py:315
  13.9 1.1 %collective-permute-done.1.p2 = bf16[16,4096]{1,0:T(8,128)(2,1)S(1)} collective-permute-done((bf16[16,4096]{1,0:T(8,128)(2,1)}, bf16[16,4096]{1,0:T(8,128)(2,1)S(1)}, u32[]{:S(2)}, u32[]{:S(2)}) %collective-permute-start.1) | collective-permute-done | bytes 131104 | tf_op jit(solution)/shard_map/ppermute | solution.py:315
  15.0 3.5 %collective-permute-start.7 = (bf16[64,1024]{1,0:T(8,128)(2,1)}, bf16[64,1024]{1,0:T(8,128)(2,1)S(1)}, u32[]{:S(2)}, u32[]{:S(2)}) collective-permute-start(bf16[64,1024]{1,0:T(8,128)(2,1)} %g0.1), channel_id=1, source_target_pairs={{0,8},{4,12},{8,0},{12,4},{16,24},{20,28},{24,16},{28,20},{32,40},... | collective-permute-start | bytes 393224 | tf_op jit(solution)/shard_map/ppermute | solution.py:315
  18.5 3.6 %collective-permute-start.6 = (bf16[64,1024]{1,0:T(8,128)(2,1)}, bf16[64,1024]{1,0:T(8,128)(2,1)S(1)}, u32[]{:S(2)}, u32[]{:S(2)}) collective-permute-start(bf16[64,1024]{1,0:T(8,128)(2,1)} %g0.1), channel_id=1, source_target_pairs={{0,4},{4,0},{8,12},{12,8},{16,20},{20,16},{24,28},{28,24},{32,36},... | collective-permute-start | bytes 393224 | tf_op jit(solution)/shard_map/ppermute | solution.py:315
  22.0 4.1 %shard_map.100 = (bf16[1024,256]{1,0:T(8,128)(2,1)}, bf16[256,256]{1,0:T(8,128)(2,1)}) custom-call(bf16[4096,256]{1,0:T(8,128)(2,1)} %weights.5, bf16[1024,1024]{1,0:T(8,128)(2,1)} %basis.3, bf16[256,1024]{1,0:T(8,128)(2,1)} %transfer.3), custom_call_target="tpu_custom_call" | custom-call | flops 671088640 | bytes 5242880 | tf_op jit(solution)/shard_map/pallas_call | solution.py:340
  26.2 0.0 copy-start.3
  26.2 0.9 copy-done.6
  27.2 0.8 shard_map.101
  27.9 5.1 %collective-permute-done.7.g2 = bf16[64,1024]{1,0:T(8,128)(2,1)S(1)} collective-permute-done((bf16[64,1024]{1,0:T(8,128)(2,1)}, bf16[64,1024]{1,0:T(8,128)(2,1)S(1)}, u32[]{:S(2)}, u32[]{:S(2)}) %collective-permute-start.7) | collective-permute-done | bytes 131104 | tf_op jit(solution)/shard_map/ppermute | solution.py:315
  33.0 2.7 %collective-permute-start.3 = (bf16[192,256]{1,0:T(8,128)(2,1)S(1)}, bf16[192,256]{1,0:T(8,128)(2,1)S(1)}, u32[]{:S(2)}, u32[]{:S(2)}) collective-permute-start(bf16[192,256]{1,0:T(8,128)(2,1)S(1)} %get-tuple-element.23), channel_id=1, source_target_pairs={{0,4},{4,0},{8,12},{12,8},{16,20},{20,16},{24,28},{28,24},{32,36},... | collective-permute-start | bytes 294920 | tf_op jit(solution)/shard_map/ppermute | solution.py:315
  35.7 0.9 collective-permute-done.3.r1
  36.7 0.4 collective-permute-start.8
  37.0 3.1 %collective-permute-done.4.r2 = bf16[192,256]{1,0:T(8,128)(2,1)S(1)} collective-permute-done((bf16[192,256]{1,0:T(8,128)(2,1)S(1)}, bf16[192,256]{1,0:T(8,128)(2,1)S(1)}, u32[]{:S(2)}, u32[]{:S(2)}) %collective-permute-start.4) | collective-permute-done | bytes 98336 | tf_op jit(solution)/shard_map/ppermute | solution.py:315
  40.1 0.7 collective-permute-start.5
  40.8 4.5 %collective-permute-done.5.r3 = bf16[192,256]{1,0:T(8,128)(2,1)S(1)} collective-permute-done((bf16[192,256]{1,0:T(8,128)(2,1)S(1)}, bf16[192,256]{1,0:T(8,128)(2,1)S(1)}, u32[]{:S(2)}, u32[]{:S(2)}) %collective-permute-start.5) | collective-permute-done | bytes 98336 | tf_op jit(solution)/shard_map/ppermute | solution.py:315
  45.3 0.3 shard_map.102
  45.6 1.8 %collective-permute-start.9 = (bf16[128,256]{1,0:T(8,128)(2,1)S(1)}, bf16[128,256]{1,0:T(8,128)(2,1)S(1)}, u32[]{:S(2)}, u32[]{:S(2)}) collective-permute-start(bf16[128,256]{1,0:T(8,128)(2,1)S(1)} %get-tuple-element.26.own), channel_id=1, source_target_pairs={{0,24},{4,28},{8,16},{12,20},{16,8},{20,12},{24,0},{28,4},{32,56},... | collective-permute-start | bytes 196616 | tf_op jit(solution)/shard_map/ppermute | solution.py:315
  47.4 2.6 %collective-permute-done.9.other = bf16[128,256]{1,0:T(8,128)(2,1)S(1)} collective-permute-done((bf16[128,256]{1,0:T(8,128)(2,1)S(1)}, bf16[128,256]{1,0:T(8,128)(2,1)S(1)}, u32[]{:S(2)}, u32[]{:S(2)}) %collective-permute-start.9) | collective-permute-done | bytes 65568 | tf_op jit(solution)/shard_map/ppermute | solution.py:315
  50.0 2.8 %collective-permute-start.10 = (bf16[256,256]{1,0:T(8,128)(2,1)S(1)}, bf16[256,256]{1,0:T(8,128)(2,1)S(1)}, u32[]{:S(2)}, u32[]{:S(2)}) collective-permute-start(bf16[256,256]{1,0:T(8,128)(2,1)S(1)} %constant_dynamic-update-slice_fusion), channel_id=1, source_target_pairs={{0,32},{4,36},{8,40},{12,44},{16,48},{20,52},{24,56},{28,60},{32,6... | collective-permute-start | bytes 393224 | tf_op jit(solution)/shard_map/ppermute | solution.py:315
  52.9 0.0 collective-permute-start.11
  52.9 1.9 %collective-permute-done.10.s1 = bf16[256,256]{1,0:T(8,128)(2,1)S(1)} collective-permute-done((bf16[256,256]{1,0:T(8,128)(2,1)S(1)}, bf16[256,256]{1,0:T(8,128)(2,1)S(1)}, u32[]{:S(2)}, u32[]{:S(2)}) %collective-permute-start.10) | collective-permute-done | bytes 131104 | tf_op jit(solution)/shard_map/ppermute | solution.py:315
  54.8 3.1 %collective-permute-start.12 = (bf16[256,256]{1,0:T(8,128)(2,1)S(1)}, bf16[256,256]{1,0:T(8,128)(2,1)S(1)}, u32[]{:S(2)}, u32[]{:S(2)}) collective-permute-start(bf16[256,256]{1,0:T(8,128)(2,1)S(1)} %collective-permute-done.10.s1), channel_id=1, source_target_pairs={{0,32},{4,36},{8,40},{12,44},{16,48},{20,52},{24,56},{28,60},{32,6... | collective-permute-start | bytes 393224 | tf_op jit(solution)/shard_map/ppermute | solution.py:315
  57.9 1.9 %collective-permute-done.12.s3 = bf16[256,256]{1,0:T(8,128)(2,1)S(1)} collective-permute-done((bf16[256,256]{1,0:T(8,128)(2,1)S(1)}, bf16[256,256]{1,0:T(8,128)(2,1)S(1)}, u32[]{:S(2)}, u32[]{:S(2)}) %collective-permute-start.12) | collective-permute-done | bytes 131104 | tf_op jit(solution)/shard_map/ppermute | solution.py:315
  59.9 3.1 %collective-permute-start.14 = (bf16[256,256]{1,0:T(8,128)(2,1)S(1)}, bf16[256,256]{1,0:T(8,128)(2,1)S(1)}, u32[]{:S(2)}, u32[]{:S(2)}) collective-permute-start(bf16[256,256]{1,0:T(8,128)(2,1)S(1)} %collective-permute-done.12.s3), channel_id=1, source_target_pairs={{0,32},{4,36},{8,40},{12,44},{16,48},{20,52},{24,56},{28,60},{32,6... | collective-permute-start | bytes 393224 | tf_op jit(solution)/shard_map/ppermute | solution.py:315
  62.9 0.4 shard_map.105
  63.3 0.0 collective-permute-done.13.s4
  63.4 0.1 collective-permute-start.15
  63.4 1.4 %collective-permute-done.14.s5 = bf16[256,256]{1,0:T(8,128)(2,1)S(1)} collective-permute-done((bf16[256,256]{1,0:T(8,128)(2,1)S(1)}, bf16[256,256]{1,0:T(8,128)(2,1)S(1)}, u32[]{:S(2)}, u32[]{:S(2)}) %collective-permute-start.14) | collective-permute-done | bytes 131104 | tf_op jit(solution)/shard_map/ppermute | solution.py:315
  64.9 3.1 %collective-permute-start.16 = (bf16[256,256]{1,0:T(8,128)(2,1)S(1)}, bf16[256,256]{1,0:T(8,128)(2,1)S(1)}, u32[]{:S(2)}, u32[]{:S(2)}) collective-permute-start(bf16[256,256]{1,0:T(8,128)(2,1)S(1)} %collective-permute-done.14.s5), channel_id=1, source_target_pairs={{0,32},{4,36},{8,40},{12,44},{16,48},{20,52},{24,56},{28,60},{32,6... | collective-permute-start | bytes 393224 | tf_op jit(solution)/shard_map/ppermute | solution.py:315
  68.0 4.8 %shard_map.106.start_a = f32[2048,256]{1,0:T(8,128)S(1)} custom-call(s32[4,3]{1,0:T(4,128)S(1)} %copy-done.9, s32[4]{0:T(128)S(1)} %copy-done.11, bf16[4096,128]{1,0:T(8,128)(2,1)S(1)} %get-tuple-element.35.left, bf16[128,4096]{1,0:T(8,128)(2,1)S(1)} %get-tuple-element.36.right, bf16[4096,256]{1,0:T(8,128)(2,1)S(1)} %copy-done.2), custom_call_target="tpu_custom_call" | custom-call | flops 2684354560 | bytes 6291456 | tf_op jit(solution)/shard_map/pallas_call | solution.py:402
  72.8 7.4 %collective-permute-start.20 = (bf16[64,4096]{1,0:T(8,128)(2,1)S(1)}, bf16[64,4096]{1,0:T(8,128)(2,1)S(1)}, u32[]{:S(2)}, u32[]{:S(2)}) collective-permute-start(bf16[64,4096]{1,0:T(8,128)(2,1)S(1)} %get-tuple-element.34.coords), channel_id=1, source_target_pairs={{0,4},{4,8},{8,12},{12,16},{16,20},{20,24},{24,28},{28,32},{32,36}... | collective-permute-start | bytes 1572872 | tf_op jit(solution)/shard_map/ppermute | solution.py:315
  80.3 1.9 %collective-permute-start.21 = (bf16[64,4096]{1,0:T(8,128)(2,1)S(1)}, bf16[64,4096]{1,0:T(8,128)(2,1)S(1)}, u32[]{:S(2)}, u32[]{:S(2)}) collective-permute-start(bf16[64,4096]{1,0:T(8,128)(2,1)S(1)} %get-tuple-element.34.coords), channel_id=1, source_target_pairs={{4,0},{8,4},{12,8},{16,12},{20,16},{24,20},{28,24},{32,28},{36,32}... | collective-permute-start | bytes 1572872 | tf_op jit(solution)/shard_map/ppermute | solution.py:315
  82.2 1.3 %shard_map.104.field = f32[1024,256]{1,0:T(8,128)S(1)} custom-call(bf16[64,1024]{1,0:T(8,128)(2,1)S(1)} %get-tuple-element.32.coords, bf16[1024,256]{1,0:T(8,128)(2,1)S(1)} %copy-done.4), custom_call_target="tpu_custom_call" | custom-call | flops 1073741824 | bytes 2097152 | tf_op jit(solution)/shard_map/pallas_call | solution.py:389
  83.5 3.4 %shard_map.107.start_b = f32[2048,256]{1,0:T(8,128)S(1)} custom-call(s32[4,3]{1,0:T(4,128)S(1)} %copy-done.9, s32[4]{0:T(128)S(1)} %copy-done.11, bf16[4096,128]{1,0:T(8,128)(2,1)S(1)} %get-tuple-element.35.left, bf16[128,4096]{1,0:T(8,128)(2,1)S(1)} %get-tuple-element.36.right, bf16[4096,256]{1,0:T(8,128)(2,1)S(1)} %copy-done.2), custom_call_target="tpu_custom_call" | custom-call | flops 2684354560 | bytes 6291456 | tf_op jit(solution)/shard_map/pallas_call | solution.py:402
  87.0 3.3 %shard_map.103 = (bf16[64,256]{1,0:T(8,128)(2,1)S(1)}, bf16[64,256]{1,0:T(8,128)(2,1)S(1)}, bf16[64,256]{1,0:T(8,128)(2,1)S(1)}, bf16[64,256]{1,0:T(8,128)(2,1)S(1)}) custom-call(bf16[128,256]{1,0:T(8,128)(2,1)S(1)} %get-tuple-element.26.own, bf16[128,256]{1,0:T(8,128)(2,1)S(1)} %collective-permute-done.9.other, ...), custom_call_target="tpu_custom_call" | custom-call | flops 2147483648 | bytes 2097152 | tf_op jit(solution)/shard_map/pallas_call | solution.py:412
  90.3 0.0 collective-permute-done.20.before
  90.3 4.7 %collective-permute-start.17 = (bf16[64,256]{1,0:T(8,128)(2,1)S(1)}, bf16[64,256]{1,0:T(8,128)(2,1)S(1)}, u32[]{:S(2)}, u32[]{:S(2)}) collective-permute-start(bf16[64,256]{1,0:T(8,128)(2,1)S(1)} %get-tuple-element.29), channel_id=1, source_target_pairs={{0,4},{4,0},{8,12},{12,8},{16,20},{20,16},{24,28},{28,24},{32,36},... | collective-permute-start | bytes 98312 | tf_op jit(solution)/shard_map/ppermute | solution.py:315
  95.0 0.0 copy-start
  95.0 0.0 copy-start.1
  95.0 1.7 %collective-permute-start.19 = (bf16[64,256]{1,0:T(8,128)(2,1)S(1)}, bf16[64,256]{1,0:T(8,128)(2,1)S(1)}, u32[]{:S(2)}, u32[]{:S(2)}) collective-permute-start(bf16[64,256]{1,0:T(8,128)(2,1)S(1)} %get-tuple-element.31), channel_id=1, source_target_pairs={{0,12},{4,8},{8,4},{12,0},{16,28},{20,24},{24,20},{28,16},{32,44},... | collective-permute-start | bytes 98312 | tf_op jit(solution)/shard_map/ppermute | solution.py:315
  96.8 10.7 %shard_map.108.near = f32[4096,256]{1,0:T(8,128)S(1)} custom-call(s32[4,3]{1,0:T(4,128)S(1)} %copy-done.9, s32[4]{0:T(128)S(1)} %copy-done.11, bf16[4096,128]{1,0:T(8,128)(2,1)S(1)} %get-tuple-element.35.left, bf16[64,4096]{1,0:T(8,128)(2,1)S(1)} %collective-permute-done.20.before, bf16[64,4096]{1,0:T(8,128)(2,1)S(1)} %collective-permute-done.21.after, ...), custom_call_target="tpu_custom_call" | custom-call | flops 7516192768 | bytes 12582912 | tf_op jit(solution)/shard_map/pallas_call | solution.py:423
  107.5 3.8 %finish.1 = f32[4096,256]{1,0:T(8,128)} custom-call(bf16[64,256]{1,0:T(8,128)(2,1)S(1)} %get-tuple-element.28.t0, bf16[64,256]{1,0:T(8,128)(2,1)S(1)} %collective-permute-done.17.t1, bf16[64,256]{1,0:T(8,128)(2,1)S(1)} %collective-permute-done.18.t2, bf16[64,256]{1,0:T(8,128)(2,1)S(1)} %collective-permute-done.19.t3, bf16[256,1024]{1,0:T(8,128)(2,1)S(1)} %copy-done.1, ...), custom_call_target="tpu_custom_call" | custom-call | flops 671088640 | bytes 10485760 | tf_op jit(solution)/shard_map/finish/pallas_call | solution.py:434
  (38 shorter events, 0.1 us)
Async XLA Ops:
  0.0 95.0 %collective-permute-start.22 = (bf16[4096,256]{1,0:T(8,128)(2,1)}, bf16[4096,256]{1,0:T(8,128)(2,1)S(1)}, u32[]{:S(2)}, u32[]{:S(2)}) collective-permute-start(bf16[4096,256]{1,0:T(8,128)(2,1)} %weights.5), channel_id=1, source_target_pairs={{0,4},{8,12},{16,20},{24,28},{28,32},{32,36},{40,44},{48,52},{56,6... | collective-permute-start | bytes 6291464 | tf_op jit(solution)/shard_map/ppermute | solution.py:315
  1.3 95.5 %collective-permute-start.23 = (bf16[4096,256]{1,0:T(8,128)(2,1)}, bf16[4096,256]{1,0:T(8,128)(2,1)S(1)}, u32[]{:S(2)}, u32[]{:S(2)}) collective-permute-start(bf16[4096,256]{1,0:T(8,128)(2,1)} %weights.5), channel_id=1, source_target_pairs={{4,0},{12,8},{20,16},{28,24},{32,28},{36,32},{44,40},{52,48},{60,5... | collective-permute-start | bytes 6291464 | tf_op jit(solution)/shard_map/ppermute | solution.py:315
  4.6 92.1 %collective-permute-start.24 = (bf16[4096,256]{1,0:T(8,128)(2,1)}, bf16[4096,256]{1,0:T(8,128)(2,1)}, u32[]{:S(2)}, u32[]{:S(2)}) collective-permute-start(bf16[4096,256]{1,0:T(8,128)(2,1)} %weights.5), channel_id=1, source_target_pairs={{4,8},{12,16},{20,24},{36,40},{44,48},{52,56},{68,72},{76,80},{84,... | collective-permute-start | bytes 6291464 | tf_op jit(solution)/shard_map/ppermute | solution.py:315
  6.9 19.2 %copy-start.5 = (bf16[4096,16]{0,1:T(8,128)(2,1)S(1)}, bf16[4096,16]{0,1:T(8,128)(2,1)}, u32[]{:S(2)}) copy-start(bf16[4096,16]{0,1:T(8,128)(2,1)} %param.10) | copy-start | bytes 393220
  7.0 19.2 %copy-start.7 = (s32[16,256]{1,0:T(8,128)S(1)}, s32[16,256]{1,0:T(8,128)}, u32[]{:S(2)}) copy-start(s32[16,256]{1,0:T(8,128)} %group_skeleton.1) | copy-start | bytes 49156
  7.0 19.2 %copy-start.8 = (s32[4,256]{1,0:T(4,128)S(1)}, s32[4,256]{1,0:T(4,128)}, u32[]{:S(2)}) copy-start(s32[4,256]{1,0:T(4,128)} %leaf_skeleton.1) | copy-start | bytes 12292
  7.0 19.2 %copy-start.10 = (s32[1,256]{1,0:T(1,128)S(1)}, s32[1,256]{1,0:T(1,128)}, u32[]{:S(2)}) copy-start(s32[1,256]{1,0:T(1,128)} %dev_skeleton.1) | copy-start | bytes 3076
  7.0 5.6 %collective-permute-start = (bf16[16,4096]{1,0:T(8,128)(2,1)}, bf16[16,4096]{1,0:T(8,128)(2,1)S(1)}, u32[]{:S(2)}, u32[]{:S(2)}) collective-permute-start(bf16[16,4096]{1,0:T(8,128)(2,1)} %bitcast.1), channel_id=1, source_target_pairs={{0,1},{1,2},{2,3},{3,0},{4,5},{5,6},{6,7},{7,4},{8,9},{9,10},{10,1... | collective-permute-start | bytes 393224 | tf_op jit(solution)/shard_map/ppermute | solution.py:315
  8.3 6.7 %collective-permute-start.1 = (bf16[16,4096]{1,0:T(8,128)(2,1)}, bf16[16,4096]{1,0:T(8,128)(2,1)S(1)}, u32[]{:S(2)}, u32[]{:S(2)}) collective-permute-start(bf16[16,4096]{1,0:T(8,128)(2,1)} %bitcast.2), channel_id=1, source_target_pairs={{0,2},{1,3},{2,0},{3,1},{4,6},{5,7},{6,4},{7,5},{8,10},{9,11},{10,... | collective-permute-start | bytes 393224 | tf_op jit(solution)/shard_map/ppermute | solution.py:315
  12.6 5.9 %collective-permute-start.2 = (bf16[16,4096]{1,0:T(8,128)(2,1)}, bf16[16,4096]{1,0:T(8,128)(2,1)S(1)}, u32[]{:S(2)}, u32[]{:S(2)}) collective-permute-start(bf16[16,4096]{1,0:T(8,128)(2,1)} %bitcast.3), channel_id=1, source_target_pairs={{0,3},{1,0},{2,1},{3,2},{4,7},{5,4},{6,5},{7,6},{8,11},{9,8},{10,9... | collective-permute-start | bytes 393224 | tf_op jit(solution)/shard_map/ppermute | solution.py:315
  15.0 18.0 %collective-permute-start.7 = (bf16[64,1024]{1,0:T(8,128)(2,1)}, bf16[64,1024]{1,0:T(8,128)(2,1)S(1)}, u32[]{:S(2)}, u32[]{:S(2)}) collective-permute-start(bf16[64,1024]{1,0:T(8,128)(2,1)} %g0.1), channel_id=1, source_target_pairs={{0,8},{4,12},{8,0},{12,4},{16,24},{20,28},{24,16},{28,20},{32,40},... | collective-permute-start | bytes 393224 | tf_op jit(solution)/shard_map/ppermute | solution.py:315
  18.5 17.3 %collective-permute-start.6 = (bf16[64,1024]{1,0:T(8,128)(2,1)}, bf16[64,1024]{1,0:T(8,128)(2,1)S(1)}, u32[]{:S(2)}, u32[]{:S(2)}) collective-permute-start(bf16[64,1024]{1,0:T(8,128)(2,1)} %g0.1), channel_id=1, source_target_pairs={{0,4},{4,0},{8,12},{12,8},{16,20},{20,16},{24,28},{28,24},{32,36},... | collective-permute-start | bytes 393224 | tf_op jit(solution)/shard_map/ppermute | solution.py:315
  26.2 19.1 %copy-start.3 = (bf16[64,1024]{1,0:T(8,128)(2,1)S(1)}, bf16[64,1024]{1,0:T(8,128)(2,1)}, u32[]{:S(2)}) copy-start(bf16[64,1024]{1,0:T(8,128)(2,1)} %g0.1) | copy-start | bytes 393220
  26.2 0.9 copy-start.6
  27.2 40.8 %copy-start.2 = (bf16[4096,256]{1,0:T(8,128)(2,1)S(1)}, bf16[4096,256]{1,0:T(8,128)(2,1)}, u32[]{:S(2)}) copy-start(bf16[4096,256]{1,0:T(8,128)(2,1)} %weights.5) | copy-start | bytes 6291460
  27.2 40.8 %copy-start.9 = (s32[4,3]{1,0:T(4,128)S(1)}, s32[4,3]{1,0:T(4,128)}, u32[]{:S(2)}) copy-start(s32[4,3]{1,0:T(4,128)} %near_list.5) | copy-start | bytes 148
  27.2 40.8 %copy-start.11 = (s32[4]{0:T(128)S(1)}, s32[4]{0:T(128)}, u32[]{:S(2)}) copy-start(s32[4]{0:T(128)} %near_count.5) | copy-start | bytes 52
  33.0 3.6 %collective-permute-start.3 = (bf16[192,256]{1,0:T(8,128)(2,1)S(1)}, bf16[192,256]{1,0:T(8,128)(2,1)S(1)}, u32[]{:S(2)}, u32[]{:S(2)}) collective-permute-start(bf16[192,256]{1,0:T(8,128)(2,1)S(1)} %get-tuple-element.23), channel_id=1, source_target_pairs={{0,4},{4,0},{8,12},{12,8},{16,20},{20,16},{24,28},{28,24},{32,36},... | collective-permute-start | bytes 294920 | tf_op jit(solution)/shard_map/ppermute | solution.py:315
  35.7 4.3 %collective-permute-start.4 = (bf16[192,256]{1,0:T(8,128)(2,1)S(1)}, bf16[192,256]{1,0:T(8,128)(2,1)S(1)}, u32[]{:S(2)}, u32[]{:S(2)}) collective-permute-start(bf16[192,256]{1,0:T(8,128)(2,1)S(1)} %get-tuple-element.24), channel_id=1, source_target_pairs={{0,8},{4,12},{8,0},{12,4},{16,24},{20,28},{24,16},{28,20},{32,40},... | collective-permute-start | bytes 294920 | tf_op jit(solution)/shard_map/ppermute | solution.py:315
  36.7 8.6 %collective-permute-start.8 = (bf16[64,1024]{1,0:T(8,128)(2,1)S(1)}, bf16[64,1024]{1,0:T(8,128)(2,1)S(1)}, u32[]{:S(2)}, u32[]{:S(2)}) collective-permute-start(bf16[64,1024]{1,0:T(8,128)(2,1)S(1)} %collective-permute-done.7.g2), channel_id=1, source_target_pairs={{0,4},{4,0},{8,12},{12,8},{16,20},{20,16},{24,28},{28,24},{32,36},... | collective-permute-start | bytes 393224 | tf_op jit(solution)/shard_map/ppermute | solution.py:315
  40.1 5.2 %collective-permute-start.5 = (bf16[192,256]{1,0:T(8,128)(2,1)S(1)}, bf16[192,256]{1,0:T(8,128)(2,1)S(1)}, u32[]{:S(2)}, u32[]{:S(2)}) collective-permute-start(bf16[192,256]{1,0:T(8,128)(2,1)S(1)} %get-tuple-element.25), channel_id=1, source_target_pairs={{0,12},{4,8},{8,4},{12,0},{16,28},{20,24},{24,20},{28,16},{32,44},... | collective-permute-start | bytes 294920 | tf_op jit(solution)/shard_map/ppermute | solution.py:315
  45.6 4.4 %collective-permute-start.9 = (bf16[128,256]{1,0:T(8,128)(2,1)S(1)}, bf16[128,256]{1,0:T(8,128)(2,1)S(1)}, u32[]{:S(2)}, u32[]{:S(2)}) collective-permute-start(bf16[128,256]{1,0:T(8,128)(2,1)S(1)} %get-tuple-element.26.own), channel_id=1, source_target_pairs={{0,24},{4,28},{8,16},{12,20},{16,8},{20,12},{24,0},{28,4},{32,56},... | collective-permute-start | bytes 196616 | tf_op jit(solution)/shard_map/ppermute | solution.py:315
  50.0 4.8 %collective-permute-start.10 = (bf16[256,256]{1,0:T(8,128)(2,1)S(1)}, bf16[256,256]{1,0:T(8,128)(2,1)S(1)}, u32[]{:S(2)}, u32[]{:S(2)}) collective-permute-start(bf16[256,256]{1,0:T(8,128)(2,1)S(1)} %constant_dynamic-update-slice_fusion), channel_id=1, source_target_pairs={{0,32},{4,36},{8,40},{12,44},{16,48},{20,52},{24,56},{28,60},{32,6... | collective-permute-start | bytes 393224 | tf_op jit(solution)/shard_map/ppermute | solution.py:315
  52.9 5.0 %collective-permute-start.11 = (bf16[256,256]{1,0:T(8,128)(2,1)S(1)}, bf16[256,256]{1,0:T(8,128)(2,1)S(1)}, u32[]{:S(2)}, u32[]{:S(2)}) collective-permute-start(bf16[256,256]{1,0:T(8,128)(2,1)S(1)} %constant_dynamic-update-slice_fusion), channel_id=1, source_target_pairs={{0,224},{4,228},{8,232},{12,236},{16,240},{20,244},{24,248},{28,25... | collective-permute-start | bytes 393224 | tf_op jit(solution)/shard_map/ppermute | solution.py:315
  54.8 5.0 %collective-permute-start.12 = (bf16[256,256]{1,0:T(8,128)(2,1)S(1)}, bf16[256,256]{1,0:T(8,128)(2,1)S(1)}, u32[]{:S(2)}, u32[]{:S(2)}) collective-permute-start(bf16[256,256]{1,0:T(8,128)(2,1)S(1)} %collective-permute-done.10.s1), channel_id=1, source_target_pairs={{0,32},{4,36},{8,40},{12,44},{16,48},{20,52},{24,56},{28,60},{32,6... | collective-permute-start | bytes 393224 | tf_op jit(solution)/shard_map/ppermute | solution.py:315
  57.9 5.4 %collective-permute-start.13 = (bf16[256,256]{1,0:T(8,128)(2,1)S(1)}, bf16[256,256]{1,0:T(8,128)(2,1)S(1)}, u32[]{:S(2)}, u32[]{:S(2)}) collective-permute-start(bf16[256,256]{1,0:T(8,128)(2,1)S(1)} %collective-permute-done.11.s2), channel_id=1, source_target_pairs={{0,224},{4,228},{8,232},{12,236},{16,240},{20,244},{24,248},{28,25... | collective-permute-start | bytes 393224 | tf_op jit(solution)/shard_map/ppermute | solution.py:315
  59.9 5.0 %collective-permute-start.14 = (bf16[256,256]{1,0:T(8,128)(2,1)S(1)}, bf16[256,256]{1,0:T(8,128)(2,1)S(1)}, u32[]{:S(2)}, u32[]{:S(2)}) collective-permute-start(bf16[256,256]{1,0:T(8,128)(2,1)S(1)} %collective-permute-done.12.s3), channel_id=1, source_target_pairs={{0,32},{4,36},{8,40},{12,44},{16,48},{20,52},{24,56},{28,60},{32,6... | collective-permute-start | bytes 393224 | tf_op jit(solution)/shard_map/ppermute | solution.py:315
  63.4 9.5 %collective-permute-start.15 = (bf16[256,256]{1,0:T(8,128)(2,1)S(1)}, bf16[256,256]{1,0:T(8,128)(2,1)S(1)}, u32[]{:S(2)}, u32[]{:S(2)}) collective-permute-start(bf16[256,256]{1,0:T(8,128)(2,1)S(1)} %collective-permute-done.13.s4), channel_id=1, source_target_pairs={{0,224},{4,228},{8,232},{12,236},{16,240},{20,244},{24,248},{28,25... | collective-permute-start | bytes 393224 | tf_op jit(solution)/shard_map/ppermute | solution.py:315
  64.9 15.4 %collective-permute-start.16 = (bf16[256,256]{1,0:T(8,128)(2,1)S(1)}, bf16[256,256]{1,0:T(8,128)(2,1)S(1)}, u32[]{:S(2)}, u32[]{:S(2)}) collective-permute-start(bf16[256,256]{1,0:T(8,128)(2,1)S(1)} %collective-permute-done.14.s5), channel_id=1, source_target_pairs={{0,32},{4,36},{8,40},{12,44},{16,48},{20,52},{24,56},{28,60},{32,6... | collective-permute-start | bytes 393224 | tf_op jit(solution)/shard_map/ppermute | solution.py:315
  68.0 14.2 %copy-start.4 = (bf16[1024,256]{1,0:T(8,128)(2,1)S(1)}, bf16[1024,256]{1,0:T(8,128)(2,1)}, u32[]{:S(2)}) copy-start(bf16[1024,256]{1,0:T(8,128)(2,1)} %get-tuple-element.33.leaf_skel) | copy-start | bytes 1572868
  72.8 17.4 %collective-permute-start.20 = (bf16[64,4096]{1,0:T(8,128)(2,1)S(1)}, bf16[64,4096]{1,0:T(8,128)(2,1)S(1)}, u32[]{:S(2)}, u32[]{:S(2)}) collective-permute-start(bf16[64,4096]{1,0:T(8,128)(2,1)S(1)} %get-tuple-element.34.coords), channel_id=1, source_target_pairs={{0,4},{4,8},{8,12},{12,16},{16,20},{20,24},{24,28},{28,32},{32,36}... | collective-permute-start | bytes 1572872 | tf_op jit(solution)/shard_map/ppermute | solution.py:315
  80.3 14.7 %collective-permute-start.21 = (bf16[64,4096]{1,0:T(8,128)(2,1)S(1)}, bf16[64,4096]{1,0:T(8,128)(2,1)S(1)}, u32[]{:S(2)}, u32[]{:S(2)}) collective-permute-start(bf16[64,4096]{1,0:T(8,128)(2,1)S(1)} %get-tuple-element.34.coords), channel_id=1, source_target_pairs={{4,0},{8,4},{12,8},{16,12},{20,16},{24,20},{28,24},{32,28},{36,32}... | collective-permute-start | bytes 1572872 | tf_op jit(solution)/shard_map/ppermute | solution.py:315
  90.3 17.2 %collective-permute-start.17 = (bf16[64,256]{1,0:T(8,128)(2,1)S(1)}, bf16[64,256]{1,0:T(8,128)(2,1)S(1)}, u32[]{:S(2)}, u32[]{:S(2)}) collective-permute-start(bf16[64,256]{1,0:T(8,128)(2,1)S(1)} %get-tuple-element.29), channel_id=1, source_target_pairs={{0,4},{4,0},{8,12},{12,8},{16,20},{20,16},{24,28},{28,24},{32,36},... | collective-permute-start | bytes 98312 | tf_op jit(solution)/shard_map/ppermute | solution.py:315
  95.0 12.5 %collective-permute-start.18 = (bf16[64,256]{1,0:T(8,128)(2,1)S(1)}, bf16[64,256]{1,0:T(8,128)(2,1)S(1)}, u32[]{:S(2)}, u32[]{:S(2)}) collective-permute-start(bf16[64,256]{1,0:T(8,128)(2,1)S(1)} %get-tuple-element.30), channel_id=1, source_target_pairs={{0,8},{4,12},{8,0},{12,4},{16,24},{20,28},{24,16},{28,20},{32,40},... | collective-permute-start | bytes 98312 | tf_op jit(solution)/shard_map/ppermute | solution.py:315
  95.0 12.5 %copy-start = (bf16[1024,1024]{1,0:T(8,128)(2,1)S(1)}, bf16[1024,1024]{1,0:T(8,128)(2,1)}, u32[]{:S(2)}) copy-start(bf16[1024,1024]{1,0:T(8,128)(2,1)} %basis.3) | copy-start | bytes 6291460
  95.0 12.5 %copy-start.1 = (bf16[256,1024]{1,0:T(8,128)(2,1)S(1)}, bf16[256,1024]{1,0:T(8,128)(2,1)}, u32[]{:S(2)}) copy-start(bf16[256,1024]{1,0:T(8,128)(2,1)} %transfer.3) | copy-start | bytes 1572868
  95.0 12.5 %collective-permute-start.19 = (bf16[64,256]{1,0:T(8,128)(2,1)S(1)}, bf16[64,256]{1,0:T(8,128)(2,1)S(1)}, u32[]{:S(2)}, u32[]{:S(2)}) collective-permute-start(bf16[64,256]{1,0:T(8,128)(2,1)S(1)} %get-tuple-element.31), channel_id=1, source_target_pairs={{0,12},{4,8},{8,4},{12,0},{16,28},{20,24},{24,20},{28,16},{32,44},... | collective-permute-start | bytes 98312 | tf_op jit(solution)/shard_map/ppermute | solution.py:315
where the time goes:
time: 112 us; the launch traced here: 111 us
  starting transfers between devices  52.5 us (47%)
  Pallas kernels  33 us (29%)
  waiting for transfers between devices  24.5 us (22%)
    ppermute x25, starting transfers between devices, moved(): return lax.ppermute(value, axis, pairs)  52.5 us
    ppermute x25, waiting for transfers between devices, moved(): return lax.ppermute(value, axis, pairs)  24.5 us
    pallas_call x1, Pallas kernels, per_device(): call(functools.partial(near_far_body, dim), [((rows, width), F32)], [SMEM...  10.7 us
    pallas_call x2, Pallas kernels, per_device(): call(functools.partial(near_own_body, dim, first), [((rows // 2, width),...  8.28 us
    pallas_call x1, Pallas kernels, per_device(): call(skel_body, [((4 * RANK, width), BF), ((width, RANK), BF)], [pl.Block...  4.13 us
    pallas_call x1, Pallas kernels, per_device(): pl.pallas_call(finish_body, grid=(4,), out_shape=jax.ShapeDtypeStruct((ro...  3.81 us
    pallas_call x1, Pallas kernels, per_device(): call(functools.partial(top_body, dim), [((64, RANK), BF)] * 4, [VMEM] * 1...  3.31 us
  transfers between devices with their start and end apart: 25, of which 10 were waited for; matrix products, arithmetic and copies ran while one was open for 0% of the time, Pallas kernels for 26%

commit v1 on v0

--- a/solution.py
+++ b/solution.py
@@ -17,6 +17,7 @@
 
 VMEM = pl.BlockSpec(memory_space=pltpu.VMEM)
 SMEM = pl.BlockSpec(memory_space=pltpu.SMEM)
+HBM = pl.BlockSpec(memory_space=pltpu.HBM)
 
 
 def mm(a, b):
@@ -88,7 +89,17 @@
     return (position % 4) ^ (2 * (position // 4 % 2))
 
 
-def skel_body(weights, basis, transfer, leaf_skel, nodes, weights_in, basis_in, transfer_in, sems):
+def skel_body(
+    weights,
+    basis,
+    transfer,
+    leaf_skel,
+    nodes,
+    weights_in,
+    basis_in,
+    transfer_in,
+    sems,
+):
     def copies(leaf):
         rows = pl.ds(leaf * LEAF, LEAF)
         ranks = pl.ds(leaf * RANK, RANK)
@@ -117,19 +128,17 @@
     nodes[...] = total.T.astype(BF)
 
 
-def select_body(
-    p0, p1, p2, p3, leaf_skeleton, dev_skeleton, group_skeleton, nodes, coords, leaf_coords, k0, k1, k2, k3
-):
+def select_body(p0, p1, p2, p3, picks, nodes, coords, leaf_coords, k0, k1, k2, k3):
     position = lax.axis_index("leaf")
-    member, group, share = position % 4, position // 4, column_share(position)
+    share = column_share(position)
     for n, part in enumerate((p0, p1, p2, p3)):
         coords[pl.ds(n * 16, 16), :] = part[...]
     for leaf in range(4):
-        hot = one_hot(leaf_skeleton[pl.ds(leaf, 1), :], LEAF)
+        hot = one_hot(picks[leaf : leaf + 1, :], LEAF)
         picked = mm(coords[:, leaf * LEAF : (leaf + 1) * LEAF], hot)
         leaf_coords[:, leaf * RANK : (leaf + 1) * RANK] = picked.astype(BF)
-    node_coords = mm(leaf_coords[...], one_hot(dev_skeleton[...], 4 * RANK)).astype(BF)
-    chosen = group_skeleton[pl.ds(group, 1), :] - member * RANK
+    node_coords = mm(leaf_coords[...], one_hot(picks[4:5, :], 4 * RANK)).astype(BF)
+    chosen = picks[pl.ds(5 + position // 4, 1), :] - (position % 4) * RANK
     group_coords = mm(node_coords, one_hot(chosen, RANK)).astype(BF)
     for flip, out in enumerate((k0, k1, k2, k3)):
         start = pl.multiple_of((share ^ flip) * 64, 64)
@@ -159,76 +168,70 @@
         field[i * RANK : (i + 1) * RANK, :] = total
 
 
-def near_tile(out, left, right, weights, leaf, source, opening, dim, first=0):
+def near_tile(out, left, right, weights, leaf, out_leaf, source, weight_leaf, dim):
     cols = pl.ds(pl.multiple_of(source * LEAF, LEAF), LEAF)
+    weight_rows = pl.ds(pl.multiple_of(weight_leaf * LEAF, LEAF), LEAF)
     for chunk in range(4):
         rows = pl.ds(pl.multiple_of(leaf * LEAF + chunk * 256, 256), 256)
-        out_rows = pl.ds(pl.multiple_of((leaf - first) * LEAF + chunk * 256, 256), 256)
+        out_rows = pl.ds(pl.multiple_of(out_leaf * LEAF + chunk * 256, 256), 256)
         block = kernel_block(left[rows, :], right[:, cols], dim)
-        part = mm(block, weights[cols, :])
-        if opening:
-            out[out_rows, :] = part
-        else:
-            out[out_rows, :] += part
-
-
-def near_own_body(dim, first, near_list, near_count, left, right, weights, out):
+        out[out_rows, :] += mm(block, weights[weight_rows, :])
+
+
+def near_own_body(dim, leaf, near_list, near_count, left, right, weights, out):
     base = lax.axis_index("leaf") * 4
+    out[...] = jnp.zeros_like(out)
+
+    def slot_step(slot, carry):
+        source = near_list[leaf, slot] - base
+        active = (slot < near_count[leaf]) & (source >= 0) & (source < 4)
+
+        @pl.when(active)
+        def _():
+            near_tile(out, left, right, weights, leaf, 0, source, source, dim)
+
+        return carry
+
+    lax.fori_loop(0, 3, slot_step, 0)
+
+
+def near_neighbour_body(dim, inside, near_list, near_count, left, coords, *refs):
+    if inside:
+        weights, s0, s1, s2, s3, out, right = refs
+        for leaf, start in enumerate((s0, s1, s2, s3)):
+            out[leaf * LEAF : (leaf + 1) * LEAF, :] = start[...]
+    else:
+        weights_late, weights_cross, start, out, right, held = refs
+        out[...] = start[...]
+    position = lax.axis_index("leaf")
+    even = position % 2 == 0
+    edge = (position % 8 == 0) | (position % 8 == 7)
+    first = jnp.where(even if inside else jnp.logical_not(even), position + 1, position - 1) * 4
+    for leaf in range(4):
+        cols = slice(leaf * LEAF, (leaf + 1) * LEAF)
+        right[:, cols] = right_form(coords[:, cols])
 
     def leaf_step(leaf, carry):
-        near_tile(out, left, right, weights, leaf, leaf, True, dim, first)
-
         def slot_step(slot, carry):
-            source = near_list[leaf, slot] - base
+            source = near_list[leaf, slot] - first
             active = (slot < near_count[leaf]) & (source >= 0) & (source < 4)
+
+            if not inside:
+
+                @pl.when(active & edge)
+                def _():
+                    held[...] = weights_cross[pl.ds(pl.multiple_of(source * LEAF, LEAF), LEAF), :]
+
+                @pl.when(active & jnp.logical_not(edge))
+                def _():
+                    held[...] = weights_late[pl.ds(pl.multiple_of(source * LEAF, LEAF), LEAF), :]
 
             @pl.when(active)
             def _():
-                near_tile(out, left, right, weights, leaf, source, False, dim, first)
-
-            return carry
-
-        return lax.fori_loop(1, 3, slot_step, carry)
-
-    lax.fori_loop(first, first + out.shape[0] // LEAF, leaf_step, 0)
-
-
-def near_far_body(dim, near_list, near_count, left, before, after, w_up, w_down, w_late, start_a, start_b, out, right):
-    position = lax.axis_index("leaf")
-    base = position * 4
-    low = position % 2 == 0
-    up_late = low & (position % 8 != 0)
-    down_late = jnp.logical_not(low) & (position % 8 != 7)
-    for leaf in range(4):
-        cols = slice(leaf * LEAF, (leaf + 1) * LEAF)
-        right[0, :, cols] = right_form(before[:, cols])
-        right[1, :, cols] = right_form(after[:, cols])
-    half = start_a.shape[0]
-    out[:half, :] = start_a[...]
-    out[half:, :] = start_b[...]
-
-    def leaf_step(leaf, carry):
-        def slot_step(slot, carry):
-            source = near_list[leaf, slot] - base
-            active = slot < near_count[leaf]
-            behind = active & (source < 0) & (source >= -4)
-            ahead = active & (source >= 4) & (source < 8)
-
-            @pl.when(behind & up_late)
-            def _():
-                near_tile(out, left, right.at[0], w_late, leaf, source + 4, False, dim)
-
-            @pl.when(behind & jnp.logical_not(up_late))
-            def _():
-                near_tile(out, left, right.at[0], w_up, leaf, source + 4, False, dim)
-
-            @pl.when(ahead & down_late)
-            def _():
-                near_tile(out, left, right.at[1], w_late, leaf, source - 4, False, dim)
-
-            @pl.when(ahead & jnp.logical_not(down_late))
-            def _():
-                near_tile(out, left, right.at[1], w_down, leaf, source - 4, False, dim)
+                if inside:
+                    near_tile(out, left, right, weights, leaf, leaf, source, source, dim)
+                else:
+                    near_tile(out, left, right, held, leaf, leaf, source, 0, dim)
 
             return carry
 
@@ -253,26 +256,37 @@
     packed[64:128, :] = coords.astype(BF)
 
 
-def top_body(dim, own, other, s1, s2, s3, s4, s5, s6, s7, r0, r1, r2, r3, transfer, *outs):
-    member = lax.axis_index("leaf") % 4
-    own_left = left_form(own[64:128, :])
-    top = None
-    blocks = [(other, 0)] + [(ref, row) for ref in (s1, s2, s3, s4, s5, s6, s7) for row in (0, 128)]
+def top_part(own_left, blocks, dim, total):
     for ref, row in blocks:
         block = kernel_block(own_left, right_form(ref[row + 64 : row + 128, :]), dim)
         part = mm_nt(ref[row : row + 64, :], block)
-        top = part if top is None else top + part
-    top = top.astype(BF)
+        total = part if total is None else total + part
+    return total
+
+
+def top_start_body(dim, own, other, s1, s2, s3, s4, s5, s6, r0, r1, r2, r3, top, fields):
+    own_left = left_form(own[64:128, :])
+    blocks = [(other, 0)] + [(ref, row) for ref in (s1, s2, s3, s4, s5, s6) for row in (0, 128)]
+    top[...] = top_part(own_left, blocks, dim, None)
     nodes = (r0, r1, r2, r3)
     lefts = [left_form(node[64:128, :]) for node in nodes]
     rights = [right_form(node[64:128, :]) for node in nodes]
     for i in range(4):
-        cols = pl.ds(pl.multiple_of((member ^ i) * RANK, RANK), RANK)
-        total = mm(top, transfer[:, cols])
+        total = None
         for j in range(4):
             if i != j:
-                total = total + mm(nodes[j][0:64, :], kernel_block(lefts[j], rights[i], dim))
-        outs[i][...] = total.astype(BF)
+                part = mm(nodes[j][0:64, :], kernel_block(lefts[j], rights[i], dim))
+                total = part if total is None else total + part
+        fields[i * 64 : (i + 1) * 64, :] = total
+
+
+def top_body(dim, own, s7, top_start, fields, transfer, *outs):
+    member = lax.axis_index("leaf") % 4
+    own_left = left_form(own[64:128, :])
+    top = top_part(own_left, [(s7, 0), (s7, 128)], dim, top_start[...]).astype(BF)
+    for i in range(4):
+        cols = pl.ds(pl.multiple_of((member ^ i) * RANK, RANK), RANK)
+        outs[i][...] = (fields[i * 64 : (i + 1) * 64, :] + mm(top, transfer[:, cols])).astype(BF)
 
 
 def finish_body(t0, t1, t2, t3, transfer, basis, field, near, out, total):
@@ -322,25 +336,27 @@
         return moved(value, pairs, "cols")
 
     def raised(value, step):
-        return moved(value, [(i, (i + 8 * step) % count) for i in range(count)])
+        return moved(value, [(i, (i + (-8 if i % 8 == 7 else 8) * step) % count) for i in range(count)])
 
     up = [(i, i + 1) for i in range(count - 1)]
     down = [(j, i) for i, j in up]
+    picks = jnp.concatenate([leaf_skeleton, dev_skeleton, group_skeleton], axis=0)
     shard = points.T
     parts = [shard] + [shifted(shard, step) for step in (1, 2, 3)]
     transfer_1 = flipped(group_transfer, 1)
     transfer_2 = flipped(group_transfer, 2)
     transfer_3 = flipped(transfer_2, 1)
     transfers = [group_transfer, transfer_1, transfer_2, transfer_3]
-    is_late = lambda pair: pair[1] % 8 != (0 if pair[0] < pair[1] else 7) and pair[1] % 2 == (pair[0] > pair[1])
-    w_up = moved(weights, [pair for pair in up if not is_late(pair)])
-    w_down = moved(weights, [pair for pair in down if not is_late(pair)])
-    w_late = moved(weights, [pair for pair in up + down if is_late(pair)])
+    w_swap = flipped(weights, 1)
+    others = [(i, j) for i, j in up if j % 2 == 0] + [(i, j) for i, j in down if j % 2 == 1]
+    crossing = [(i, j) for i, j in others if i // 8 != j // 8]
+    w_cross = moved(weights, crossing)
+    w_late = moved(weights, [(i, j) for i, j in others if i // 8 == j // 8])
 
     leaf_skel, nodes = call(
         skel_body,
         [((4 * RANK, width), BF), ((width, RANK), BF)],
-        [pl.BlockSpec(memory_space=pl.ANY)] * 3,
+        [HBM] * 3,
         scratch=[
             pltpu.VMEM((rows, width), BF),
             pltpu.VMEM((4 * RANK, LEAF), BF),
@@ -349,15 +365,15 @@
         ],
         flops=2 * 5 * RANK * LEAF * width,
         nbytes=5 * 1024 * 1024,
-        vmem=58,
+        vmem=53,
     )(weights, leaf_basis, dev_transfer)
     coords, leaf_coords, *packs = call(
         select_body,
         [((dim, rows), BF), ((dim, 4 * RANK), BF)] + [((192, RANK), BF)] * 4,
-        [VMEM] * 8,
+        [VMEM] * 6,
         flops=2 * 64 * RANK * 5 * LEAF * 4,
         nbytes=1024 * 1024,
-    )(*parts, leaf_skeleton, dev_skeleton, group_skeleton, nodes)
+    )(*parts, picks, nodes)
     family = [packs[0]] + [flipped(packs[flip], flip) for flip in (1, 2, 3)]
 
     group_skel, full_transfer = call(
@@ -383,8 +399,8 @@
         nbytes=rows * 128 * 8,
         vmem=10,
     )(coords)
-    before = moved(coords, up)
-    after_coords = moved(coords, down)
+    inner = flipped(coords, 1)
+    outer = moved(coords, others)
 
     (leaf_field,) = call(
         functools.partial(leaf_field_body, dim),
@@ -398,38 +414,50 @@
 
     tile_flops = 2 * LEAF * LEAF * 512
     near_parts = []
-    for first in (0, 2):
+    for first in range(4):
         near_parts += call(
             functools.partial(near_own_body, dim, first),
-            [((rows // 2, width), F32)],
+            [((LEAF, width), F32)],
             [SMEM, SMEM, VMEM, VMEM, VMEM],
-            flops=5 * tile_flops // 2,
-            exps=5 * LEAF * LEAF // 2,
+            flops=3 * tile_flops // 2,
+            exps=3 * LEAF * LEAF // 2,
             nbytes=6 * 1024 * 1024,
             vmem=16,
         )(near_list, near_count, left, right, weights)
 
-    totals = call(
-        functools.partial(top_body, dim),
-        [((64, RANK), BF)] * 4,
-        [VMEM] * 14,
+    top_start, fields = call(
+        functools.partial(top_start_body, dim),
+        [((64, RANK), F32), ((4 * 64, RANK), F32)],
+        [VMEM] * 12,
         flops=2 * LEAF * LEAF * 512 * 2,
         exps=2 * LEAF * LEAF,
         nbytes=2 * 1024 * 1024,
         vmem=12,
-    )(group_skel, other, *rings, *family, full_transfer)
+    )(group_skel, other, *rings[:6], *family)
+    totals = call(
+        functools.partial(top_body, dim),
+        [((64, RANK), BF)] * 4,
+        [VMEM] * 5,
+        flops=2 * LEAF * LEAF * 64,
+        exps=RANK * RANK * 2,
+        nbytes=1024 * 1024,
+    )(group_skel, rings[6], top_start, fields, full_transfer)
     returned = [totals[0]] + [flipped(totals[flip], flip) for flip in (1, 2, 3)]
 
-    (near_sum,) = call(
-        functools.partial(near_far_body, dim),
-        [((rows, width), F32)],
-        [SMEM, SMEM] + [VMEM] * 8,
-        scratch=[pltpu.VMEM((2, 128, rows), BF)],
-        flops=7 * tile_flops,
-        exps=7 * LEAF * LEAF,
-        nbytes=12 * 1024 * 1024,
-        vmem=24,
-    )(near_list, near_count, left, before, after_coords, w_up, w_down, w_late, *near_parts)
+    def near_neighbour(inside, *args):
+        return call(
+            functools.partial(near_neighbour_body, dim, inside),
+            [((rows, width), F32)],
+            [SMEM, SMEM] + [VMEM] * len(args),
+            scratch=[pltpu.VMEM((128, rows), BF)] + [pltpu.VMEM((LEAF, width), BF)] * (not inside),
+            flops=3 * tile_flops,
+            exps=3 * LEAF * LEAF,
+            nbytes=12 * 1024 * 1024,
+            vmem=12,
+        )(near_list, near_count, *args)[0]
+
+    near_inner = near_neighbour(True, left, inner, w_swap, *near_parts)
+    near_sum = near_neighbour(False, left, outer, w_late, w_cross, near_inner)
 
     return pl.pallas_call(
         finish_body,

time: 112 us -> 107 us (0.955)
  the two profiles are of different devices: /device:TPU:97 before, /device:TPU:121 now
where the time goes in v1:
time: 107 us
  starting transfers between devices  43.5 us (41%)
  waiting for transfers between devices  34.5 us (32%)
  Pallas kernels  27.8 us (26%)
    ppermute x25, starting transfers between devices, moved(): return lax.ppermute(value, axis, pairs)  43.5 us
    ppermute x25, waiting for transfers between devices, moved(): return lax.ppermute(value, axis, pairs)  34.5 us
    pallas_call x4, Pallas kernels, per_device(): call(functools.partial(near_own_body, dim, first), [((LEAF, width), F32)]...  8.28 us
    pallas_call x2, Pallas kernels, near_neighbour(): call(functools.partial(near_neighbour_body, dim, inside), [((rows, width)...  6.59 us
    pallas_call x1, Pallas kernels, per_device(): pl.pallas_call(finish_body, grid=(4,), out_shape=jax.ShapeDtypeStruct((ro...  3.81 us
    pallas_call x1, Pallas kernels, per_device(): call(skel_body, [((4 * RANK, width), BF), ((width, RANK), BF)], [HBM] * 3...  3.47 us
    pallas_call x1, Pallas kernels, per_device(): call(functools.partial(top_start_body, dim), [((64, RANK), F32), ((4 * 64...  2.21 us
  transfers between devices with their start and end apart: 25, of which 9 were waited for; matrix products, arithmetic and copies ran while one was open for 1% of the time, Pallas kernels for 22%

profile of v1, /device:TPU:121, one launch (start us, length us, event | category | flops | bytes accessed | tf_op | source)
XLA Modules:
  0.0 106.8 jit_solution(17667320944898558013)
XLA Ops:
  0.0 0.7 collective-permute-start.24
  0.7 1.2 %collective-permute-start = (bf16[16,4096]{1,0:T(8,128)(2,1)}, bf16[16,4096]{1,0:T(8,128)(2,1)S(1)}, u32[]{:S(2)}, u32[]{:S(2)}) collective-permute-start(bf16[16,4096]{1,0:T(8,128)(2,1)} %bitcast.1), channel_id=1, source_target_pairs={{0,1},{1,2},{2,3},{3,0},{4,5},{5,6},{6,7},{7,4},{8,9},{9,10},{10,1... | collective-permute-start | bytes 393224 | tf_op jit(solution)/shard_map/ppermute | solution.py:329
  1.9 2.5 %collective-permute-start.1 = (bf16[16,4096]{1,0:T(8,128)(2,1)}, bf16[16,4096]{1,0:T(8,128)(2,1)S(1)}, u32[]{:S(2)}, u32[]{:S(2)}) collective-permute-start(bf16[16,4096]{1,0:T(8,128)(2,1)} %bitcast.2), channel_id=1, source_target_pairs={{0,2},{1,3},{2,0},{3,1},{4,6},{5,7},{6,4},{7,5},{8,10},{9,11},{10,... | collective-permute-start | bytes 393224 | tf_op jit(solution)/shard_map/ppermute | solution.py:329
  4.3 0.8 collective-permute-start.21
  5.1 4.9 %collective-permute-start.22 = (bf16[4096,256]{1,0:T(8,128)(2,1)}, bf16[4096,256]{1,0:T(8,128)(2,1)S(1)}, u32[]{:S(2)}, u32[]{:S(2)}) collective-permute-start(bf16[4096,256]{1,0:T(8,128)(2,1)} %weights.9), channel_id=1, source_target_pairs={{28,32},{60,64},{92,96},{124,128},{156,160},{188,192},{220,224},{3... | collective-permute-start | bytes 6291464 | tf_op jit(solution)/shard_map/ppermute | solution.py:329
  10.0 1.2 %collective-permute-start.2 = (bf16[16,4096]{1,0:T(8,128)(2,1)}, bf16[16,4096]{1,0:T(8,128)(2,1)S(1)}, u32[]{:S(2)}, u32[]{:S(2)}) collective-permute-start(bf16[16,4096]{1,0:T(8,128)(2,1)} %bitcast.3), channel_id=1, source_target_pairs={{0,3},{1,0},{2,1},{3,2},{4,7},{5,4},{6,5},{7,6},{8,11},{9,8},{10,9... | collective-permute-start | bytes 393224 | tf_op jit(solution)/shard_map/ppermute | solution.py:329
  11.2 0.2 collective-permute-start.7
  11.4 0.7 pad_add_fusion.picks
  12.2 2.3 %collective-permute-done.2.p3 = bf16[16,4096]{1,0:T(8,128)(2,1)S(1)} collective-permute-done((bf16[16,4096]{1,0:T(8,128)(2,1)}, bf16[16,4096]{1,0:T(8,128)(2,1)S(1)}, u32[]{:S(2)}, u32[]{:S(2)}) %collective-permute-start.2) | collective-permute-done | bytes 131104 | tf_op jit(solution)/shard_map/ppermute | solution.py:329
  14.4 3.5 %shard_map.100 = (bf16[1024,256]{1,0:T(8,128)(2,1)S(1)}, bf16[256,256]{1,0:T(8,128)(2,1)S(1)}) custom-call(bf16[4096,256]{1,0:T(8,128)(2,1)} %weights.9, bf16[1024,1024]{1,0:T(8,128)(2,1)} %basis.3, bf16[256,1024]{1,0:T(8,128)(2,1)} %transfer.3), custom_call_target="tpu_custom_call" | custom-call | flops 671088640 | bytes 5242880 | tf_op jit(solution)/shard_map/pallas_call | solution.py:356
  17.9 0.0 copy-start.3
  17.9 0.0 copy-start.4
  17.9 0.0 copy-start.5
  18.0 0.8 shard_map.101
  18.7 15.8 %collective-permute-done.7.g2 = bf16[64,1024]{1,0:T(8,128)(2,1)S(1)} collective-permute-done((bf16[64,1024]{1,0:T(8,128)(2,1)}, bf16[64,1024]{1,0:T(8,128)(2,1)S(1)}, u32[]{:S(2)}, u32[]{:S(2)}) %collective-permute-start.7) | collective-permute-done | bytes 131104 | tf_op jit(solution)/shard_map/ppermute | solution.py:329
  34.6 1.3 %collective-permute-start.4 = (bf16[192,256]{1,0:T(8,128)(2,1)S(1)}, bf16[192,256]{1,0:T(8,128)(2,1)S(1)}, u32[]{:S(2)}, u32[]{:S(2)}) collective-permute-start(bf16[192,256]{1,0:T(8,128)(2,1)S(1)} %get-tuple-element.26), channel_id=1, source_target_pairs={{0,8},{4,12},{8,0},{12,4},{16,24},{20,28},{24,16},{28,20},{32,40},... | collective-permute-start | bytes 294920 | tf_op jit(solution)/shard_map/ppermute | solution.py:329
  35.9 0.0 collective-permute-done.3.r1
  35.9 0.3 collective-permute-start.8
  36.1 2.3 %collective-permute-done.4.r2 = bf16[192,256]{1,0:T(8,128)(2,1)S(1)} collective-permute-done((bf16[192,256]{1,0:T(8,128)(2,1)S(1)}, bf16[192,256]{1,0:T(8,128)(2,1)S(1)}, u32[]{:S(2)}, u32[]{:S(2)}) %collective-permute-start.4) | collective-permute-done | bytes 98336 | tf_op jit(solution)/shard_map/ppermute | solution.py:329
  38.4 2.5 %collective-permute-start.5 = (bf16[192,256]{1,0:T(8,128)(2,1)S(1)}, bf16[192,256]{1,0:T(8,128)(2,1)S(1)}, u32[]{:S(2)}, u32[]{:S(2)}) collective-permute-start(bf16[192,256]{1,0:T(8,128)(2,1)S(1)} %get-tuple-element.27), channel_id=1, source_target_pairs={{0,12},{4,8},{8,4},{12,0},{16,28},{20,24},{24,20},{28,16},{32,44},... | collective-permute-start | bytes 294920 | tf_op jit(solution)/shard_map/ppermute | solution.py:329
  41.0 3.4 %collective-permute-done.5.r3 = bf16[192,256]{1,0:T(8,128)(2,1)S(1)} collective-permute-done((bf16[192,256]{1,0:T(8,128)(2,1)S(1)}, bf16[192,256]{1,0:T(8,128)(2,1)S(1)}, u32[]{:S(2)}, u32[]{:S(2)}) %collective-permute-start.5) | collective-permute-done | bytes 98336 | tf_op jit(solution)/shard_map/ppermute | solution.py:329
  44.4 0.3 shard_map.102
  44.7 0.6 collective-permute-start.9
  45.3 3.8 %collective-permute-done.9.other = bf16[128,256]{1,0:T(8,128)(2,1)S(1)} collective-permute-done((bf16[128,256]{1,0:T(8,128)(2,1)S(1)}, bf16[128,256]{1,0:T(8,128)(2,1)S(1)}, u32[]{:S(2)}, u32[]{:S(2)}) %collective-permute-start.9) | collective-permute-done | bytes 65568 | tf_op jit(solution)/shard_map/ppermute | solution.py:329
  49.2 0.4 shard_map.106
  49.6 2.9 %collective-permute-start.14 = (bf16[256,256]{1,0:T(8,128)(2,1)S(1)}, bf16[256,256]{1,0:T(8,128)(2,1)S(1)}, u32[]{:S(2)}, u32[]{:S(2)}) collective-permute-start(bf16[256,256]{1,0:T(8,128)(2,1)S(1)} %constant_dynamic-update-slice_fusion), channel_id=1, source_target_pairs={{0,224},{4,228},{8,232},{12,236},{16,240},{20,244},{24,248},{28,60... | collective-permute-start | bytes 393224 | tf_op jit(solution)/shard_map/ppermute | solution.py:329
  52.5 1.9 %collective-permute-done.10.s1 = bf16[256,256]{1,0:T(8,128)(2,1)S(1)} collective-permute-done((bf16[256,256]{1,0:T(8,128)(2,1)S(1)}, bf16[256,256]{1,0:T(8,128)(2,1)S(1)}, u32[]{:S(2)}, u32[]{:S(2)}) %collective-permute-start.10) | collective-permute-done | bytes 131104 | tf_op jit(solution)/shard_map/ppermute | solution.py:329
  54.4 2.1 %shard_map.107.refs_1_ = f32[1024,256]{1,0:T(8,128)S(1)} custom-call(s32[4,3]{1,0:T(4,128)S(1)} %copy-done.4, s32[4]{0:T(128)S(1)} %copy-done.5, bf16[4096,128]{1,0:T(8,128)(2,1)S(1)} %get-tuple-element.39.left, bf16[128,4096]{1,0:T(8,128)(2,1)S(1)} %get-tuple-element.40.right, bf16[4096,256]{1,0:T(8,128)(2,1)S(1)} %copy-done.2), custom_call_target="tpu_custom_call" | custom-call | flops 1610612736 | bytes 6291456 | tf_op jit(solution)/shard_map/pallas_call | solution.py:418
  56.5 2.7 %collective-permute-start.15 = (bf16[256,256]{1,0:T(8,128)(2,1)S(1)}, bf16[256,256]{1,0:T(8,128)(2,1)S(1)}, u32[]{:S(2)}, u32[]{:S(2)}) collective-permute-start(bf16[256,256]{1,0:T(8,128)(2,1)S(1)} %collective-permute-done.14.s2), channel_id=1, source_target_pairs={{0,224},{4,228},{8,232},{12,236},{16,240},{20,244},{24,248},{28,60... | collective-permute-start | bytes 393224 | tf_op jit(solution)/shard_map/ppermute | solution.py:329
  59.2 1.5 %collective-permute-done.11.s3 = bf16[256,256]{1,0:T(8,128)(2,1)S(1)} collective-permute-done((bf16[256,256]{1,0:T(8,128)(2,1)S(1)}, bf16[256,256]{1,0:T(8,128)(2,1)S(1)}, u32[]{:S(2)}, u32[]{:S(2)}) %collective-permute-start.11) | collective-permute-done | bytes 131104 | tf_op jit(solution)/shard_map/ppermute | solution.py:329
  60.7 2.1 %shard_map.108.refs_2_ = f32[1024,256]{1,0:T(8,128)S(1)} custom-call(s32[4,3]{1,0:T(4,128)S(1)} %copy-done.4, s32[4]{0:T(128)S(1)} %copy-done.5, bf16[4096,128]{1,0:T(8,128)(2,1)S(1)} %get-tuple-element.39.left, bf16[128,4096]{1,0:T(8,128)(2,1)S(1)} %get-tuple-element.40.right, bf16[4096,256]{1,0:T(8,128)(2,1)S(1)} %copy-done.2), custom_call_target="tpu_custom_call" | custom-call | flops 1610612736 | bytes 6291456 | tf_op jit(solution)/shard_map/pallas_call | solution.py:418
  62.8 6.0 %collective-permute-start.23 = (bf16[64,4096]{1,0:T(8,128)(2,1)S(1)}, bf16[64,4096]{1,0:T(8,128)(2,1)S(1)}, u32[]{:S(2)}, u32[]{:S(2)}) collective-permute-start(bf16[64,4096]{1,0:T(8,128)(2,1)S(1)} %get-tuple-element.38.coords), channel_id=1, source_target_pairs={{0,4},{4,0},{8,12},{12,8},{16,20},{20,16},{24,28},{28,24},{32,36},... | collective-permute-start | bytes 1572872 | tf_op jit(solution)/shard_map/ppermute | solution.py:329
  68.8 2.1 %shard_map.109.refs_3_ = f32[1024,256]{1,0:T(8,128)S(1)} custom-call(s32[4,3]{1,0:T(4,128)S(1)} %copy-done.4, s32[4]{0:T(128)S(1)} %copy-done.5, bf16[4096,128]{1,0:T(8,128)(2,1)S(1)} %get-tuple-element.39.left, bf16[128,4096]{1,0:T(8,128)(2,1)S(1)} %get-tuple-element.40.right, bf16[4096,256]{1,0:T(8,128)(2,1)S(1)} %copy-done.2), custom_call_target="tpu_custom_call" | custom-call | flops 1610612736 | bytes 6291456 | tf_op jit(solution)/shard_map/pallas_call | solution.py:418
  70.9 1.7 %collective-permute-done.16.s6 = bf16[256,256]{1,0:T(8,128)(2,1)S(1)} collective-permute-done((bf16[256,256]{1,0:T(8,128)(2,1)S(1)}, bf16[256,256]{1,0:T(8,128)(2,1)S(1)}, u32[]{:S(2)}, u32[]{:S(2)}) %collective-permute-start.16) | collective-permute-done | bytes 131104 | tf_op jit(solution)/shard_map/ppermute | solution.py:329
  72.6 1.2 %collective-permute-start.13 = (bf16[256,256]{1,0:T(8,128)(2,1)S(1)}, bf16[256,256]{1,0:T(8,128)(2,1)S(1)}, u32[]{:S(2)}, u32[]{:S(2)}) collective-permute-start(bf16[256,256]{1,0:T(8,128)(2,1)S(1)} %collective-permute-done.12.s5), channel_id=1, source_target_pairs={{0,32},{4,36},{8,40},{12,44},{16,48},{20,52},{24,56},{28,252},{32,... | collective-permute-start | bytes 393224 | tf_op jit(solution)/shard_map/ppermute | solution.py:329
  73.8 2.1 %shard_map.110.refs_4_ = f32[1024,256]{1,0:T(8,128)S(1)} custom-call(s32[4,3]{1,0:T(4,128)S(1)} %copy-done.4, s32[4]{0:T(128)S(1)} %copy-done.5, bf16[4096,128]{1,0:T(8,128)(2,1)S(1)} %get-tuple-element.39.left, bf16[128,4096]{1,0:T(8,128)(2,1)S(1)} %get-tuple-element.40.right, bf16[4096,256]{1,0:T(8,128)(2,1)S(1)} %copy-done.2), custom_call_target="tpu_custom_call" | custom-call | flops 1610612736 | bytes 6291456 | tf_op jit(solution)/shard_map/pallas_call | solution.py:418
  75.9 1.7 %collective-permute-done.13.s7 = bf16[256,256]{1,0:T(8,128)(2,1)S(1)} collective-permute-done((bf16[256,256]{1,0:T(8,128)(2,1)S(1)}, bf16[256,256]{1,0:T(8,128)(2,1)S(1)}, u32[]{:S(2)}, u32[]{:S(2)}) %collective-permute-start.13) | collective-permute-done | bytes 131104 | tf_op jit(solution)/shard_map/ppermute | solution.py:329
  77.6 8.0 %collective-permute-start.20 = (bf16[64,4096]{1,0:T(8,128)(2,1)S(1)}, bf16[64,4096]{1,0:T(8,128)(2,1)S(1)}, u32[]{:S(2)}, u32[]{:S(2)}) collective-permute-start(bf16[64,4096]{1,0:T(8,128)(2,1)S(1)} %get-tuple-element.38.coords), channel_id=1, source_target_pairs={{4,8},{12,16},{20,24},{28,32},{36,40},{44,48},{52,56},{60,64},{68,... | collective-permute-start | bytes 1572872 | tf_op jit(solution)/shard_map/ppermute | solution.py:329
  85.7 1.3 %shard_map.105.field = f32[1024,256]{1,0:T(8,128)S(1)} custom-call(bf16[64,1024]{1,0:T(8,128)(2,1)S(1)} %get-tuple-element.36.coords, bf16[1024,256]{1,0:T(8,128)(2,1)S(1)} %get-tuple-element.37.leaf_skel), custom_call_target="tpu_custom_call" | custom-call | flops 1073741824 | bytes 2097152 | tf_op jit(solution)/shard_map/pallas_call | solution.py:405
  87.0 2.2 %shard_map.103 = (f32[64,256]{1,0:T(8,128)S(1)}, f32[256,256]{1,0:T(8,128)S(1)}) custom-call(bf16[128,256]{1,0:T(8,128)(2,1)S(1)} %get-tuple-element.28.own, bf16[128,256]{1,0:T(8,128)(2,1)S(1)} %collective-permute-done.9.other, bf16[256,256]{1,0:T(8,128)(2,1)S(1)} %collective-permute-done.10.s1, bf16[256,256]{1,0:T(8,128)(2,1)S(1)} %collective-permute-done.14.s2, ...), custom_call_target="tpu_custom_call" | custom-call | flops 2147483648 | bytes 2097152 | tf_op jit(solution)/shard_map/pallas_call | solution.py:428
  89.2 0.6 shard_map.104
  89.8 0.1 collective-permute-start.17
  89.9 0.1 collective-permute-start.18
  90.0 2.5 %shard_map.111.refs_2_ = f32[4096,256]{1,0:T(8,128)S(1)} custom-call(s32[4,3]{1,0:T(4,128)S(1)} %copy-done.4, s32[4]{0:T(128)S(1)} %copy-done.5, bf16[4096,128]{1,0:T(8,128)(2,1)S(1)} %get-tuple-element.39.left, bf16[64,4096]{1,0:T(8,128)(2,1)S(1)} %collective-permute-done.23.coords, bf16[4096,256]{1,0:T(8,128)(2,1)S(1)} %collective-permute-done.24.refs_0_, ...), custom_call_target="tpu_custom_call" | custom-call | flops 3221225472 | bytes 12582912 | tf_op jit(solution)/shard_map/pallas_call | solution.py:448
  92.5 0.0 copy-start
  92.6 6.3 %collective-permute-start.19 = (bf16[64,256]{1,0:T(8,128)(2,1)S(1)}, bf16[64,256]{1,0:T(8,128)(2,1)S(1)}, u32[]{:S(2)}, u32[]{:S(2)}) collective-permute-start(bf16[64,256]{1,0:T(8,128)(2,1)S(1)} %get-tuple-element.35), channel_id=1, source_target_pairs={{0,12},{4,8},{8,4},{12,0},{16,28},{20,24},{24,20},{28,16},{32,44},... | collective-permute-start | bytes 98312 | tf_op jit(solution)/shard_map/ppermute | solution.py:329
  98.9 4.1 %shard_map.112.near = f32[4096,256]{1,0:T(8,128)S(1)} custom-call(s32[4,3]{1,0:T(4,128)S(1)} %copy-done.4, s32[4]{0:T(128)S(1)} %copy-done.5, bf16[4096,128]{1,0:T(8,128)(2,1)S(1)} %get-tuple-element.39.left, bf16[64,4096]{1,0:T(8,128)(2,1)S(1)} %collective-permute-done.20.coords, bf16[4096,256]{1,0:T(8,128)(2,1)S(1)} %collective-permute-done.21.refs_0_, ...), custom_call_target="tpu_custom_call" | custom-call | flops 3221225472 | bytes 12582912 | tf_op jit(solution)/shard_map/pallas_call | solution.py:448
  103.0 3.8 %finish.1 = f32[4096,256]{1,0:T(8,128)} custom-call(bf16[64,256]{1,0:T(8,128)(2,1)S(1)} %get-tuple-element.32.t0, bf16[64,256]{1,0:T(8,128)(2,1)S(1)} %collective-permute-done.17.t1, bf16[64,256]{1,0:T(8,128)(2,1)S(1)} %collective-permute-done.18.t2, bf16[64,256]{1,0:T(8,128)(2,1)S(1)} %collective-permute-done.19.t3, bf16[256,1024]{1,0:T(8,128)(2,1)S(1)} %copy-done.1, ...), custom_call_target="tpu_custom_call" | custom-call | flops 671088640 | bytes 10485760 | tf_op jit(solution)/shard_map/finish/pallas_call | solution.py:462
  (33 shorter events, 0.1 us)
Async XLA Ops:
  0.0 89.9 %collective-permute-start.24 = (bf16[4096,256]{1,0:T(8,128)(2,1)}, bf16[4096,256]{1,0:T(8,128)(2,1)S(1)}, u32[]{:S(2)}, u32[]{:S(2)}) collective-permute-start(bf16[4096,256]{1,0:T(8,128)(2,1)} %weights.9), channel_id=1, source_target_pairs={{0,4},{4,0},{8,12},{12,8},{16,20},{20,16},{24,28},{28,24},{32,36},... | collective-permute-start | bytes 6291464 | tf_op jit(solution)/shard_map/ppermute | solution.py:329
  0.7 9.3 %collective-permute-start = (bf16[16,4096]{1,0:T(8,128)(2,1)}, bf16[16,4096]{1,0:T(8,128)(2,1)S(1)}, u32[]{:S(2)}, u32[]{:S(2)}) collective-permute-start(bf16[16,4096]{1,0:T(8,128)(2,1)} %bitcast.1), channel_id=1, source_target_pairs={{0,1},{1,2},{2,3},{3,0},{4,5},{5,6},{6,7},{7,4},{8,9},{9,10},{10,1... | collective-permute-start | bytes 393224 | tf_op jit(solution)/shard_map/ppermute | solution.py:329
  1.9 9.4 %collective-permute-start.1 = (bf16[16,4096]{1,0:T(8,128)(2,1)}, bf16[16,4096]{1,0:T(8,128)(2,1)S(1)}, u32[]{:S(2)}, u32[]{:S(2)}) collective-permute-start(bf16[16,4096]{1,0:T(8,128)(2,1)} %bitcast.2), channel_id=1, source_target_pairs={{0,2},{1,3},{2,0},{3,1},{4,6},{5,7},{6,4},{7,5},{8,10},{9,11},{10,... | collective-permute-start | bytes 393224 | tf_op jit(solution)/shard_map/ppermute | solution.py:329
  4.3 94.5 %collective-permute-start.21 = (bf16[4096,256]{1,0:T(8,128)(2,1)}, bf16[4096,256]{1,0:T(8,128)(2,1)S(1)}, u32[]{:S(2)}, u32[]{:S(2)}) collective-permute-start(bf16[4096,256]{1,0:T(8,128)(2,1)} %weights.9), channel_id=1, source_target_pairs={{4,8},{12,16},{20,24},{36,40},{44,48},{52,56},{68,72},{76,80},{84,... | collective-permute-start | bytes 6291464 | tf_op jit(solution)/shard_map/ppermute | solution.py:329
  5.1 93.7 %collective-permute-start.22 = (bf16[4096,256]{1,0:T(8,128)(2,1)}, bf16[4096,256]{1,0:T(8,128)(2,1)S(1)}, u32[]{:S(2)}, u32[]{:S(2)}) collective-permute-start(bf16[4096,256]{1,0:T(8,128)(2,1)} %weights.9), channel_id=1, source_target_pairs={{28,32},{60,64},{92,96},{124,128},{156,160},{188,192},{220,224},{3... | collective-permute-start | bytes 6291464 | tf_op jit(solution)/shard_map/ppermute | solution.py:329
  10.0 4.4 %collective-permute-start.2 = (bf16[16,4096]{1,0:T(8,128)(2,1)}, bf16[16,4096]{1,0:T(8,128)(2,1)S(1)}, u32[]{:S(2)}, u32[]{:S(2)}) collective-permute-start(bf16[16,4096]{1,0:T(8,128)(2,1)} %bitcast.3), channel_id=1, source_target_pairs={{0,3},{1,0},{2,1},{3,2},{4,7},{5,4},{6,5},{7,6},{8,11},{9,8},{10,9... | collective-permute-start | bytes 393224 | tf_op jit(solution)/shard_map/ppermute | solution.py:329
  11.2 23.3 %collective-permute-start.7 = (bf16[64,1024]{1,0:T(8,128)(2,1)}, bf16[64,1024]{1,0:T(8,128)(2,1)S(1)}, u32[]{:S(2)}, u32[]{:S(2)}) collective-permute-start(bf16[64,1024]{1,0:T(8,128)(2,1)} %g0.1), channel_id=1, source_target_pairs={{0,8},{4,12},{8,0},{12,4},{16,24},{20,28},{24,16},{28,20},{32,40},... | collective-permute-start | bytes 393224 | tf_op jit(solution)/shard_map/ppermute | solution.py:329
  12.2 5.8 %copy-start.6 = (bf16[4096,16]{0,1:T(8,128)(2,1)S(1)}, bf16[4096,16]{0,1:T(8,128)(2,1)}, u32[]{:S(2)}) copy-start(bf16[4096,16]{0,1:T(8,128)(2,1)} %param.10) | copy-start | bytes 393220
  14.4 20.2 %collective-permute-start.6 = (bf16[64,1024]{1,0:T(8,128)(2,1)}, bf16[64,1024]{1,0:T(8,128)(2,1)S(1)}, u32[]{:S(2)}, u32[]{:S(2)}) collective-permute-start(bf16[64,1024]{1,0:T(8,128)(2,1)} %g0.1), channel_id=1, source_target_pairs={{0,4},{4,0},{8,12},{12,8},{16,20},{20,16},{24,28},{28,24},{32,36},... | collective-permute-start | bytes 393224 | tf_op jit(solution)/shard_map/ppermute | solution.py:329
  17.9 26.5 %copy-start.3 = (bf16[64,1024]{1,0:T(8,128)(2,1)S(1)}, bf16[64,1024]{1,0:T(8,128)(2,1)}, u32[]{:S(2)}) copy-start(bf16[64,1024]{1,0:T(8,128)(2,1)} %g0.1) | copy-start | bytes 393220
  17.9 36.4 %copy-start.2 = (bf16[4096,256]{1,0:T(8,128)(2,1)S(1)}, bf16[4096,256]{1,0:T(8,128)(2,1)}, u32[]{:S(2)}) copy-start(bf16[4096,256]{1,0:T(8,128)(2,1)} %weights.9) | copy-start | bytes 6291460
  17.9 36.4 %copy-start.4 = (s32[4,3]{1,0:T(4,128)S(1)}, s32[4,3]{1,0:T(4,128)}, u32[]{:S(2)}) copy-start(s32[4,3]{1,0:T(4,128)} %near_list.11) | copy-start | bytes 148
  17.9 36.4 %copy-start.5 = (s32[4]{0:T(128)S(1)}, s32[4]{0:T(128)}, u32[]{:S(2)}) copy-start(s32[4]{0:T(128)} %near_count.11) | copy-start | bytes 52
  34.6 1.3 %collective-permute-start.3 = (bf16[192,256]{1,0:T(8,128)(2,1)S(1)}, bf16[192,256]{1,0:T(8,128)(2,1)S(1)}, u32[]{:S(2)}, u32[]{:S(2)}) collective-permute-start(bf16[192,256]{1,0:T(8,128)(2,1)S(1)} %get-tuple-element.25), channel_id=1, source_target_pairs={{0,4},{4,0},{8,12},{12,8},{16,20},{20,16},{24,28},{28,24},{32,36},... | collective-permute-start | bytes 294920 | tf_op jit(solution)/shard_map/ppermute | solution.py:329
  34.6 3.8 %collective-permute-start.4 = (bf16[192,256]{1,0:T(8,128)(2,1)S(1)}, bf16[192,256]{1,0:T(8,128)(2,1)S(1)}, u32[]{:S(2)}, u32[]{:S(2)}) collective-permute-start(bf16[192,256]{1,0:T(8,128)(2,1)S(1)} %get-tuple-element.26), channel_id=1, source_target_pairs={{0,8},{4,12},{8,0},{12,4},{16,24},{20,28},{24,16},{28,20},{32,40},... | collective-permute-start | bytes 294920 | tf_op jit(solution)/shard_map/ppermute | solution.py:329
  35.9 8.5 %collective-permute-start.8 = (bf16[64,1024]{1,0:T(8,128)(2,1)S(1)}, bf16[64,1024]{1,0:T(8,128)(2,1)S(1)}, u32[]{:S(2)}, u32[]{:S(2)}) collective-permute-start(bf16[64,1024]{1,0:T(8,128)(2,1)S(1)} %collective-permute-done.7.g2), channel_id=1, source_target_pairs={{0,4},{4,0},{8,12},{12,8},{16,20},{20,16},{24,28},{28,24},{32,36},... | collective-permute-start | bytes 393224 | tf_op jit(solution)/shard_map/ppermute | solution.py:329
  38.4 6.0 %collective-permute-start.5 = (bf16[192,256]{1,0:T(8,128)(2,1)S(1)}, bf16[192,256]{1,0:T(8,128)(2,1)S(1)}, u32[]{:S(2)}, u32[]{:S(2)}) collective-permute-start(bf16[192,256]{1,0:T(8,128)(2,1)S(1)} %get-tuple-element.27), channel_id=1, source_target_pairs={{0,12},{4,8},{8,4},{12,0},{16,28},{20,24},{24,20},{28,16},{32,44},... | collective-permute-start | bytes 294920 | tf_op jit(solution)/shard_map/ppermute | solution.py:329
  44.7 4.4 %collective-permute-start.9 = (bf16[128,256]{1,0:T(8,128)(2,1)S(1)}, bf16[128,256]{1,0:T(8,128)(2,1)S(1)}, u32[]{:S(2)}, u32[]{:S(2)}) collective-permute-start(bf16[128,256]{1,0:T(8,128)(2,1)S(1)} %get-tuple-element.28.own), channel_id=1, source_target_pairs={{0,24},{4,28},{8,16},{12,20},{16,8},{20,12},{24,0},{28,4},{32,56},... | collective-permute-start | bytes 196616 | tf_op jit(solution)/shard_map/ppermute | solution.py:329
  49.1 5.2 %collective-permute-start.10 = (bf16[256,256]{1,0:T(8,128)(2,1)S(1)}, bf16[256,256]{1,0:T(8,128)(2,1)S(1)}, u32[]{:S(2)}, u32[]{:S(2)}) collective-permute-start(bf16[256,256]{1,0:T(8,128)(2,1)S(1)} %constant_dynamic-update-slice_fusion), channel_id=1, source_target_pairs={{0,32},{4,36},{8,40},{12,44},{16,48},{20,52},{24,56},{28,252},{32,... | collective-permute-start | bytes 393224 | tf_op jit(solution)/shard_map/ppermute | solution.py:329
  49.6 6.9 %collective-permute-start.14 = (bf16[256,256]{1,0:T(8,128)(2,1)S(1)}, bf16[256,256]{1,0:T(8,128)(2,1)S(1)}, u32[]{:S(2)}, u32[]{:S(2)}) collective-permute-start(bf16[256,256]{1,0:T(8,128)(2,1)S(1)} %constant_dynamic-update-slice_fusion), channel_id=1, source_target_pairs={{0,224},{4,228},{8,232},{12,236},{16,240},{20,244},{24,248},{28,60... | collective-permute-start | bytes 393224 | tf_op jit(solution)/shard_map/ppermute | solution.py:329
  54.3 6.3 %collective-permute-start.11 = (bf16[256,256]{1,0:T(8,128)(2,1)S(1)}, bf16[256,256]{1,0:T(8,128)(2,1)S(1)}, u32[]{:S(2)}, u32[]{:S(2)}) collective-permute-start(bf16[256,256]{1,0:T(8,128)(2,1)S(1)} %collective-permute-done.10.s1), channel_id=1, source_target_pairs={{0,32},{4,36},{8,40},{12,44},{16,48},{20,52},{24,56},{28,252},{32,... | collective-permute-start | bytes 393224 | tf_op jit(solution)/shard_map/ppermute | solution.py:329
  56.5 6.3 %collective-permute-start.15 = (bf16[256,256]{1,0:T(8,128)(2,1)S(1)}, bf16[256,256]{1,0:T(8,128)(2,1)S(1)}, u32[]{:S(2)}, u32[]{:S(2)}) collective-permute-start(bf16[256,256]{1,0:T(8,128)(2,1)S(1)} %collective-permute-done.14.s2), channel_id=1, source_target_pairs={{0,224},{4,228},{8,232},{12,236},{16,240},{20,244},{24,248},{28,60... | collective-permute-start | bytes 393224 | tf_op jit(solution)/shard_map/ppermute | solution.py:329
  60.7 8.1 %collective-permute-start.12 = (bf16[256,256]{1,0:T(8,128)(2,1)S(1)}, bf16[256,256]{1,0:T(8,128)(2,1)S(1)}, u32[]{:S(2)}, u32[]{:S(2)}) collective-permute-start(bf16[256,256]{1,0:T(8,128)(2,1)S(1)} %collective-permute-done.11.s3), channel_id=1, source_target_pairs={{0,32},{4,36},{8,40},{12,44},{16,48},{20,52},{24,56},{28,252},{32,... | collective-permute-start | bytes 393224 | tf_op jit(solution)/shard_map/ppermute | solution.py:329
  62.8 27.0 %collective-permute-start.23 = (bf16[64,4096]{1,0:T(8,128)(2,1)S(1)}, bf16[64,4096]{1,0:T(8,128)(2,1)S(1)}, u32[]{:S(2)}, u32[]{:S(2)}) collective-permute-start(bf16[64,4096]{1,0:T(8,128)(2,1)S(1)} %get-tuple-element.38.coords), channel_id=1, source_target_pairs={{0,4},{4,0},{8,12},{12,8},{16,20},{20,16},{24,28},{28,24},{32,36},... | collective-permute-start | bytes 1572872 | tf_op jit(solution)/shard_map/ppermute | solution.py:329
  68.8 3.8 %collective-permute-start.16 = (bf16[256,256]{1,0:T(8,128)(2,1)S(1)}, bf16[256,256]{1,0:T(8,128)(2,1)S(1)}, u32[]{:S(2)}, u32[]{:S(2)}) collective-permute-start(bf16[256,256]{1,0:T(8,128)(2,1)S(1)} %collective-permute-done.15.s4), channel_id=1, source_target_pairs={{0,224},{4,228},{8,232},{12,236},{16,240},{20,244},{24,248},{28,60... | collective-permute-start | bytes 393224 | tf_op jit(solution)/shard_map/ppermute | solution.py:329
  72.6 5.0 %collective-permute-start.13 = (bf16[256,256]{1,0:T(8,128)(2,1)S(1)}, bf16[256,256]{1,0:T(8,128)(2,1)S(1)}, u32[]{:S(2)}, u32[]{:S(2)}) collective-permute-start(bf16[256,256]{1,0:T(8,128)(2,1)S(1)} %collective-permute-done.12.s5), channel_id=1, source_target_pairs={{0,32},{4,36},{8,40},{12,44},{16,48},{20,52},{24,56},{28,252},{32,... | collective-permute-start | bytes 393224 | tf_op jit(solution)/shard_map/ppermute | solution.py:329
  77.6 14.9 %collective-permute-start.20 = (bf16[64,4096]{1,0:T(8,128)(2,1)S(1)}, bf16[64,4096]{1,0:T(8,128)(2,1)S(1)}, u32[]{:S(2)}, u32[]{:S(2)}) collective-permute-start(bf16[64,4096]{1,0:T(8,128)(2,1)S(1)} %get-tuple-element.38.coords), channel_id=1, source_target_pairs={{4,8},{12,16},{20,24},{28,32},{36,40},{44,48},{52,56},{60,64},{68,... | collective-permute-start | bytes 1572872 | tf_op jit(solution)/shard_map/ppermute | solution.py:329
  89.8 13.2 %collective-permute-start.17 = (bf16[64,256]{1,0:T(8,128)(2,1)S(1)}, bf16[64,256]{1,0:T(8,128)(2,1)S(1)}, u32[]{:S(2)}, u32[]{:S(2)}) collective-permute-start(bf16[64,256]{1,0:T(8,128)(2,1)S(1)} %get-tuple-element.33), channel_id=1, source_target_pairs={{0,4},{4,0},{8,12},{12,8},{16,20},{20,16},{24,28},{28,24},{32,36},... | collective-permute-start | bytes 98312 | tf_op jit(solution)/shard_map/ppermute | solution.py:329
  89.9 13.1 %collective-permute-start.18 = (bf16[64,256]{1,0:T(8,128)(2,1)S(1)}, bf16[64,256]{1,0:T(8,128)(2,1)S(1)}, u32[]{:S(2)}, u32[]{:S(2)}) collective-permute-start(bf16[64,256]{1,0:T(8,128)(2,1)S(1)} %get-tuple-element.34), channel_id=1, source_target_pairs={{0,8},{4,12},{8,0},{12,4},{16,24},{20,28},{24,16},{28,20},{32,40},... | collective-permute-start | bytes 98312 | tf_op jit(solution)/shard_map/ppermute | solution.py:329
  92.5 10.4 %copy-start = (bf16[1024,1024]{1,0:T(8,128)(2,1)S(1)}, bf16[1024,1024]{1,0:T(8,128)(2,1)}, u32[]{:S(2)}) copy-start(bf16[1024,1024]{1,0:T(8,128)(2,1)} %basis.3) | copy-start | bytes 6291460
  92.5 10.4 %copy-start.1 = (bf16[256,1024]{1,0:T(8,128)(2,1)S(1)}, bf16[256,1024]{1,0:T(8,128)(2,1)}, u32[]{:S(2)}) copy-start(bf16[256,1024]{1,0:T(8,128)(2,1)} %transfer.3) | copy-start | bytes 1572868
  92.6 10.4 %collective-permute-start.19 = (bf16[64,256]{1,0:T(8,128)(2,1)S(1)}, bf16[64,256]{1,0:T(8,128)(2,1)S(1)}, u32[]{:S(2)}, u32[]{:S(2)}) collective-permute-start(bf16[64,256]{1,0:T(8,128)(2,1)S(1)} %get-tuple-element.35), channel_id=1, source_target_pairs={{0,12},{4,8},{8,4},{12,0},{16,28},{20,24},{24,20},{28,16},{32,44},... | collective-permute-start | bytes 98312 | tf_op jit(solution)/shard_map/ppermute | solution.py:329

commit v2 on v1

--- a/solution.py
+++ b/solution.py
@@ -195,14 +195,15 @@
     lax.fori_loop(0, 3, slot_step, 0)
 
 
-def near_neighbour_body(dim, inside, near_list, near_count, left, coords, *refs):
+def near_neighbour_body(dim, inside, opening, near_list, near_count, left, coords, *refs):
     if inside:
-        weights, s0, s1, s2, s3, out, right = refs
-        for leaf, start in enumerate((s0, s1, s2, s3)):
-            out[leaf * LEAF : (leaf + 1) * LEAF, :] = start[...]
+        weights, s0, s1, out, right = refs
+        held = None
     else:
-        weights_late, weights_cross, start, out, right, held = refs
-        out[...] = start[...]
+        weights_late, weights_cross, s0, s1, out, right, held = refs
+    half = s0.shape[0]
+    out[:half, :] = s0[...]
+    out[half:, :] = s1[...]
     position = lax.axis_index("leaf")
     even = position % 2 == 0
     edge = (position % 8 == 0) | (position % 8 == 7)
@@ -229,7 +230,7 @@
             @pl.when(active)
             def _():
                 if inside:
-                    near_tile(out, left, right, weights, leaf, leaf, source, source, dim)
+                    near_tile(out, left, right, weights, leaf, leaf - opening, source, source, dim)
                 else:
                     near_tile(out, left, right, held, leaf, leaf, source, 0, dim)
 
@@ -237,7 +238,7 @@
 
         return lax.fori_loop(1, 3, slot_step, carry)
 
-    lax.fori_loop(0, 4, leaf_step, 0)
+    lax.fori_loop(opening, opening + out.shape[0] // LEAF, leaf_step, 0)
 
 
 def group_body(r0, r1, r2, r3, g0, g1, g2, g3, packed, transfer):
@@ -340,7 +341,6 @@
 
     up = [(i, i + 1) for i in range(count - 1)]
     down = [(j, i) for i, j in up]
-    picks = jnp.concatenate([leaf_skeleton, dev_skeleton, group_skeleton], axis=0)
     shard = points.T
     parts = [shard] + [shifted(shard, step) for step in (1, 2, 3)]
     transfer_1 = flipped(group_transfer, 1)
@@ -367,6 +367,9 @@
         nbytes=5 * 1024 * 1024,
         vmem=53,
     )(weights, leaf_basis, dev_transfer)
+    tables = (leaf_skeleton, dev_skeleton, group_skeleton)
+    nodes, *tables = lax.optimization_barrier((nodes, *tables))
+    picks = jnp.concatenate(tables, axis=0)
     coords, leaf_coords, *packs = call(
         select_body,
         [((dim, rows), BF), ((dim, 4 * RANK), BF)] + [((192, RANK), BF)] * 4,
@@ -444,10 +447,10 @@
     )(group_skel, rings[6], top_start, fields, full_transfer)
     returned = [totals[0]] + [flipped(totals[flip], flip) for flip in (1, 2, 3)]
 
-    def near_neighbour(inside, *args):
+    def near_neighbour(inside, opening, *args):
         return call(
-            functools.partial(near_neighbour_body, dim, inside),
-            [((rows, width), F32)],
+            functools.partial(near_neighbour_body, dim, inside, opening),
+            [((2 * args[-1].shape[0], width), F32)],
             [SMEM, SMEM] + [VMEM] * len(args),
             scratch=[pltpu.VMEM((128, rows), BF)] + [pltpu.VMEM((LEAF, width), BF)] * (not inside),
             flops=3 * tile_flops,
@@ -456,8 +459,10 @@
             vmem=12,
         )(near_list, near_count, *args)[0]
 
-    near_inner = near_neighbour(True, left, inner, w_swap, *near_parts)
-    near_sum = near_neighbour(False, left, outer, w_late, w_cross, near_inner)
+    halves = [
+        near_neighbour(True, n, left, inner, w_swap, near_parts[n], near_parts[n + 1]) for n in (0, 2)
+    ]
+    near_sum = near_neighbour(False, 0, left, outer, w_late, w_cross, *halves)
 
     return pl.pallas_call(
         finish_body,

time: 107 us -> 108 us (level)
  the two profiles are of different devices: /device:TPU:121 before, /device:TPU:97 now
where the time goes in v2:
time: 108 us; the launch traced here: 106 us
  starting transfers between devices  38.5 us (36%)
  Pallas kernels  34.1 us (32%)
  waiting for transfers between devices  33.1 us (31%)
    ppermute x25, starting transfers between devices, moved(): return lax.ppermute(value, axis, pairs)  38.5 us
    ppermute x25, waiting for transfers between devices, moved(): return lax.ppermute(value, axis, pairs)  33.1 us
    pallas_call x3, Pallas kernels, near_neighbour(): call(functools.partial(near_neighbour_body, dim, inside, opening), [((2 *...  11.5 us
    pallas_call x4, Pallas kernels, per_device(): call(functools.partial(near_own_body, dim, first), [((LEAF, width), F32)]...  9.73 us
    pallas_call x1, Pallas kernels, per_device(): pl.pallas_call(finish_body, grid=(4,), out_shape=jax.ShapeDtypeStruct((ro...  3.81 us
    pallas_call x1, Pallas kernels, per_device(): call(skel_body, [((4 * RANK, width), BF), ((width, RANK), BF)], [HBM] * 3...  3.47 us
    pallas_call x1, Pallas kernels, per_device(): call(functools.partial(top_start_body, dim), [((64, RANK), F32), ((4 * 64...  2.19 us
  transfers between devices with their start and end apart: 25, of which 8 were waited for; matrix products, arithmetic and copies ran while one was open for 0% of the time, Pallas kernels for 29%

profile of v2, /device:TPU:97, one launch (start us, length us, event | category | flops | bytes accessed | tf_op | source)
XLA Modules:
  0.0 106.1 jit_solution(16172661888323192961)
XLA Ops:
  0.0 0.7 collective-permute-start.24
  0.7 1.3 %collective-permute-start = (bf16[16,4096]{1,0:T(8,128)(2,1)}, bf16[16,4096]{1,0:T(8,128)(2,1)S(1)}, u32[]{:S(2)}, u32[]{:S(2)}) collective-permute-start(bf16[16,4096]{1,0:T(8,128)(2,1)} %bitcast.1), channel_id=1, source_target_pairs={{0,1},{1,2},{2,3},{3,0},{4,5},{5,6},{6,7},{7,4},{8,9},{9,10},{10,1... | collective-permute-start | bytes 393224 | tf_op jit(solution)/shard_map/ppermute | solution.py:330
  2.0 2.5 %collective-permute-start.1 = (bf16[16,4096]{1,0:T(8,128)(2,1)}, bf16[16,4096]{1,0:T(8,128)(2,1)S(1)}, u32[]{:S(2)}, u32[]{:S(2)}) collective-permute-start(bf16[16,4096]{1,0:T(8,128)(2,1)} %bitcast.2), channel_id=1, source_target_pairs={{0,2},{1,3},{2,0},{3,1},{4,6},{5,7},{6,4},{7,5},{8,10},{9,11},{10,... | collective-permute-start | bytes 393224 | tf_op jit(solution)/shard_map/ppermute | solution.py:330
  4.4 1.2 %collective-permute-start.2 = (bf16[16,4096]{1,0:T(8,128)(2,1)}, bf16[16,4096]{1,0:T(8,128)(2,1)S(1)}, u32[]{:S(2)}, u32[]{:S(2)}) collective-permute-start(bf16[16,4096]{1,0:T(8,128)(2,1)} %bitcast.3), channel_id=1, source_target_pairs={{0,3},{1,0},{2,1},{3,2},{4,7},{5,4},{6,5},{7,6},{8,11},{9,8},{10,9... | collective-permute-start | bytes 393224 | tf_op jit(solution)/shard_map/ppermute | solution.py:330
  5.6 3.9 %collective-permute-start.21 = (bf16[4096,256]{1,0:T(8,128)(2,1)}, bf16[4096,256]{1,0:T(8,128)(2,1)S(1)}, u32[]{:S(2)}, u32[]{:S(2)}) collective-permute-start(bf16[4096,256]{1,0:T(8,128)(2,1)} %weights.9), channel_id=1, source_target_pairs={{4,8},{12,16},{20,24},{36,40},{44,48},{52,56},{68,72},{76,80},{84,... | collective-permute-start | bytes 6291464 | tf_op jit(solution)/shard_map/ppermute | solution.py:330
  9.5 3.5 %shard_map.100 = (bf16[1024,256]{1,0:T(8,128)(2,1)S(1)}, bf16[256,256]{1,0:T(8,128)(2,1)S(1)}) custom-call(bf16[4096,256]{1,0:T(8,128)(2,1)} %weights.9, bf16[1024,1024]{1,0:T(8,128)(2,1)} %basis.3, bf16[256,1024]{1,0:T(8,128)(2,1)} %transfer.3), custom_call_target="tpu_custom_call" | custom-call | flops 671088640 | bytes 5242880 | tf_op jit(solution)/shard_map/pallas_call | solution.py:356
  13.0 0.8 collective-permute-start.22
  13.9 1.4 %collective-permute-start.7 = (bf16[64,1024]{1,0:T(8,128)(2,1)S(1)}, bf16[64,1024]{1,0:T(8,128)(2,1)S(1)}, u32[]{:S(2)}, u32[]{:S(2)}) collective-permute-start(bf16[64,1024]{1,0:T(8,128)(2,1)S(1)} %copy-done.3), channel_id=1, source_target_pairs={{0,8},{4,12},{8,0},{12,4},{16,24},{20,28},{24,16},{28,20},{32,40},... | collective-permute-start | bytes 393224 | tf_op jit(solution)/shard_map/ppermute | solution.py:330
  15.3 0.0 copy-start.4
  15.3 0.0 copy-start.5
  15.3 0.8 shard_map.101
  16.1 19.4 %collective-permute-done.7.g2 = bf16[64,1024]{1,0:T(8,128)(2,1)S(1)} collective-permute-done((bf16[64,1024]{1,0:T(8,128)(2,1)S(1)}, bf16[64,1024]{1,0:T(8,128)(2,1)S(1)}, u32[]{:S(2)}, u32[]{:S(2)}) %collective-permute-start.7) | collective-permute-done | bytes 131104 | tf_op jit(solution)/shard_map/ppermute | solution.py:330
  35.5 1.4 %collective-permute-start.3 = (bf16[192,256]{1,0:T(8,128)(2,1)S(1)}, bf16[192,256]{1,0:T(8,128)(2,1)S(1)}, u32[]{:S(2)}, u32[]{:S(2)}) collective-permute-start(bf16[192,256]{1,0:T(8,128)(2,1)S(1)} %get-tuple-element.33), channel_id=1, source_target_pairs={{0,4},{4,0},{8,12},{12,8},{16,20},{20,16},{24,28},{28,24},{32,36},... | collective-permute-start | bytes 294920 | tf_op jit(solution)/shard_map/ppermute | solution.py:330
  37.0 0.5 collective-permute-start.4
  37.4 0.5 collective-permute-done.3.r1
  37.9 0.4 collective-permute-start.8
  38.3 3.1 %collective-permute-done.4.r2 = bf16[192,256]{1,0:T(8,128)(2,1)S(1)} collective-permute-done((bf16[192,256]{1,0:T(8,128)(2,1)S(1)}, bf16[192,256]{1,0:T(8,128)(2,1)S(1)}, u32[]{:S(2)}, u32[]{:S(2)}) %collective-permute-start.4) | collective-permute-done | bytes 98336 | tf_op jit(solution)/shard_map/ppermute | solution.py:330
  41.3 1.2 %collective-permute-start.5 = (bf16[192,256]{1,0:T(8,128)(2,1)S(1)}, bf16[192,256]{1,0:T(8,128)(2,1)S(1)}, u32[]{:S(2)}, u32[]{:S(2)}) collective-permute-start(bf16[192,256]{1,0:T(8,128)(2,1)S(1)} %get-tuple-element.35), channel_id=1, source_target_pairs={{0,12},{4,8},{8,4},{12,0},{16,28},{20,24},{24,20},{28,16},{32,44},... | collective-permute-start | bytes 294920 | tf_op jit(solution)/shard_map/ppermute | solution.py:330
  42.5 0.4 shard_map.106
  42.9 3.6 %collective-permute-done.5.r3 = bf16[192,256]{1,0:T(8,128)(2,1)S(1)} collective-permute-done((bf16[192,256]{1,0:T(8,128)(2,1)S(1)}, bf16[192,256]{1,0:T(8,128)(2,1)S(1)}, u32[]{:S(2)}, u32[]{:S(2)}) %collective-permute-start.5) | collective-permute-done | bytes 98336 | tf_op jit(solution)/shard_map/ppermute | solution.py:330
  46.5 0.3 shard_map.102
  46.9 2.0 %collective-permute-start.9 = (bf16[128,256]{1,0:T(8,128)(2,1)S(1)}, bf16[128,256]{1,0:T(8,128)(2,1)S(1)}, u32[]{:S(2)}, u32[]{:S(2)}) collective-permute-start(bf16[128,256]{1,0:T(8,128)(2,1)S(1)} %get-tuple-element.36.own), channel_id=1, source_target_pairs={{0,24},{4,28},{8,16},{12,20},{16,8},{20,12},{24,0},{28,4},{32,56},... | collective-permute-start | bytes 196616 | tf_op jit(solution)/shard_map/ppermute | solution.py:330
  48.9 2.4 %collective-permute-done.9.other = bf16[128,256]{1,0:T(8,128)(2,1)S(1)} collective-permute-done((bf16[128,256]{1,0:T(8,128)(2,1)S(1)}, bf16[128,256]{1,0:T(8,128)(2,1)S(1)}, u32[]{:S(2)}, u32[]{:S(2)}) %collective-permute-start.9) | collective-permute-done | bytes 65568 | tf_op jit(solution)/shard_map/ppermute | solution.py:330
  51.3 2.9 %collective-permute-start.10 = (bf16[256,256]{1,0:T(8,128)(2,1)S(1)}, bf16[256,256]{1,0:T(8,128)(2,1)S(1)}, u32[]{:S(2)}, u32[]{:S(2)}) collective-permute-start(bf16[256,256]{1,0:T(8,128)(2,1)S(1)} %constant_dynamic-update-slice_fusion), channel_id=1, source_target_pairs={{0,32},{4,36},{8,40},{12,44},{16,48},{20,52},{24,56},{28,252},{32,... | collective-permute-start | bytes 393224 | tf_op jit(solution)/shard_map/ppermute | solution.py:330
  54.1 2.1 %shard_map.110.refs_1_ = f32[1024,256]{1,0:T(8,128)S(1)} custom-call(s32[4,3]{1,0:T(4,128)S(1)} %copy-done.4, s32[4]{0:T(128)S(1)} %copy-done.5, bf16[4096,128]{1,0:T(8,128)(2,1)S(1)} %get-tuple-element.47.left, bf16[128,4096]{1,0:T(8,128)(2,1)S(1)} %get-tuple-element.48.right, bf16[4096,256]{1,0:T(8,128)(2,1)S(1)} %copy-done.2), custom_call_target="tpu_custom_call" | custom-call | flops 1610612736 | bytes 6291456 | tf_op jit(solution)/shard_map/pallas_call | solution.py:421
  56.2 2.9 %collective-permute-start.11 = (bf16[256,256]{1,0:T(8,128)(2,1)S(1)}, bf16[256,256]{1,0:T(8,128)(2,1)S(1)}, u32[]{:S(2)}, u32[]{:S(2)}) collective-permute-start(bf16[256,256]{1,0:T(8,128)(2,1)S(1)} %collective-permute-done.10.s1), channel_id=1, source_target_pairs={{0,32},{4,36},{8,40},{12,44},{16,48},{20,52},{24,56},{28,252},{32,... | collective-permute-start | bytes 393224 | tf_op jit(solution)/shard_map/ppermute | solution.py:330
  59.2 2.1 %shard_map.111.refs_2_ = f32[1024,256]{1,0:T(8,128)S(1)} custom-call(s32[4,3]{1,0:T(4,128)S(1)} %copy-done.4, s32[4]{0:T(128)S(1)} %copy-done.5, bf16[4096,128]{1,0:T(8,128)(2,1)S(1)} %get-tuple-element.47.left, bf16[128,4096]{1,0:T(8,128)(2,1)S(1)} %get-tuple-element.48.right, bf16[4096,256]{1,0:T(8,128)(2,1)S(1)} %copy-done.2), custom_call_target="tpu_custom_call" | custom-call | flops 1610612736 | bytes 6291456 | tf_op jit(solution)/shard_map/pallas_call | solution.py:421
  61.3 3.6 %collective-permute-start.23 = (bf16[64,4096]{1,0:T(8,128)(2,1)S(1)}, bf16[64,4096]{1,0:T(8,128)(2,1)S(1)}, u32[]{:S(2)}, u32[]{:S(2)}) collective-permute-start(bf16[64,4096]{1,0:T(8,128)(2,1)S(1)} %get-tuple-element.46.coords), channel_id=1, source_target_pairs={{0,4},{4,0},{8,12},{12,8},{16,20},{20,16},{24,28},{28,24},{32,36},... | collective-permute-start | bytes 1572872 | tf_op jit(solution)/shard_map/ppermute | solution.py:330
  64.8 1.3 %shard_map.105.field = f32[1024,256]{1,0:T(8,128)S(1)} custom-call(bf16[64,1024]{1,0:T(8,128)(2,1)S(1)} %get-tuple-element.44.coords, bf16[1024,256]{1,0:T(8,128)(2,1)S(1)} %get-tuple-element.45.leaf_skel), custom_call_target="tpu_custom_call" | custom-call | flops 1073741824 | bytes 2097152 | tf_op jit(solution)/shard_map/pallas_call | solution.py:408
  66.1 3.5 %collective-permute-start.12 = (bf16[256,256]{1,0:T(8,128)(2,1)S(1)}, bf16[256,256]{1,0:T(8,128)(2,1)S(1)}, u32[]{:S(2)}, u32[]{:S(2)}) collective-permute-start(bf16[256,256]{1,0:T(8,128)(2,1)S(1)} %collective-permute-done.11.s3), channel_id=1, source_target_pairs={{0,32},{4,36},{8,40},{12,44},{16,48},{20,52},{24,56},{28,252},{32,... | collective-permute-start | bytes 393224 | tf_op jit(solution)/shard_map/ppermute | solution.py:330
  69.6 2.1 %shard_map.107.refs_1_ = f32[1024,256]{1,0:T(8,128)S(1)} custom-call(s32[4,3]{1,0:T(4,128)S(1)} %copy-done.4, s32[4]{0:T(128)S(1)} %copy-done.5, bf16[4096,128]{1,0:T(8,128)(2,1)S(1)} %get-tuple-element.47.left, bf16[128,4096]{1,0:T(8,128)(2,1)S(1)} %get-tuple-element.48.right, bf16[4096,256]{1,0:T(8,128)(2,1)S(1)} %copy-done.2), custom_call_target="tpu_custom_call" | custom-call | flops 1610612736 | bytes 6291456 | tf_op jit(solution)/shard_map/pallas_call | solution.py:421
  71.7 0.8 collective-permute-done.12.s5
  72.5 3.5 %shard_map.108.refs_2_ = f32[1024,256]{1,0:T(8,128)S(1)} custom-call(s32[4,3]{1,0:T(4,128)S(1)} %copy-done.4, s32[4]{0:T(128)S(1)} %copy-done.5, bf16[4096,128]{1,0:T(8,128)(2,1)S(1)} %get-tuple-element.47.left, bf16[128,4096]{1,0:T(8,128)(2,1)S(1)} %get-tuple-element.48.right, bf16[4096,256]{1,0:T(8,128)(2,1)S(1)} %copy-done.2), custom_call_target="tpu_custom_call" | custom-call | flops 1610612736 | bytes 6291456 | tf_op jit(solution)/shard_map/pallas_call | solution.py:421
  75.9 2.9 %collective-permute-done.16.s6 = bf16[256,256]{1,0:T(8,128)(2,1)S(1)} collective-permute-done((bf16[256,256]{1,0:T(8,128)(2,1)S(1)}, bf16[256,256]{1,0:T(8,128)(2,1)S(1)}, u32[]{:S(2)}, u32[]{:S(2)}) %collective-permute-start.16) | collective-permute-done | bytes 131104 | tf_op jit(solution)/shard_map/ppermute | solution.py:330
  78.9 1.2 %collective-permute-start.13 = (bf16[256,256]{1,0:T(8,128)(2,1)S(1)}, bf16[256,256]{1,0:T(8,128)(2,1)S(1)}, u32[]{:S(2)}, u32[]{:S(2)}) collective-permute-start(bf16[256,256]{1,0:T(8,128)(2,1)S(1)} %collective-permute-done.12.s5), channel_id=1, source_target_pairs={{0,32},{4,36},{8,40},{12,44},{16,48},{20,52},{24,56},{28,252},{32,... | collective-permute-start | bytes 393224 | tf_op jit(solution)/shard_map/ppermute | solution.py:330
  80.1 2.2 %shard_map.103 = (f32[64,256]{1,0:T(8,128)S(1)}, f32[256,256]{1,0:T(8,128)S(1)}) custom-call(bf16[128,256]{1,0:T(8,128)(2,1)S(1)} %get-tuple-element.36.own, bf16[128,256]{1,0:T(8,128)(2,1)S(1)} %collective-permute-done.9.other, bf16[256,256]{1,0:T(8,128)(2,1)S(1)} %collective-permute-done.10.s1, bf16[256,256]{1,0:T(8,128)(2,1)S(1)} %collective-permute-done.14.s2, ...), custom_call_target="tpu_custom_call" | custom-call | flops 2147483648 | bytes 2097152 | tf_op jit(solution)/shard_map/pallas_call | solution.py:431
  82.3 0.4 collective-permute-done.13.s7
  82.7 3.7 %collective-permute-start.20 = (bf16[64,4096]{1,0:T(8,128)(2,1)S(1)}, bf16[64,4096]{1,0:T(8,128)(2,1)S(1)}, u32[]{:S(2)}, u32[]{:S(2)}) collective-permute-start(bf16[64,4096]{1,0:T(8,128)(2,1)S(1)} %get-tuple-element.46.coords), channel_id=1, source_target_pairs={{4,8},{12,16},{20,24},{28,32},{36,40},{44,48},{52,56},{60,64},{68,... | collective-permute-start | bytes 1572872 | tf_op jit(solution)/shard_map/ppermute | solution.py:330
  86.4 0.6 shard_map.104
  87.0 0.9 collective-permute-start.17
  87.9 1.7 %collective-permute-start.18 = (bf16[64,256]{1,0:T(8,128)(2,1)S(1)}, bf16[64,256]{1,0:T(8,128)(2,1)S(1)}, u32[]{:S(2)}, u32[]{:S(2)}) collective-permute-start(bf16[64,256]{1,0:T(8,128)(2,1)S(1)} %get-tuple-element.42), channel_id=1, source_target_pairs={{0,8},{4,12},{8,0},{12,4},{16,24},{20,28},{24,16},{28,20},{32,40},... | collective-permute-start | bytes 98312 | tf_op jit(solution)/shard_map/ppermute | solution.py:330
  89.6 2.3 %shard_map.112.refs_3_ = f32[2048,256]{1,0:T(8,128)S(1)} custom-call(s32[4,3]{1,0:T(4,128)S(1)} %copy-done.4, s32[4]{0:T(128)S(1)} %copy-done.5, bf16[4096,128]{1,0:T(8,128)(2,1)S(1)} %get-tuple-element.47.left, bf16[64,4096]{1,0:T(8,128)(2,1)S(1)} %collective-permute-done.23.coords, bf16[4096,256]{1,0:T(8,128)(2,1)S(1)} %collective-permute-done.24.refs_0_, ...), custom_call_target="tpu_custom_call" | custom-call | flops 3221225472 | bytes 12582912 | tf_op jit(solution)/shard_map/pallas_call | solution.py:451
  91.9 2.3 %shard_map.109.refs_2_ = f32[2048,256]{1,0:T(8,128)S(1)} custom-call(s32[4,3]{1,0:T(4,128)S(1)} %copy-done.4, s32[4]{0:T(128)S(1)} %copy-done.5, bf16[4096,128]{1,0:T(8,128)(2,1)S(1)} %get-tuple-element.47.left, bf16[64,4096]{1,0:T(8,128)(2,1)S(1)} %collective-permute-done.23.coords, bf16[4096,256]{1,0:T(8,128)(2,1)S(1)} %collective-permute-done.24.refs_0_, ...), custom_call_target="tpu_custom_call" | custom-call | flops 3221225472 | bytes 12582912 | tf_op jit(solution)/shard_map/pallas_call | solution.py:451
  94.3 0.0 copy-start
  94.3 0.0 copy-start.1
  94.3 1.1 %collective-permute-start.19 = (bf16[64,256]{1,0:T(8,128)(2,1)S(1)}, bf16[64,256]{1,0:T(8,128)(2,1)S(1)}, u32[]{:S(2)}, u32[]{:S(2)}) collective-permute-start(bf16[64,256]{1,0:T(8,128)(2,1)S(1)} %get-tuple-element.43), channel_id=1, source_target_pairs={{0,12},{4,8},{8,4},{12,0},{16,28},{20,24},{24,20},{28,16},{32,44},... | collective-permute-start | bytes 98312 | tf_op jit(solution)/shard_map/ppermute | solution.py:330
  95.4 6.9 %shard_map.113.near = f32[4096,256]{1,0:T(8,128)S(1)} custom-call(s32[4,3]{1,0:T(4,128)S(1)} %copy-done.4, s32[4]{0:T(128)S(1)} %copy-done.5, bf16[4096,128]{1,0:T(8,128)(2,1)S(1)} %get-tuple-element.47.left, bf16[64,4096]{1,0:T(8,128)(2,1)S(1)} %collective-permute-done.20.coords, bf16[4096,256]{1,0:T(8,128)(2,1)S(1)} %collective-permute-done.21.refs_0_, ...), custom_call_target="tpu_custom_call" | custom-call | flops 3221225472 | bytes 12582912 | tf_op jit(solution)/shard_map/pallas_call | solution.py:451
  102.3 3.8 %finish.1 = f32[4096,256]{1,0:T(8,128)} custom-call(bf16[64,256]{1,0:T(8,128)(2,1)S(1)} %get-tuple-element.40.t0, bf16[64,256]{1,0:T(8,128)(2,1)S(1)} %collective-permute-done.17.t1, bf16[64,256]{1,0:T(8,128)(2,1)S(1)} %collective-permute-done.18.t2, bf16[64,256]{1,0:T(8,128)(2,1)S(1)} %collective-permute-done.19.t3, bf16[256,1024]{1,0:T(8,128)(2,1)S(1)} %copy-done.1, ...), custom_call_target="tpu_custom_call" | custom-call | flops 671088640 | bytes 10485760 | tf_op jit(solution)/shard_map/finish/pallas_call | solution.py:467
  (40 shorter events, 0.1 us)
Async XLA Ops:
  0.0 87.9 %collective-permute-start.24 = (bf16[4096,256]{1,0:T(8,128)(2,1)}, bf16[4096,256]{1,0:T(8,128)(2,1)S(1)}, u32[]{:S(2)}, u32[]{:S(2)}) collective-permute-start(bf16[4096,256]{1,0:T(8,128)(2,1)} %weights.9), channel_id=1, source_target_pairs={{0,4},{4,0},{8,12},{12,8},{16,20},{20,16},{24,28},{28,24},{32,36},... | collective-permute-start | bytes 6291464 | tf_op jit(solution)/shard_map/ppermute | solution.py:330
  0.7 12.4 %copy-start.2 = (bf16[4096,256]{1,0:T(8,128)(2,1)S(1)}, bf16[4096,256]{1,0:T(8,128)(2,1)}, u32[]{:S(2)}) copy-start(bf16[4096,256]{1,0:T(8,128)(2,1)} %weights.9) | copy-start | bytes 6291460
  0.7 13.2 %copy-start.3 = (bf16[64,1024]{1,0:T(8,128)(2,1)S(1)}, bf16[64,1024]{1,0:T(8,128)(2,1)}, u32[]{:S(2)}) copy-start(bf16[64,1024]{1,0:T(8,128)(2,1)} %g0.1) | copy-start | bytes 393220
  0.7 14.6 %copy-start.7 = (s32[16,256]{1,0:T(8,128)S(1)}, s32[16,256]{1,0:T(8,128)}, u32[]{:S(2)}) copy-start(s32[16,256]{1,0:T(8,128)} %param.17) | copy-start | bytes 49156
  0.7 14.6 %copy-start.8 = (s32[4,256]{1,0:T(4,128)S(1)}, s32[4,256]{1,0:T(4,128)}, u32[]{:S(2)}) copy-start(s32[4,256]{1,0:T(4,128)} %param.15) | copy-start | bytes 12292
  0.7 14.6 %copy-start.9 = (s32[1,256]{1,0:T(1,128)S(1)}, s32[1,256]{1,0:T(1,128)}, u32[]{:S(2)}) copy-start(s32[1,256]{1,0:T(1,128)} %param.16) | copy-start | bytes 3076
  0.7 14.6 %copy-start.6 = (bf16[4096,16]{0,1:T(8,128)(2,1)S(1)}, bf16[4096,16]{0,1:T(8,128)(2,1)}, u32[]{:S(2)}) copy-start(bf16[4096,16]{0,1:T(8,128)(2,1)} %param.10) | copy-start | bytes 393220
  0.7 12.3 %collective-permute-start = (bf16[16,4096]{1,0:T(8,128)(2,1)}, bf16[16,4096]{1,0:T(8,128)(2,1)S(1)}, u32[]{:S(2)}, u32[]{:S(2)}) collective-permute-start(bf16[16,4096]{1,0:T(8,128)(2,1)} %bitcast.1), channel_id=1, source_target_pairs={{0,1},{1,2},{2,3},{3,0},{4,5},{5,6},{6,7},{7,4},{8,9},{9,10},{10,1... | collective-permute-start | bytes 393224 | tf_op jit(solution)/shard_map/ppermute | solution.py:330
  2.0 11.9 %collective-permute-start.1 = (bf16[16,4096]{1,0:T(8,128)(2,1)}, bf16[16,4096]{1,0:T(8,128)(2,1)S(1)}, u32[]{:S(2)}, u32[]{:S(2)}) collective-permute-start(bf16[16,4096]{1,0:T(8,128)(2,1)} %bitcast.2), channel_id=1, source_target_pairs={{0,2},{1,3},{2,0},{3,1},{4,6},{5,7},{6,4},{7,5},{8,10},{9,11},{10,... | collective-permute-start | bytes 393224 | tf_op jit(solution)/shard_map/ppermute | solution.py:330
  4.4 10.8 %collective-permute-start.2 = (bf16[16,4096]{1,0:T(8,128)(2,1)}, bf16[16,4096]{1,0:T(8,128)(2,1)S(1)}, u32[]{:S(2)}, u32[]{:S(2)}) collective-permute-start(bf16[16,4096]{1,0:T(8,128)(2,1)} %bitcast.3), channel_id=1, source_target_pairs={{0,3},{1,0},{2,1},{3,2},{4,7},{5,4},{6,5},{7,6},{8,11},{9,8},{10,9... | collective-permute-start | bytes 393224 | tf_op jit(solution)/shard_map/ppermute | solution.py:330
  5.6 89.8 %collective-permute-start.21 = (bf16[4096,256]{1,0:T(8,128)(2,1)}, bf16[4096,256]{1,0:T(8,128)(2,1)S(1)}, u32[]{:S(2)}, u32[]{:S(2)}) collective-permute-start(bf16[4096,256]{1,0:T(8,128)(2,1)} %weights.9), channel_id=1, source_target_pairs={{4,8},{12,16},{20,24},{36,40},{44,48},{52,56},{68,72},{76,80},{84,... | collective-permute-start | bytes 6291464 | tf_op jit(solution)/shard_map/ppermute | solution.py:330
  13.0 82.3 %collective-permute-start.22 = (bf16[4096,256]{1,0:T(8,128)(2,1)S(1)}, bf16[4096,256]{1,0:T(8,128)(2,1)S(1)}, u32[]{:S(2)}, u32[]{:S(2)}) collective-permute-start(bf16[4096,256]{1,0:T(8,128)(2,1)S(1)} %copy-done.2), channel_id=1, source_target_pairs={{28,32},{60,64},{92,96},{124,128},{156,160},{188,192},{220,224},{3... | collective-permute-start | bytes 6291464 | tf_op jit(solution)/shard_map/ppermute | solution.py:330
  13.9 21.7 %collective-permute-start.7 = (bf16[64,1024]{1,0:T(8,128)(2,1)S(1)}, bf16[64,1024]{1,0:T(8,128)(2,1)S(1)}, u32[]{:S(2)}, u32[]{:S(2)}) collective-permute-start(bf16[64,1024]{1,0:T(8,128)(2,1)S(1)} %copy-done.3), channel_id=1, source_target_pairs={{0,8},{4,12},{8,0},{12,4},{16,24},{20,28},{24,16},{28,20},{32,40},... | collective-permute-start | bytes 393224 | tf_op jit(solution)/shard_map/ppermute | solution.py:330
  15.3 21.7 %collective-permute-start.6 = (bf16[64,1024]{1,0:T(8,128)(2,1)S(1)}, bf16[64,1024]{1,0:T(8,128)(2,1)S(1)}, u32[]{:S(2)}, u32[]{:S(2)}) collective-permute-start(bf16[64,1024]{1,0:T(8,128)(2,1)S(1)} %copy-done.3), channel_id=1, source_target_pairs={{0,4},{4,0},{8,12},{12,8},{16,20},{20,16},{24,28},{28,24},{32,36},... | collective-permute-start | bytes 393224 | tf_op jit(solution)/shard_map/ppermute | solution.py:330
  15.3 38.8 %copy-start.4 = (s32[4,3]{1,0:T(4,128)S(1)}, s32[4,3]{1,0:T(4,128)}, u32[]{:S(2)}) copy-start(s32[4,3]{1,0:T(4,128)} %near_list.13) | copy-start | bytes 148
  15.3 38.8 %copy-start.5 = (s32[4]{0:T(128)S(1)}, s32[4]{0:T(128)}, u32[]{:S(2)}) copy-start(s32[4]{0:T(128)} %near_count.13) | copy-start | bytes 52
  35.5 2.4 %collective-permute-start.3 = (bf16[192,256]{1,0:T(8,128)(2,1)S(1)}, bf16[192,256]{1,0:T(8,128)(2,1)S(1)}, u32[]{:S(2)}, u32[]{:S(2)}) collective-permute-start(bf16[192,256]{1,0:T(8,128)(2,1)S(1)} %get-tuple-element.33), channel_id=1, source_target_pairs={{0,4},{4,0},{8,12},{12,8},{16,20},{20,16},{24,28},{28,24},{32,36},... | collective-permute-start | bytes 294920 | tf_op jit(solution)/shard_map/ppermute | solution.py:330
  37.0 4.3 %collective-permute-start.4 = (bf16[192,256]{1,0:T(8,128)(2,1)S(1)}, bf16[192,256]{1,0:T(8,128)(2,1)S(1)}, u32[]{:S(2)}, u32[]{:S(2)}) collective-permute-start(bf16[192,256]{1,0:T(8,128)(2,1)S(1)} %get-tuple-element.34), channel_id=1, source_target_pairs={{0,8},{4,12},{8,0},{12,4},{16,24},{20,28},{24,16},{28,20},{32,40},... | collective-permute-start | bytes 294920 | tf_op jit(solution)/shard_map/ppermute | solution.py:330
  37.9 8.6 %collective-permute-start.8 = (bf16[64,1024]{1,0:T(8,128)(2,1)S(1)}, bf16[64,1024]{1,0:T(8,128)(2,1)S(1)}, u32[]{:S(2)}, u32[]{:S(2)}) collective-permute-start(bf16[64,1024]{1,0:T(8,128)(2,1)S(1)} %collective-permute-done.7.g2), channel_id=1, source_target_pairs={{0,4},{4,0},{8,12},{12,8},{16,20},{20,16},{24,28},{28,24},{32,36},... | collective-permute-start | bytes 393224 | tf_op jit(solution)/shard_map/ppermute | solution.py:330
  41.3 5.2 %collective-permute-start.5 = (bf16[192,256]{1,0:T(8,128)(2,1)S(1)}, bf16[192,256]{1,0:T(8,128)(2,1)S(1)}, u32[]{:S(2)}, u32[]{:S(2)}) collective-permute-start(bf16[192,256]{1,0:T(8,128)(2,1)S(1)} %get-tuple-element.35), channel_id=1, source_target_pairs={{0,12},{4,8},{8,4},{12,0},{16,28},{20,24},{24,20},{28,16},{32,44},... | collective-permute-start | bytes 294920 | tf_op jit(solution)/shard_map/ppermute | solution.py:330
  46.9 4.4 %collective-permute-start.9 = (bf16[128,256]{1,0:T(8,128)(2,1)S(1)}, bf16[128,256]{1,0:T(8,128)(2,1)S(1)}, u32[]{:S(2)}, u32[]{:S(2)}) collective-permute-start(bf16[128,256]{1,0:T(8,128)(2,1)S(1)} %get-tuple-element.36.own), channel_id=1, source_target_pairs={{0,24},{4,28},{8,16},{12,20},{16,8},{20,12},{24,0},{28,4},{32,56},... | collective-permute-start | bytes 196616 | tf_op jit(solution)/shard_map/ppermute | solution.py:330
  51.3 4.9 %collective-permute-start.10 = (bf16[256,256]{1,0:T(8,128)(2,1)S(1)}, bf16[256,256]{1,0:T(8,128)(2,1)S(1)}, u32[]{:S(2)}, u32[]{:S(2)}) collective-permute-start(bf16[256,256]{1,0:T(8,128)(2,1)S(1)} %constant_dynamic-update-slice_fusion), channel_id=1, source_target_pairs={{0,32},{4,36},{8,40},{12,44},{16,48},{20,52},{24,56},{28,252},{32,... | collective-permute-start | bytes 393224 | tf_op jit(solution)/shard_map/ppermute | solution.py:330
  54.1 5.0 %collective-permute-start.14 = (bf16[256,256]{1,0:T(8,128)(2,1)S(1)}, bf16[256,256]{1,0:T(8,128)(2,1)S(1)}, u32[]{:S(2)}, u32[]{:S(2)}) collective-permute-start(bf16[256,256]{1,0:T(8,128)(2,1)S(1)} %constant_dynamic-update-slice_fusion), channel_id=1, source_target_pairs={{0,224},{4,228},{8,232},{12,236},{16,240},{20,244},{24,248},{28,60... | collective-permute-start | bytes 393224 | tf_op jit(solution)/shard_map/ppermute | solution.py:330
  56.2 5.0 %collective-permute-start.11 = (bf16[256,256]{1,0:T(8,128)(2,1)S(1)}, bf16[256,256]{1,0:T(8,128)(2,1)S(1)}, u32[]{:S(2)}, u32[]{:S(2)}) collective-permute-start(bf16[256,256]{1,0:T(8,128)(2,1)S(1)} %collective-permute-done.10.s1), channel_id=1, source_target_pairs={{0,32},{4,36},{8,40},{12,44},{16,48},{20,52},{24,56},{28,252},{32,... | collective-permute-start | bytes 393224 | tf_op jit(solution)/shard_map/ppermute | solution.py:330
  59.2 7.0 %collective-permute-start.15 = (bf16[256,256]{1,0:T(8,128)(2,1)S(1)}, bf16[256,256]{1,0:T(8,128)(2,1)S(1)}, u32[]{:S(2)}, u32[]{:S(2)}) collective-permute-start(bf16[256,256]{1,0:T(8,128)(2,1)S(1)} %collective-permute-done.14.s2), channel_id=1, source_target_pairs={{0,224},{4,228},{8,232},{12,236},{16,240},{20,244},{24,248},{28,60... | collective-permute-start | bytes 393224 | tf_op jit(solution)/shard_map/ppermute | solution.py:330
  61.3 25.7 %collective-permute-start.23 = (bf16[64,4096]{1,0:T(8,128)(2,1)S(1)}, bf16[64,4096]{1,0:T(8,128)(2,1)S(1)}, u32[]{:S(2)}, u32[]{:S(2)}) collective-permute-start(bf16[64,4096]{1,0:T(8,128)(2,1)S(1)} %get-tuple-element.46.coords), channel_id=1, source_target_pairs={{0,4},{4,0},{8,12},{12,8},{16,20},{20,16},{24,28},{28,24},{32,36},... | collective-permute-start | bytes 1572872 | tf_op jit(solution)/shard_map/ppermute | solution.py:330
  66.1 6.3 %collective-permute-start.12 = (bf16[256,256]{1,0:T(8,128)(2,1)S(1)}, bf16[256,256]{1,0:T(8,128)(2,1)S(1)}, u32[]{:S(2)}, u32[]{:S(2)}) collective-permute-start(bf16[256,256]{1,0:T(8,128)(2,1)S(1)} %collective-permute-done.11.s3), channel_id=1, source_target_pairs={{0,32},{4,36},{8,40},{12,44},{16,48},{20,52},{24,56},{28,252},{32,... | collective-permute-start | bytes 393224 | tf_op jit(solution)/shard_map/ppermute | solution.py:330
  72.5 6.4 %collective-permute-start.16 = (bf16[256,256]{1,0:T(8,128)(2,1)S(1)}, bf16[256,256]{1,0:T(8,128)(2,1)S(1)}, u32[]{:S(2)}, u32[]{:S(2)}) collective-permute-start(bf16[256,256]{1,0:T(8,128)(2,1)S(1)} %collective-permute-done.15.s4), channel_id=1, source_target_pairs={{0,224},{4,228},{8,232},{12,236},{16,240},{20,244},{24,248},{28,60... | collective-permute-start | bytes 393224 | tf_op jit(solution)/shard_map/ppermute | solution.py:330
  78.9 3.8 %collective-permute-start.13 = (bf16[256,256]{1,0:T(8,128)(2,1)S(1)}, bf16[256,256]{1,0:T(8,128)(2,1)S(1)}, u32[]{:S(2)}, u32[]{:S(2)}) collective-permute-start(bf16[256,256]{1,0:T(8,128)(2,1)S(1)} %collective-permute-done.12.s5), channel_id=1, source_target_pairs={{0,32},{4,36},{8,40},{12,44},{16,48},{20,52},{24,56},{28,252},{32,... | collective-permute-start | bytes 393224 | tf_op jit(solution)/shard_map/ppermute | solution.py:330
  82.7 11.6 %collective-permute-start.20 = (bf16[64,4096]{1,0:T(8,128)(2,1)S(1)}, bf16[64,4096]{1,0:T(8,128)(2,1)S(1)}, u32[]{:S(2)}, u32[]{:S(2)}) collective-permute-start(bf16[64,4096]{1,0:T(8,128)(2,1)S(1)} %get-tuple-element.46.coords), channel_id=1, source_target_pairs={{4,8},{12,16},{20,24},{28,32},{36,40},{44,48},{52,56},{60,64},{68,... | collective-permute-start | bytes 1572872 | tf_op jit(solution)/shard_map/ppermute | solution.py:330
  87.0 15.2 %collective-permute-start.17 = (bf16[64,256]{1,0:T(8,128)(2,1)S(1)}, bf16[64,256]{1,0:T(8,128)(2,1)S(1)}, u32[]{:S(2)}, u32[]{:S(2)}) collective-permute-start(bf16[64,256]{1,0:T(8,128)(2,1)S(1)} %get-tuple-element.41), channel_id=1, source_target_pairs={{0,4},{4,0},{8,12},{12,8},{16,20},{20,16},{24,28},{28,24},{32,36},... | collective-permute-start | bytes 98312 | tf_op jit(solution)/shard_map/ppermute | solution.py:330
  87.9 14.4 %collective-permute-start.18 = (bf16[64,256]{1,0:T(8,128)(2,1)S(1)}, bf16[64,256]{1,0:T(8,128)(2,1)S(1)}, u32[]{:S(2)}, u32[]{:S(2)}) collective-permute-start(bf16[64,256]{1,0:T(8,128)(2,1)S(1)} %get-tuple-element.42), channel_id=1, source_target_pairs={{0,8},{4,12},{8,0},{12,4},{16,24},{20,28},{24,16},{28,20},{32,40},... | collective-permute-start | bytes 98312 | tf_op jit(solution)/shard_map/ppermute | solution.py:330
  94.3 8.0 %copy-start = (bf16[1024,1024]{1,0:T(8,128)(2,1)S(1)}, bf16[1024,1024]{1,0:T(8,128)(2,1)}, u32[]{:S(2)}) copy-start(bf16[1024,1024]{1,0:T(8,128)(2,1)} %basis.3) | copy-start | bytes 6291460
  94.3 8.0 %copy-start.1 = (bf16[256,1024]{1,0:T(8,128)(2,1)S(1)}, bf16[256,1024]{1,0:T(8,128)(2,1)}, u32[]{:S(2)}) copy-start(bf16[256,1024]{1,0:T(8,128)(2,1)} %transfer.3) | copy-start | bytes 1572868
  94.3 8.0 %collective-permute-start.19 = (bf16[64,256]{1,0:T(8,128)(2,1)S(1)}, bf16[64,256]{1,0:T(8,128)(2,1)S(1)}, u32[]{:S(2)}, u32[]{:S(2)}) collective-permute-start(bf16[64,256]{1,0:T(8,128)(2,1)S(1)} %get-tuple-element.43), channel_id=1, source_target_pairs={{0,12},{4,8},{8,4},{12,0},{16,28},{20,24},{24,20},{28,16},{32,44},... | collective-permute-start | bytes 98312 | tf_op jit(solution)/shard_map/ppermute | solution.py:330

commit v3 on v2

--- a/solution.py
+++ b/solution.py
@@ -8,6 +8,7 @@
 from jax.sharding import PartitionSpec as P
 
 LEAF = 1024
+ROWS, COLS = "leaf", "cols"
 RANK = 256
 SHARPNESS = 2.0
 LOG2E = 1.4426950408889634
@@ -33,7 +34,7 @@
 
 
 def call(body, outs, in_specs, scratch=(), flops=0, exps=0, nbytes=0, vmem=8):
-    return pl.pallas_call(
+    kernel = pl.pallas_call(
         body,
         out_shape=[jax.ShapeDtypeStruct(s, d) for s, d in outs],
         in_specs=in_specs,
@@ -42,6 +43,7 @@
         cost_estimate=pl.CostEstimate(flops=flops, transcendentals=exps, bytes_accessed=nbytes),
         compiler_params=pltpu.CompilerParams(vmem_limit_bytes=vmem * 1024 * 1024),
     )
+    return kernel
 
 
 def one_hot(index_row, rows):
@@ -129,7 +131,7 @@
 
 
 def select_body(p0, p1, p2, p3, picks, nodes, coords, leaf_coords, k0, k1, k2, k3):
-    position = lax.axis_index("leaf")
+    position = lax.axis_index(ROWS)
     share = column_share(position)
     for n, part in enumerate((p0, p1, p2, p3)):
         coords[pl.ds(n * 16, 16), :] = part[...]
@@ -179,7 +181,7 @@
 
 
 def near_own_body(dim, leaf, near_list, near_count, left, right, weights, out):
-    base = lax.axis_index("leaf") * 4
+    base = lax.axis_index(ROWS) * 4
     out[...] = jnp.zeros_like(out)
 
     def slot_step(slot, carry):
@@ -204,7 +206,7 @@
     half = s0.shape[0]
     out[:half, :] = s0[...]
     out[half:, :] = s1[...]
-    position = lax.axis_index("leaf")
+    position = lax.axis_index(ROWS)
     even = position % 2 == 0
     edge = (position % 8 == 0) | (position % 8 == 7)
     first = jnp.where(even if inside else jnp.logical_not(even), position + 1, position - 1) * 4
@@ -242,7 +244,7 @@
 
 
 def group_body(r0, r1, r2, r3, g0, g1, g2, g3, packed, transfer):
-    member = lax.axis_index("leaf") % 4
+    member = lax.axis_index(ROWS) % 4
     for flip, part in enumerate((g0, g1, g2, g3)):
         rows = pl.ds(pl.multiple_of((member ^ flip) * 64, 64), 64)
         transfer[rows, :] = part[...]
@@ -282,7 +284,7 @@
 
 
 def top_body(dim, own, s7, top_start, fields, transfer, *outs):
-    member = lax.axis_index("leaf") % 4
+    member = lax.axis_index(ROWS) % 4
     own_left = left_form(own[64:128, :])
     top = top_part(own_left, [(s7, 0), (s7, 128)], dim, top_start[...]).astype(BF)
     for i in range(4):
@@ -292,7 +294,7 @@
 
 def finish_body(t0, t1, t2, t3, transfer, basis, field, near, out, total):
     leaf = pl.program_id(0)
-    share = column_share(lax.axis_index("leaf"))
+    share = column_share(lax.axis_index(ROWS))
 
     @pl.when(leaf == 0)
     def _():
@@ -320,13 +322,13 @@
     near_list,
     near_count,
 ):
-    count = lax.axis_size("leaf")
-    cols_count = lax.axis_size("cols")
+    count = lax.axis_size(ROWS)
+    cols_count = lax.axis_size(COLS)
     dim = points.shape[1] * cols_count
     width = weights.shape[1]
     rows = points.shape[0]
 
-    def moved(value, pairs, axis="leaf"):
+    def moved(value, pairs, axis=ROWS):
         return lax.ppermute(value, axis, pairs)
 
     def flipped(value, flip):
@@ -334,7 +336,7 @@
 
     def shifted(value, step):
         pairs = [(i, (i + step) % cols_count) for i in range(cols_count)]
-        return moved(value, pairs, "cols")
+        return moved(value, pairs, COLS)
 
     def raised(value, step):
         return moved(value, [(i, (i + (-8 if i % 8 == 7 else 8) * step) % count) for i in range(count)])
@@ -475,22 +477,21 @@
         cost_estimate=pl.CostEstimate(
             flops=2 * 5 * RANK * LEAF * width, transcendentals=0, bytes_accessed=10 * 1024 * 1024
         ),
-        name="finish",
     )(*returned, dev_transfer, leaf_basis, leaf_field, near_sum)
 
 
 def solution(mesh):
     in_specs = (
-        P("leaf", "cols"),
-        P("leaf", "cols"),
-        P("leaf", None),
-        P("leaf", None),
-        P("leaf", None),
-        P("leaf", None),
-        P("leaf", None),
+        P(ROWS, COLS),
+        P(ROWS, COLS),
+        P(ROWS, None),
+        P(ROWS, None),
+        P(ROWS, None),
+        P(ROWS, None),
+        P(ROWS, None),
         P(),
-        P("leaf", None),
-        P("leaf"),
+        P(ROWS, None),
+        P(ROWS),
     )
-    out_specs = P("leaf", "cols")
+    out_specs = P(ROWS, COLS)
     return jax.shard_map(per_device, mesh=mesh, in_specs=in_specs, out_specs=out_specs, check_vma=False)

time: 108 us -> 108 us (level)
  no operation moved by 1% of the time
where the time goes in v3:
time: 108 us; the launch traced here: 106 us
  starting transfers between devices  38.5 us (36%)
  Pallas kernels  34.1 us (32%)
  waiting for transfers between devices  33.1 us (31%)
    ppermute x25, starting transfers between devices, moved(): return lax.ppermute(value, axis, pairs)  38.5 us
    ppermute x25, waiting for transfers between devices, moved(): return lax.ppermute(value, axis, pairs)  33.1 us
    pallas_call x3, Pallas kernels, near_neighbour(): call(functools.partial(near_neighbour_body, dim, inside, opening), [((2 *...  11.5 us
    pallas_call x4, Pallas kernels, per_device(): call(functools.partial(near_own_body, dim, first), [((LEAF, width), F32)]...  9.73 us
    pallas_call x1, Pallas kernels, per_device(): pl.pallas_call(finish_body, grid=(4,), out_shape=jax.ShapeDtypeStruct((ro...  3.81 us
    pallas_call x1, Pallas kernels, per_device(): call(skel_body, [((4 * RANK, width), BF), ((width, RANK), BF)], [HBM] * 3...  3.47 us
    pallas_call x1, Pallas kernels, per_device(): call(functools.partial(top_start_body, dim), [((64, RANK), F32), ((4 * 64...  2.19 us
  transfers between devices with their start and end apart: 25, of which 8 were waited for; matrix products, arithmetic and copies ran while one was open for 0% of the time, Pallas kernels for 29%

profile of v3, /device:TPU:97, one launch (start us, length us, event | category | flops | bytes accessed | tf_op | source)
XLA Modules:
  0.0 106.1 jit_solution(16172661888323192961)
XLA Ops:
  0.0 0.7 collective-permute-start.24
  0.7 1.3 %collective-permute-start = (bf16[16,4096]{1,0:T(8,128)(2,1)}, bf16[16,4096]{1,0:T(8,128)(2,1)S(1)}, u32[]{:S(2)}, u32[]{:S(2)}) collective-permute-start(bf16[16,4096]{1,0:T(8,128)(2,1)} %bitcast.1), channel_id=1, source_target_pairs={{0,1},{1,2},{2,3},{3,0},{4,5},{5,6},{6,7},{7,4},{8,9},{9,10},{10,1... | collective-permute-start | bytes 393224 | tf_op jit(solution)/shard_map/ppermute | solution.py:332
  2.0 2.5 %collective-permute-start.1 = (bf16[16,4096]{1,0:T(8,128)(2,1)}, bf16[16,4096]{1,0:T(8,128)(2,1)S(1)}, u32[]{:S(2)}, u32[]{:S(2)}) collective-permute-start(bf16[16,4096]{1,0:T(8,128)(2,1)} %bitcast.2), channel_id=1, source_target_pairs={{0,2},{1,3},{2,0},{3,1},{4,6},{5,7},{6,4},{7,5},{8,10},{9,11},{10,... | collective-permute-start | bytes 393224 | tf_op jit(solution)/shard_map/ppermute | solution.py:332
  4.4 1.2 %collective-permute-start.2 = (bf16[16,4096]{1,0:T(8,128)(2,1)}, bf16[16,4096]{1,0:T(8,128)(2,1)S(1)}, u32[]{:S(2)}, u32[]{:S(2)}) collective-permute-start(bf16[16,4096]{1,0:T(8,128)(2,1)} %bitcast.3), channel_id=1, source_target_pairs={{0,3},{1,0},{2,1},{3,2},{4,7},{5,4},{6,5},{7,6},{8,11},{9,8},{10,9... | collective-permute-start | bytes 393224 | tf_op jit(solution)/shard_map/ppermute | solution.py:332
  5.6 3.9 %collective-permute-start.21 = (bf16[4096,256]{1,0:T(8,128)(2,1)}, bf16[4096,256]{1,0:T(8,128)(2,1)S(1)}, u32[]{:S(2)}, u32[]{:S(2)}) collective-permute-start(bf16[4096,256]{1,0:T(8,128)(2,1)} %weights.9), channel_id=1, source_target_pairs={{4,8},{12,16},{20,24},{36,40},{44,48},{52,56},{68,72},{76,80},{84,... | collective-permute-start | bytes 6291464 | tf_op jit(solution)/shard_map/ppermute | solution.py:332
  9.5 3.5 %shard_map.100 = (bf16[1024,256]{1,0:T(8,128)(2,1)S(1)}, bf16[256,256]{1,0:T(8,128)(2,1)S(1)}) custom-call(bf16[4096,256]{1,0:T(8,128)(2,1)} %weights.9, bf16[1024,1024]{1,0:T(8,128)(2,1)} %basis.3, bf16[256,1024]{1,0:T(8,128)(2,1)} %transfer.3), custom_call_target="tpu_custom_call" | custom-call | flops 671088640 | bytes 5242880 | tf_op jit(solution)/shard_map/pallas_call | solution.py:358
  13.0 0.8 collective-permute-start.22
  13.9 1.4 %collective-permute-start.7 = (bf16[64,1024]{1,0:T(8,128)(2,1)S(1)}, bf16[64,1024]{1,0:T(8,128)(2,1)S(1)}, u32[]{:S(2)}, u32[]{:S(2)}) collective-permute-start(bf16[64,1024]{1,0:T(8,128)(2,1)S(1)} %copy-done.3), channel_id=1, source_target_pairs={{0,8},{4,12},{8,0},{12,4},{16,24},{20,28},{24,16},{28,20},{32,40},... | collective-permute-start | bytes 393224 | tf_op jit(solution)/shard_map/ppermute | solution.py:332
  15.3 0.0 copy-start.4
  15.3 0.0 copy-start.5
  15.3 0.8 shard_map.101
  16.1 19.4 %collective-permute-done.7.g2 = bf16[64,1024]{1,0:T(8,128)(2,1)S(1)} collective-permute-done((bf16[64,1024]{1,0:T(8,128)(2,1)S(1)}, bf16[64,1024]{1,0:T(8,128)(2,1)S(1)}, u32[]{:S(2)}, u32[]{:S(2)}) %collective-permute-start.7) | collective-permute-done | bytes 131104 | tf_op jit(solution)/shard_map/ppermute | solution.py:332
  35.5 1.4 %collective-permute-start.3 = (bf16[192,256]{1,0:T(8,128)(2,1)S(1)}, bf16[192,256]{1,0:T(8,128)(2,1)S(1)}, u32[]{:S(2)}, u32[]{:S(2)}) collective-permute-start(bf16[192,256]{1,0:T(8,128)(2,1)S(1)} %get-tuple-element.33), channel_id=1, source_target_pairs={{0,4},{4,0},{8,12},{12,8},{16,20},{20,16},{24,28},{28,24},{32,36},... | collective-permute-start | bytes 294920 | tf_op jit(solution)/shard_map/ppermute | solution.py:332
  37.0 0.5 collective-permute-start.4
  37.4 0.5 collective-permute-done.3.r1
  37.9 0.4 collective-permute-start.8
  38.3 3.1 %collective-permute-done.4.r2 = bf16[192,256]{1,0:T(8,128)(2,1)S(1)} collective-permute-done((bf16[192,256]{1,0:T(8,128)(2,1)S(1)}, bf16[192,256]{1,0:T(8,128)(2,1)S(1)}, u32[]{:S(2)}, u32[]{:S(2)}) %collective-permute-start.4) | collective-permute-done | bytes 98336 | tf_op jit(solution)/shard_map/ppermute | solution.py:332
  41.3 1.2 %collective-permute-start.5 = (bf16[192,256]{1,0:T(8,128)(2,1)S(1)}, bf16[192,256]{1,0:T(8,128)(2,1)S(1)}, u32[]{:S(2)}, u32[]{:S(2)}) collective-permute-start(bf16[192,256]{1,0:T(8,128)(2,1)S(1)} %get-tuple-element.35), channel_id=1, source_target_pairs={{0,12},{4,8},{8,4},{12,0},{16,28},{20,24},{24,20},{28,16},{32,44},... | collective-permute-start | bytes 294920 | tf_op jit(solution)/shard_map/ppermute | solution.py:332
  42.5 0.4 shard_map.106
  42.9 3.6 %collective-permute-done.5.r3 = bf16[192,256]{1,0:T(8,128)(2,1)S(1)} collective-permute-done((bf16[192,256]{1,0:T(8,128)(2,1)S(1)}, bf16[192,256]{1,0:T(8,128)(2,1)S(1)}, u32[]{:S(2)}, u32[]{:S(2)}) %collective-permute-start.5) | collective-permute-done | bytes 98336 | tf_op jit(solution)/shard_map/ppermute | solution.py:332
  46.5 0.3 shard_map.102
  46.9 2.0 %collective-permute-start.9 = (bf16[128,256]{1,0:T(8,128)(2,1)S(1)}, bf16[128,256]{1,0:T(8,128)(2,1)S(1)}, u32[]{:S(2)}, u32[]{:S(2)}) collective-permute-start(bf16[128,256]{1,0:T(8,128)(2,1)S(1)} %get-tuple-element.36.own), channel_id=1, source_target_pairs={{0,24},{4,28},{8,16},{12,20},{16,8},{20,12},{24,0},{28,4},{32,56},... | collective-permute-start | bytes 196616 | tf_op jit(solution)/shard_map/ppermute | solution.py:332
  48.9 2.4 %collective-permute-done.9.other = bf16[128,256]{1,0:T(8,128)(2,1)S(1)} collective-permute-done((bf16[128,256]{1,0:T(8,128)(2,1)S(1)}, bf16[128,256]{1,0:T(8,128)(2,1)S(1)}, u32[]{:S(2)}, u32[]{:S(2)}) %collective-permute-start.9) | collective-permute-done | bytes 65568 | tf_op jit(solution)/shard_map/ppermute | solution.py:332
  51.3 2.9 %collective-permute-start.10 = (bf16[256,256]{1,0:T(8,128)(2,1)S(1)}, bf16[256,256]{1,0:T(8,128)(2,1)S(1)}, u32[]{:S(2)}, u32[]{:S(2)}) collective-permute-start(bf16[256,256]{1,0:T(8,128)(2,1)S(1)} %constant_dynamic-update-slice_fusion), channel_id=1, source_target_pairs={{0,32},{4,36},{8,40},{12,44},{16,48},{20,52},{24,56},{28,252},{32,... | collective-permute-start | bytes 393224 | tf_op jit(solution)/shard_map/ppermute | solution.py:332
  54.1 2.1 %shard_map.110.refs_1_ = f32[1024,256]{1,0:T(8,128)S(1)} custom-call(s32[4,3]{1,0:T(4,128)S(1)} %copy-done.4, s32[4]{0:T(128)S(1)} %copy-done.5, bf16[4096,128]{1,0:T(8,128)(2,1)S(1)} %get-tuple-element.47.left, bf16[128,4096]{1,0:T(8,128)(2,1)S(1)} %get-tuple-element.48.right, bf16[4096,256]{1,0:T(8,128)(2,1)S(1)} %copy-done.2), custom_call_target="tpu_custom_call" | custom-call | flops 1610612736 | bytes 6291456 | tf_op jit(solution)/shard_map/pallas_call | solution.py:423
  56.2 2.9 %collective-permute-start.11 = (bf16[256,256]{1,0:T(8,128)(2,1)S(1)}, bf16[256,256]{1,0:T(8,128)(2,1)S(1)}, u32[]{:S(2)}, u32[]{:S(2)}) collective-permute-start(bf16[256,256]{1,0:T(8,128)(2,1)S(1)} %collective-permute-done.10.s1), channel_id=1, source_target_pairs={{0,32},{4,36},{8,40},{12,44},{16,48},{20,52},{24,56},{28,252},{32,... | collective-permute-start | bytes 393224 | tf_op jit(solution)/shard_map/ppermute | solution.py:332
  59.2 2.1 %shard_map.111.refs_2_ = f32[1024,256]{1,0:T(8,128)S(1)} custom-call(s32[4,3]{1,0:T(4,128)S(1)} %copy-done.4, s32[4]{0:T(128)S(1)} %copy-done.5, bf16[4096,128]{1,0:T(8,128)(2,1)S(1)} %get-tuple-element.47.left, bf16[128,4096]{1,0:T(8,128)(2,1)S(1)} %get-tuple-element.48.right, bf16[4096,256]{1,0:T(8,128)(2,1)S(1)} %copy-done.2), custom_call_target="tpu_custom_call" | custom-call | flops 1610612736 | bytes 6291456 | tf_op jit(solution)/shard_map/pallas_call | solution.py:423
  61.3 3.6 %collective-permute-start.23 = (bf16[64,4096]{1,0:T(8,128)(2,1)S(1)}, bf16[64,4096]{1,0:T(8,128)(2,1)S(1)}, u32[]{:S(2)}, u32[]{:S(2)}) collective-permute-start(bf16[64,4096]{1,0:T(8,128)(2,1)S(1)} %get-tuple-element.46.coords), channel_id=1, source_target_pairs={{0,4},{4,0},{8,12},{12,8},{16,20},{20,16},{24,28},{28,24},{32,36},... | collective-permute-start | bytes 1572872 | tf_op jit(solution)/shard_map/ppermute | solution.py:332
  64.8 1.3 %shard_map.105.field = f32[1024,256]{1,0:T(8,128)S(1)} custom-call(bf16[64,1024]{1,0:T(8,128)(2,1)S(1)} %get-tuple-element.44.coords, bf16[1024,256]{1,0:T(8,128)(2,1)S(1)} %get-tuple-element.45.leaf_skel), custom_call_target="tpu_custom_call" | custom-call | flops 1073741824 | bytes 2097152 | tf_op jit(solution)/shard_map/pallas_call | solution.py:410
  66.1 3.5 %collective-permute-start.12 = (bf16[256,256]{1,0:T(8,128)(2,1)S(1)}, bf16[256,256]{1,0:T(8,128)(2,1)S(1)}, u32[]{:S(2)}, u32[]{:S(2)}) collective-permute-start(bf16[256,256]{1,0:T(8,128)(2,1)S(1)} %collective-permute-done.11.s3), channel_id=1, source_target_pairs={{0,32},{4,36},{8,40},{12,44},{16,48},{20,52},{24,56},{28,252},{32,... | collective-permute-start | bytes 393224 | tf_op jit(solution)/shard_map/ppermute | solution.py:332
  69.6 2.1 %shard_map.107.refs_1_ = f32[1024,256]{1,0:T(8,128)S(1)} custom-call(s32[4,3]{1,0:T(4,128)S(1)} %copy-done.4, s32[4]{0:T(128)S(1)} %copy-done.5, bf16[4096,128]{1,0:T(8,128)(2,1)S(1)} %get-tuple-element.47.left, bf16[128,4096]{1,0:T(8,128)(2,1)S(1)} %get-tuple-element.48.right, bf16[4096,256]{1,0:T(8,128)(2,1)S(1)} %copy-done.2), custom_call_target="tpu_custom_call" | custom-call | flops 1610612736 | bytes 6291456 | tf_op jit(solution)/shard_map/pallas_call | solution.py:423
  71.7 0.8 collective-permute-done.12.s5
  72.5 3.5 %shard_map.108.refs_2_ = f32[1024,256]{1,0:T(8,128)S(1)} custom-call(s32[4,3]{1,0:T(4,128)S(1)} %copy-done.4, s32[4]{0:T(128)S(1)} %copy-done.5, bf16[4096,128]{1,0:T(8,128)(2,1)S(1)} %get-tuple-element.47.left, bf16[128,4096]{1,0:T(8,128)(2,1)S(1)} %get-tuple-element.48.right, bf16[4096,256]{1,0:T(8,128)(2,1)S(1)} %copy-done.2), custom_call_target="tpu_custom_call" | custom-call | flops 1610612736 | bytes 6291456 | tf_op jit(solution)/shard_map/pallas_call | solution.py:423
  75.9 2.9 %collective-permute-done.16.s6 = bf16[256,256]{1,0:T(8,128)(2,1)S(1)} collective-permute-done((bf16[256,256]{1,0:T(8,128)(2,1)S(1)}, bf16[256,256]{1,0:T(8,128)(2,1)S(1)}, u32[]{:S(2)}, u32[]{:S(2)}) %collective-permute-start.16) | collective-permute-done | bytes 131104 | tf_op jit(solution)/shard_map/ppermute | solution.py:332
  78.9 1.2 %collective-permute-start.13 = (bf16[256,256]{1,0:T(8,128)(2,1)S(1)}, bf16[256,256]{1,0:T(8,128)(2,1)S(1)}, u32[]{:S(2)}, u32[]{:S(2)}) collective-permute-start(bf16[256,256]{1,0:T(8,128)(2,1)S(1)} %collective-permute-done.12.s5), channel_id=1, source_target_pairs={{0,32},{4,36},{8,40},{12,44},{16,48},{20,52},{24,56},{28,252},{32,... | collective-permute-start | bytes 393224 | tf_op jit(solution)/shard_map/ppermute | solution.py:332
  80.1 2.2 %shard_map.103 = (f32[64,256]{1,0:T(8,128)S(1)}, f32[256,256]{1,0:T(8,128)S(1)}) custom-call(bf16[128,256]{1,0:T(8,128)(2,1)S(1)} %get-tuple-element.36.own, bf16[128,256]{1,0:T(8,128)(2,1)S(1)} %collective-permute-done.9.other, bf16[256,256]{1,0:T(8,128)(2,1)S(1)} %collective-permute-done.10.s1, bf16[256,256]{1,0:T(8,128)(2,1)S(1)} %collective-permute-done.14.s2, ...), custom_call_target="tpu_custom_call" | custom-call | flops 2147483648 | bytes 2097152 | tf_op jit(solution)/shard_map/pallas_call | solution.py:433
  82.3 0.4 collective-permute-done.13.s7
  82.7 3.7 %collective-permute-start.20 = (bf16[64,4096]{1,0:T(8,128)(2,1)S(1)}, bf16[64,4096]{1,0:T(8,128)(2,1)S(1)}, u32[]{:S(2)}, u32[]{:S(2)}) collective-permute-start(bf16[64,4096]{1,0:T(8,128)(2,1)S(1)} %get-tuple-element.46.coords), channel_id=1, source_target_pairs={{4,8},{12,16},{20,24},{28,32},{36,40},{44,48},{52,56},{60,64},{68,... | collective-permute-start | bytes 1572872 | tf_op jit(solution)/shard_map/ppermute | solution.py:332
  86.4 0.6 shard_map.104
  87.0 0.9 collective-permute-start.17
  87.9 1.7 %collective-permute-start.18 = (bf16[64,256]{1,0:T(8,128)(2,1)S(1)}, bf16[64,256]{1,0:T(8,128)(2,1)S(1)}, u32[]{:S(2)}, u32[]{:S(2)}) collective-permute-start(bf16[64,256]{1,0:T(8,128)(2,1)S(1)} %get-tuple-element.42), channel_id=1, source_target_pairs={{0,8},{4,12},{8,0},{12,4},{16,24},{20,28},{24,16},{28,20},{32,40},... | collective-permute-start | bytes 98312 | tf_op jit(solution)/shard_map/ppermute | solution.py:332
  89.6 2.3 %shard_map.112.refs_3_ = f32[2048,256]{1,0:T(8,128)S(1)} custom-call(s32[4,3]{1,0:T(4,128)S(1)} %copy-done.4, s32[4]{0:T(128)S(1)} %copy-done.5, bf16[4096,128]{1,0:T(8,128)(2,1)S(1)} %get-tuple-element.47.left, bf16[64,4096]{1,0:T(8,128)(2,1)S(1)} %collective-permute-done.23.coords, bf16[4096,256]{1,0:T(8,128)(2,1)S(1)} %collective-permute-done.24.refs_0_, ...), custom_call_target="tpu_custom_call" | custom-call | flops 3221225472 | bytes 12582912 | tf_op jit(solution)/shard_map/pallas_call | solution.py:453
  91.9 2.3 %shard_map.109.refs_2_ = f32[2048,256]{1,0:T(8,128)S(1)} custom-call(s32[4,3]{1,0:T(4,128)S(1)} %copy-done.4, s32[4]{0:T(128)S(1)} %copy-done.5, bf16[4096,128]{1,0:T(8,128)(2,1)S(1)} %get-tuple-element.47.left, bf16[64,4096]{1,0:T(8,128)(2,1)S(1)} %collective-permute-done.23.coords, bf16[4096,256]{1,0:T(8,128)(2,1)S(1)} %collective-permute-done.24.refs_0_, ...), custom_call_target="tpu_custom_call" | custom-call | flops 3221225472 | bytes 12582912 | tf_op jit(solution)/shard_map/pallas_call | solution.py:453
  94.3 0.0 copy-start
  94.3 0.0 copy-start.1
  94.3 1.1 %collective-permute-start.19 = (bf16[64,256]{1,0:T(8,128)(2,1)S(1)}, bf16[64,256]{1,0:T(8,128)(2,1)S(1)}, u32[]{:S(2)}, u32[]{:S(2)}) collective-permute-start(bf16[64,256]{1,0:T(8,128)(2,1)S(1)} %get-tuple-element.43), channel_id=1, source_target_pairs={{0,12},{4,8},{8,4},{12,0},{16,28},{20,24},{24,20},{28,16},{32,44},... | collective-permute-start | bytes 98312 | tf_op jit(solution)/shard_map/ppermute | solution.py:332
  95.4 6.9 %shard_map.113.near = f32[4096,256]{1,0:T(8,128)S(1)} custom-call(s32[4,3]{1,0:T(4,128)S(1)} %copy-done.4, s32[4]{0:T(128)S(1)} %copy-done.5, bf16[4096,128]{1,0:T(8,128)(2,1)S(1)} %get-tuple-element.47.left, bf16[64,4096]{1,0:T(8,128)(2,1)S(1)} %collective-permute-done.20.coords, bf16[4096,256]{1,0:T(8,128)(2,1)S(1)} %collective-permute-done.21.refs_0_, ...), custom_call_target="tpu_custom_call" | custom-call | flops 3221225472 | bytes 12582912 | tf_op jit(solution)/shard_map/pallas_call | solution.py:453
  102.3 3.8 %shard_map.114 = f32[4096,256]{1,0:T(8,128)} custom-call(bf16[64,256]{1,0:T(8,128)(2,1)S(1)} %get-tuple-element.40.t0, bf16[64,256]{1,0:T(8,128)(2,1)S(1)} %collective-permute-done.17.t1, bf16[64,256]{1,0:T(8,128)(2,1)S(1)} %collective-permute-done.18.t2, bf16[64,256]{1,0:T(8,128)(2,1)S(1)} %collective-permute-done.19.t3, bf16[256,1024]{1,0:T(8,128)(2,1)S(1)} %copy-done.1, ...), custom_call_target="tpu_custom_call" | custom-call | flops 671088640 | bytes 10485760 | tf_op jit(solution)/shard_map/pallas_call | solution.py:469
  (40 shorter events, 0.1 us)
Async XLA Ops:
  0.0 87.9 %collective-permute-start.24 = (bf16[4096,256]{1,0:T(8,128)(2,1)}, bf16[4096,256]{1,0:T(8,128)(2,1)S(1)}, u32[]{:S(2)}, u32[]{:S(2)}) collective-permute-start(bf16[4096,256]{1,0:T(8,128)(2,1)} %weights.9), channel_id=1, source_target_pairs={{0,4},{4,0},{8,12},{12,8},{16,20},{20,16},{24,28},{28,24},{32,36},... | collective-permute-start | bytes 6291464 | tf_op jit(solution)/shard_map/ppermute | solution.py:332
  0.7 12.4 %copy-start.2 = (bf16[4096,256]{1,0:T(8,128)(2,1)S(1)}, bf16[4096,256]{1,0:T(8,128)(2,1)}, u32[]{:S(2)}) copy-start(bf16[4096,256]{1,0:T(8,128)(2,1)} %weights.9) | copy-start | bytes 6291460
  0.7 13.2 %copy-start.3 = (bf16[64,1024]{1,0:T(8,128)(2,1)S(1)}, bf16[64,1024]{1,0:T(8,128)(2,1)}, u32[]{:S(2)}) copy-start(bf16[64,1024]{1,0:T(8,128)(2,1)} %g0.1) | copy-start | bytes 393220
  0.7 14.6 %copy-start.7 = (s32[16,256]{1,0:T(8,128)S(1)}, s32[16,256]{1,0:T(8,128)}, u32[]{:S(2)}) copy-start(s32[16,256]{1,0:T(8,128)} %param.17) | copy-start | bytes 49156
  0.7 14.6 %copy-start.8 = (s32[4,256]{1,0:T(4,128)S(1)}, s32[4,256]{1,0:T(4,128)}, u32[]{:S(2)}) copy-start(s32[4,256]{1,0:T(4,128)} %param.15) | copy-start | bytes 12292
  0.7 14.6 %copy-start.9 = (s32[1,256]{1,0:T(1,128)S(1)}, s32[1,256]{1,0:T(1,128)}, u32[]{:S(2)}) copy-start(s32[1,256]{1,0:T(1,128)} %param.16) | copy-start | bytes 3076
  0.7 14.6 %copy-start.6 = (bf16[4096,16]{0,1:T(8,128)(2,1)S(1)}, bf16[4096,16]{0,1:T(8,128)(2,1)}, u32[]{:S(2)}) copy-start(bf16[4096,16]{0,1:T(8,128)(2,1)} %param.10) | copy-start | bytes 393220
  0.7 12.3 %collective-permute-start = (bf16[16,4096]{1,0:T(8,128)(2,1)}, bf16[16,4096]{1,0:T(8,128)(2,1)S(1)}, u32[]{:S(2)}, u32[]{:S(2)}) collective-permute-start(bf16[16,4096]{1,0:T(8,128)(2,1)} %bitcast.1), channel_id=1, source_target_pairs={{0,1},{1,2},{2,3},{3,0},{4,5},{5,6},{6,7},{7,4},{8,9},{9,10},{10,1... | collective-permute-start | bytes 393224 | tf_op jit(solution)/shard_map/ppermute | solution.py:332
  2.0 11.9 %collective-permute-start.1 = (bf16[16,4096]{1,0:T(8,128)(2,1)}, bf16[16,4096]{1,0:T(8,128)(2,1)S(1)}, u32[]{:S(2)}, u32[]{:S(2)}) collective-permute-start(bf16[16,4096]{1,0:T(8,128)(2,1)} %bitcast.2), channel_id=1, source_target_pairs={{0,2},{1,3},{2,0},{3,1},{4,6},{5,7},{6,4},{7,5},{8,10},{9,11},{10,... | collective-permute-start | bytes 393224 | tf_op jit(solution)/shard_map/ppermute | solution.py:332
  4.4 10.8 %collective-permute-start.2 = (bf16[16,4096]{1,0:T(8,128)(2,1)}, bf16[16,4096]{1,0:T(8,128)(2,1)S(1)}, u32[]{:S(2)}, u32[]{:S(2)}) collective-permute-start(bf16[16,4096]{1,0:T(8,128)(2,1)} %bitcast.3), channel_id=1, source_target_pairs={{0,3},{1,0},{2,1},{3,2},{4,7},{5,4},{6,5},{7,6},{8,11},{9,8},{10,9... | collective-permute-start | bytes 393224 | tf_op jit(solution)/shard_map/ppermute | solution.py:332
  5.6 89.8 %collective-permute-start.21 = (bf16[4096,256]{1,0:T(8,128)(2,1)}, bf16[4096,256]{1,0:T(8,128)(2,1)S(1)}, u32[]{:S(2)}, u32[]{:S(2)}) collective-permute-start(bf16[4096,256]{1,0:T(8,128)(2,1)} %weights.9), channel_id=1, source_target_pairs={{4,8},{12,16},{20,24},{36,40},{44,48},{52,56},{68,72},{76,80},{84,... | collective-permute-start | bytes 6291464 | tf_op jit(solution)/shard_map/ppermute | solution.py:332
  13.0 82.3 %collective-permute-start.22 = (bf16[4096,256]{1,0:T(8,128)(2,1)S(1)}, bf16[4096,256]{1,0:T(8,128)(2,1)S(1)}, u32[]{:S(2)}, u32[]{:S(2)}) collective-permute-start(bf16[4096,256]{1,0:T(8,128)(2,1)S(1)} %copy-done.2), channel_id=1, source_target_pairs={{28,32},{60,64},{92,96},{124,128},{156,160},{188,192},{220,224},{3... | collective-permute-start | bytes 6291464 | tf_op jit(solution)/shard_map/ppermute | solution.py:332
  13.9 21.7 %collective-permute-start.7 = (bf16[64,1024]{1,0:T(8,128)(2,1)S(1)}, bf16[64,1024]{1,0:T(8,128)(2,1)S(1)}, u32[]{:S(2)}, u32[]{:S(2)}) collective-permute-start(bf16[64,1024]{1,0:T(8,128)(2,1)S(1)} %copy-done.3), channel_id=1, source_target_pairs={{0,8},{4,12},{8,0},{12,4},{16,24},{20,28},{24,16},{28,20},{32,40},... | collective-permute-start | bytes 393224 | tf_op jit(solution)/shard_map/ppermute | solution.py:332
  15.3 21.7 %collective-permute-start.6 = (bf16[64,1024]{1,0:T(8,128)(2,1)S(1)}, bf16[64,1024]{1,0:T(8,128)(2,1)S(1)}, u32[]{:S(2)}, u32[]{:S(2)}) collective-permute-start(bf16[64,1024]{1,0:T(8,128)(2,1)S(1)} %copy-done.3), channel_id=1, source_target_pairs={{0,4},{4,0},{8,12},{12,8},{16,20},{20,16},{24,28},{28,24},{32,36},... | collective-permute-start | bytes 393224 | tf_op jit(solution)/shard_map/ppermute | solution.py:332
  15.3 38.8 %copy-start.4 = (s32[4,3]{1,0:T(4,128)S(1)}, s32[4,3]{1,0:T(4,128)}, u32[]{:S(2)}) copy-start(s32[4,3]{1,0:T(4,128)} %near_list.13) | copy-start | bytes 148
  15.3 38.8 %copy-start.5 = (s32[4]{0:T(128)S(1)}, s32[4]{0:T(128)}, u32[]{:S(2)}) copy-start(s32[4]{0:T(128)} %near_count.13) | copy-start | bytes 52
  35.5 2.4 %collective-permute-start.3 = (bf16[192,256]{1,0:T(8,128)(2,1)S(1)}, bf16[192,256]{1,0:T(8,128)(2,1)S(1)}, u32[]{:S(2)}, u32[]{:S(2)}) collective-permute-start(bf16[192,256]{1,0:T(8,128)(2,1)S(1)} %get-tuple-element.33), channel_id=1, source_target_pairs={{0,4},{4,0},{8,12},{12,8},{16,20},{20,16},{24,28},{28,24},{32,36},... | collective-permute-start | bytes 294920 | tf_op jit(solution)/shard_map/ppermute | solution.py:332
  37.0 4.3 %collective-permute-start.4 = (bf16[192,256]{1,0:T(8,128)(2,1)S(1)}, bf16[192,256]{1,0:T(8,128)(2,1)S(1)}, u32[]{:S(2)}, u32[]{:S(2)}) collective-permute-start(bf16[192,256]{1,0:T(8,128)(2,1)S(1)} %get-tuple-element.34), channel_id=1, source_target_pairs={{0,8},{4,12},{8,0},{12,4},{16,24},{20,28},{24,16},{28,20},{32,40},... | collective-permute-start | bytes 294920 | tf_op jit(solution)/shard_map/ppermute | solution.py:332
  37.9 8.6 %collective-permute-start.8 = (bf16[64,1024]{1,0:T(8,128)(2,1)S(1)}, bf16[64,1024]{1,0:T(8,128)(2,1)S(1)}, u32[]{:S(2)}, u32[]{:S(2)}) collective-permute-start(bf16[64,1024]{1,0:T(8,128)(2,1)S(1)} %collective-permute-done.7.g2), channel_id=1, source_target_pairs={{0,4},{4,0},{8,12},{12,8},{16,20},{20,16},{24,28},{28,24},{32,36},... | collective-permute-start | bytes 393224 | tf_op jit(solution)/shard_map/ppermute | solution.py:332
  41.3 5.2 %collective-permute-start.5 = (bf16[192,256]{1,0:T(8,128)(2,1)S(1)}, bf16[192,256]{1,0:T(8,128)(2,1)S(1)}, u32[]{:S(2)}, u32[]{:S(2)}) collective-permute-start(bf16[192,256]{1,0:T(8,128)(2,1)S(1)} %get-tuple-element.35), channel_id=1, source_target_pairs={{0,12},{4,8},{8,4},{12,0},{16,28},{20,24},{24,20},{28,16},{32,44},... | collective-permute-start | bytes 294920 | tf_op jit(solution)/shard_map/ppermute | solution.py:332
  46.9 4.4 %collective-permute-start.9 = (bf16[128,256]{1,0:T(8,128)(2,1)S(1)}, bf16[128,256]{1,0:T(8,128)(2,1)S(1)}, u32[]{:S(2)}, u32[]{:S(2)}) collective-permute-start(bf16[128,256]{1,0:T(8,128)(2,1)S(1)} %get-tuple-element.36.own), channel_id=1, source_target_pairs={{0,24},{4,28},{8,16},{12,20},{16,8},{20,12},{24,0},{28,4},{32,56},... | collective-permute-start | bytes 196616 | tf_op jit(solution)/shard_map/ppermute | solution.py:332
  51.3 4.9 %collective-permute-start.10 = (bf16[256,256]{1,0:T(8,128)(2,1)S(1)}, bf16[256,256]{1,0:T(8,128)(2,1)S(1)}, u32[]{:S(2)}, u32[]{:S(2)}) collective-permute-start(bf16[256,256]{1,0:T(8,128)(2,1)S(1)} %constant_dynamic-update-slice_fusion), channel_id=1, source_target_pairs={{0,32},{4,36},{8,40},{12,44},{16,48},{20,52},{24,56},{28,252},{32,... | collective-permute-start | bytes 393224 | tf_op jit(solution)/shard_map/ppermute | solution.py:332
  54.1 5.0 %collective-permute-start.14 = (bf16[256,256]{1,0:T(8,128)(2,1)S(1)}, bf16[256,256]{1,0:T(8,128)(2,1)S(1)}, u32[]{:S(2)}, u32[]{:S(2)}) collective-permute-start(bf16[256,256]{1,0:T(8,128)(2,1)S(1)} %constant_dynamic-update-slice_fusion), channel_id=1, source_target_pairs={{0,224},{4,228},{8,232},{12,236},{16,240},{20,244},{24,248},{28,60... | collective-permute-start | bytes 393224 | tf_op jit(solution)/shard_map/ppermute | solution.py:332
  56.2 5.0 %collective-permute-start.11 = (bf16[256,256]{1,0:T(8,128)(2,1)S(1)}, bf16[256,256]{1,0:T(8,128)(2,1)S(1)}, u32[]{:S(2)}, u32[]{:S(2)}) collective-permute-start(bf16[256,256]{1,0:T(8,128)(2,1)S(1)} %collective-permute-done.10.s1), channel_id=1, source_target_pairs={{0,32},{4,36},{8,40},{12,44},{16,48},{20,52},{24,56},{28,252},{32,... | collective-permute-start | bytes 393224 | tf_op jit(solution)/shard_map/ppermute | solution.py:332
  59.2 7.0 %collective-permute-start.15 = (bf16[256,256]{1,0:T(8,128)(2,1)S(1)}, bf16[256,256]{1,0:T(8,128)(2,1)S(1)}, u32[]{:S(2)}, u32[]{:S(2)}) collective-permute-start(bf16[256,256]{1,0:T(8,128)(2,1)S(1)} %collective-permute-done.14.s2), channel_id=1, source_target_pairs={{0,224},{4,228},{8,232},{12,236},{16,240},{20,244},{24,248},{28,60... | collective-permute-start | bytes 393224 | tf_op jit(solution)/shard_map/ppermute | solution.py:332
  61.3 25.7 %collective-permute-start.23 = (bf16[64,4096]{1,0:T(8,128)(2,1)S(1)}, bf16[64,4096]{1,0:T(8,128)(2,1)S(1)}, u32[]{:S(2)}, u32[]{:S(2)}) collective-permute-start(bf16[64,4096]{1,0:T(8,128)(2,1)S(1)} %get-tuple-element.46.coords), channel_id=1, source_target_pairs={{0,4},{4,0},{8,12},{12,8},{16,20},{20,16},{24,28},{28,24},{32,36},... | collective-permute-start | bytes 1572872 | tf_op jit(solution)/shard_map/ppermute | solution.py:332
  66.1 6.3 %collective-permute-start.12 = (bf16[256,256]{1,0:T(8,128)(2,1)S(1)}, bf16[256,256]{1,0:T(8,128)(2,1)S(1)}, u32[]{:S(2)}, u32[]{:S(2)}) collective-permute-start(bf16[256,256]{1,0:T(8,128)(2,1)S(1)} %collective-permute-done.11.s3), channel_id=1, source_target_pairs={{0,32},{4,36},{8,40},{12,44},{16,48},{20,52},{24,56},{28,252},{32,... | collective-permute-start | bytes 393224 | tf_op jit(solution)/shard_map/ppermute | solution.py:332
  72.5 6.4 %collective-permute-start.16 = (bf16[256,256]{1,0:T(8,128)(2,1)S(1)}, bf16[256,256]{1,0:T(8,128)(2,1)S(1)}, u32[]{:S(2)}, u32[]{:S(2)}) collective-permute-start(bf16[256,256]{1,0:T(8,128)(2,1)S(1)} %collective-permute-done.15.s4), channel_id=1, source_target_pairs={{0,224},{4,228},{8,232},{12,236},{16,240},{20,244},{24,248},{28,60... | collective-permute-start | bytes 393224 | tf_op jit(solution)/shard_map/ppermute | solution.py:332
  78.9 3.8 %collective-permute-start.13 = (bf16[256,256]{1,0:T(8,128)(2,1)S(1)}, bf16[256,256]{1,0:T(8,128)(2,1)S(1)}, u32[]{:S(2)}, u32[]{:S(2)}) collective-permute-start(bf16[256,256]{1,0:T(8,128)(2,1)S(1)} %collective-permute-done.12.s5), channel_id=1, source_target_pairs={{0,32},{4,36},{8,40},{12,44},{16,48},{20,52},{24,56},{28,252},{32,... | collective-permute-start | bytes 393224 | tf_op jit(solution)/shard_map/ppermute | solution.py:332
  82.7 11.6 %collective-permute-start.20 = (bf16[64,4096]{1,0:T(8,128)(2,1)S(1)}, bf16[64,4096]{1,0:T(8,128)(2,1)S(1)}, u32[]{:S(2)}, u32[]{:S(2)}) collective-permute-start(bf16[64,4096]{1,0:T(8,128)(2,1)S(1)} %get-tuple-element.46.coords), channel_id=1, source_target_pairs={{4,8},{12,16},{20,24},{28,32},{36,40},{44,48},{52,56},{60,64},{68,... | collective-permute-start | bytes 1572872 | tf_op jit(solution)/shard_map/ppermute | solution.py:332
  87.0 15.2 %collective-permute-start.17 = (bf16[64,256]{1,0:T(8,128)(2,1)S(1)}, bf16[64,256]{1,0:T(8,128)(2,1)S(1)}, u32[]{:S(2)}, u32[]{:S(2)}) collective-permute-start(bf16[64,256]{1,0:T(8,128)(2,1)S(1)} %get-tuple-element.41), channel_id=1, source_target_pairs={{0,4},{4,0},{8,12},{12,8},{16,20},{20,16},{24,28},{28,24},{32,36},... | collective-permute-start | bytes 98312 | tf_op jit(solution)/shard_map/ppermute | solution.py:332
  87.9 14.4 %collective-permute-start.18 = (bf16[64,256]{1,0:T(8,128)(2,1)S(1)}, bf16[64,256]{1,0:T(8,128)(2,1)S(1)}, u32[]{:S(2)}, u32[]{:S(2)}) collective-permute-start(bf16[64,256]{1,0:T(8,128)(2,1)S(1)} %get-tuple-element.42), channel_id=1, source_target_pairs={{0,8},{4,12},{8,0},{12,4},{16,24},{20,28},{24,16},{28,20},{32,40},... | collective-permute-start | bytes 98312 | tf_op jit(solution)/shard_map/ppermute | solution.py:332
  94.3 8.0 %copy-start = (bf16[1024,1024]{1,0:T(8,128)(2,1)S(1)}, bf16[1024,1024]{1,0:T(8,128)(2,1)}, u32[]{:S(2)}) copy-start(bf16[1024,1024]{1,0:T(8,128)(2,1)} %basis.3) | copy-start | bytes 6291460
  94.3 8.0 %copy-start.1 = (bf16[256,1024]{1,0:T(8,128)(2,1)S(1)}, bf16[256,1024]{1,0:T(8,128)(2,1)}, u32[]{:S(2)}) copy-start(bf16[256,1024]{1,0:T(8,128)(2,1)} %transfer.3) | copy-start | bytes 1572868
  94.3 8.0 %collective-permute-start.19 = (bf16[64,256]{1,0:T(8,128)(2,1)S(1)}, bf16[64,256]{1,0:T(8,128)(2,1)S(1)}, u32[]{:S(2)}, u32[]{:S(2)}) collective-permute-start(bf16[64,256]{1,0:T(8,128)(2,1)S(1)} %get-tuple-element.43), channel_id=1, source_target_pairs={{0,12},{4,8},{8,4},{12,0},{16,28},{20,24},{24,20},{28,16},{32,44},... | collective-permute-start | bytes 98312 | tf_op jit(solution)/shard_map/ppermute | solution.py:332

commit v4 on v3

--- a/solution.py
+++ b/solution.py
@@ -27,10 +27,6 @@
 
 def mm_nt(a, b):
     return lax.dot_general(a, b, (((1,), (1,)), ((), ())), preferred_element_type=F32)
-
-
-def mm_tn(a, b):
-    return lax.dot_general(a, b, (((0,), (0,)), ((), ())), preferred_element_type=F32)
 
 
 def call(body, outs, in_specs, scratch=(), flops=0, exps=0, nbytes=0, vmem=8):
@@ -292,7 +288,13 @@
         outs[i][...] = (fields[i * 64 : (i + 1) * 64, :] + mm(top, transfer[:, cols])).astype(BF)
 
 
-def finish_body(t0, t1, t2, t3, transfer, basis, field, near, out, total):
+def flip_body(transfer, basis, transfer_t, basis_t):
+    transfer_t[...] = transfer[...].T
+    for leaf in range(4):
+        basis_t[leaf * LEAF : (leaf + 1) * LEAF, :] = basis[leaf * RANK : (leaf + 1) * RANK, :].T
+
+
+def finish_body(t0, t1, t2, t3, transfer_t, basis_t, field, near, out, total):
     leaf = pl.program_id(0)
     share = column_share(lax.axis_index(ROWS))
 
@@ -306,8 +308,8 @@
 
     ranks = pl.ds(pl.multiple_of(leaf * RANK, RANK), RANK)
     rows = pl.ds(pl.multiple_of(leaf * LEAF, LEAF), LEAF)
-    leaf_total = (field[ranks, :] + mm_tn(transfer[:, ranks], total[...])).astype(BF)
-    out[...] = near[rows, :] + mm_tn(basis[ranks, :], leaf_total)
+    leaf_total = (field[ranks, :] + mm(transfer_t[ranks, :], total[...])).astype(BF)
+    out[...] = near[rows, :] + mm(basis_t[rows, :], leaf_total)
 
 
 def per_device(
@@ -449,6 +451,14 @@
     )(group_skel, rings[6], top_start, fields, full_transfer)
     returned = [totals[0]] + [flipped(totals[flip], flip) for flip in (1, 2, 3)]
 
+    transfer_t, basis_t = call(
+        flip_body,
+        [((4 * RANK, RANK), BF), ((rows, RANK), BF)],
+        [VMEM] * 2,
+        flops=rows * RANK,
+        nbytes=5 * 1024 * 1024,
+    )(dev_transfer, leaf_basis)
+
     def near_neighbour(inside, opening, *args):
         return call(
             functools.partial(near_neighbour_body, dim, inside, opening),
@@ -477,7 +487,7 @@
         cost_estimate=pl.CostEstimate(
             flops=2 * 5 * RANK * LEAF * width, transcendentals=0, bytes_accessed=10 * 1024 * 1024
         ),
-    )(*returned, dev_transfer, leaf_basis, leaf_field, near_sum)
+    )(*returned, transfer_t, basis_t, leaf_field, near_sum)
 
 
 def solution(mesh):

time: 108 us -> 108 us (level)
  no operation moved by 1% of the time
where the time goes in v4:
time: 108 us; the launch traced here: 106 us
  starting transfers between devices  38.6 us (36%)
  Pallas kernels  34.8 us (32%)
  waiting for transfers between devices  32.1 us (30%)
    ppermute x25, starting transfers between devices, moved(): return lax.ppermute(value, axis, pairs)  38.6 us
    ppermute x25, waiting for transfers between devices, moved(): return lax.ppermute(value, axis, pairs)  32.1 us
    pallas_call x3, Pallas kernels, near_neighbour(): call(functools.partial(near_neighbour_body, dim, inside, opening), [((2 *...  11.5 us
    pallas_call x4, Pallas kernels, per_device(): call(functools.partial(near_own_body, dim, first), [((LEAF, width), F32)]...  9.75 us
    pallas_call x1, Pallas kernels, per_device(): pl.pallas_call(finish_body, grid=(4,), out_shape=jax.ShapeDtypeStruct((ro...  3.7 us
    pallas_call x1, Pallas kernels, per_device(): call(skel_body, [((4 * RANK, width), BF), ((width, RANK), BF)], [HBM] * 3...  3.53 us
    pallas_call x1, Pallas kernels, per_device(): call(functools.partial(top_start_body, dim), [((64, RANK), F32), ((4 * 64...  2.2 us
  transfers between devices with their start and end apart: 25, of which 8 were waited for; matrix products, arithmetic and copies ran while one was open for 0% of the time, Pallas kernels for 29%

profile of v4, /device:TPU:97, one launch (start us, length us, event | category | flops | bytes accessed | tf_op | source)
XLA Modules:
  0.0 106.0 jit_solution(4889828666597119801)
XLA Ops:
  0.0 0.7 collective-permute-start.24
  0.7 1.3 %collective-permute-start = (bf16[16,4096]{1,0:T(8,128)(2,1)}, bf16[16,4096]{1,0:T(8,128)(2,1)S(1)}, u32[]{:S(2)}, u32[]{:S(2)}) collective-permute-start(bf16[16,4096]{1,0:T(8,128)(2,1)} %bitcast.1), channel_id=1, source_target_pairs={{0,1},{1,2},{2,3},{3,0},{4,5},{5,6},{6,7},{7,4},{8,9},{9,10},{10,1... | collective-permute-start | bytes 393224 | tf_op jit(solution)/shard_map/ppermute | solution.py:334
  2.0 2.5 %collective-permute-start.1 = (bf16[16,4096]{1,0:T(8,128)(2,1)}, bf16[16,4096]{1,0:T(8,128)(2,1)S(1)}, u32[]{:S(2)}, u32[]{:S(2)}) collective-permute-start(bf16[16,4096]{1,0:T(8,128)(2,1)} %bitcast.2), channel_id=1, source_target_pairs={{0,2},{1,3},{2,0},{3,1},{4,6},{5,7},{6,4},{7,5},{8,10},{9,11},{10,... | collective-permute-start | bytes 393224 | tf_op jit(solution)/shard_map/ppermute | solution.py:334
  4.4 1.2 %collective-permute-start.2 = (bf16[16,4096]{1,0:T(8,128)(2,1)}, bf16[16,4096]{1,0:T(8,128)(2,1)S(1)}, u32[]{:S(2)}, u32[]{:S(2)}) collective-permute-start(bf16[16,4096]{1,0:T(8,128)(2,1)} %bitcast.3), channel_id=1, source_target_pairs={{0,3},{1,0},{2,1},{3,2},{4,7},{5,4},{6,5},{7,6},{8,11},{9,8},{10,9... | collective-permute-start | bytes 393224 | tf_op jit(solution)/shard_map/ppermute | solution.py:334
  5.6 3.9 %collective-permute-start.21 = (bf16[4096,256]{1,0:T(8,128)(2,1)}, bf16[4096,256]{1,0:T(8,128)(2,1)S(1)}, u32[]{:S(2)}, u32[]{:S(2)}) collective-permute-start(bf16[4096,256]{1,0:T(8,128)(2,1)} %weights.9), channel_id=1, source_target_pairs={{4,8},{12,16},{20,24},{36,40},{44,48},{52,56},{68,72},{76,80},{84,... | collective-permute-start | bytes 6291464 | tf_op jit(solution)/shard_map/ppermute | solution.py:334
  9.6 3.5 %shard_map.100 = (bf16[1024,256]{1,0:T(8,128)(2,1)S(1)}, bf16[256,256]{1,0:T(8,128)(2,1)S(1)}) custom-call(bf16[4096,256]{1,0:T(8,128)(2,1)} %weights.9, bf16[1024,1024]{1,0:T(8,128)(2,1)} %basis.3, bf16[256,1024]{1,0:T(8,128)(2,1)} %transfer.3), custom_call_target="tpu_custom_call" | custom-call | flops 671088640 | bytes 5242880 | tf_op jit(solution)/shard_map/pallas_call | solution.py:360
  13.1 0.0 copy-start
  13.1 0.0 collective-permute-done.p1
  13.1 0.9 collective-permute-start.22
  14.1 1.4 %collective-permute-start.7 = (bf16[64,1024]{1,0:T(8,128)(2,1)S(1)}, bf16[64,1024]{1,0:T(8,128)(2,1)S(1)}, u32[]{:S(2)}, u32[]{:S(2)}) collective-permute-start(bf16[64,1024]{1,0:T(8,128)(2,1)S(1)} %copy-done.3), channel_id=1, source_target_pairs={{0,8},{4,12},{8,0},{12,4},{16,24},{20,28},{24,16},{28,20},{32,40},... | collective-permute-start | bytes 393224 | tf_op jit(solution)/shard_map/ppermute | solution.py:334
  15.5 0.8 shard_map.101
  16.3 19.2 %collective-permute-done.7.g2 = bf16[64,1024]{1,0:T(8,128)(2,1)S(1)} collective-permute-done((bf16[64,1024]{1,0:T(8,128)(2,1)S(1)}, bf16[64,1024]{1,0:T(8,128)(2,1)S(1)}, u32[]{:S(2)}, u32[]{:S(2)}) %collective-permute-start.7) | collective-permute-done | bytes 131104 | tf_op jit(solution)/shard_map/ppermute | solution.py:334
  35.5 1.4 %collective-permute-start.3 = (bf16[192,256]{1,0:T(8,128)(2,1)S(1)}, bf16[192,256]{1,0:T(8,128)(2,1)S(1)}, u32[]{:S(2)}, u32[]{:S(2)}) collective-permute-start(bf16[192,256]{1,0:T(8,128)(2,1)S(1)} %get-tuple-element.35), channel_id=1, source_target_pairs={{0,4},{4,0},{8,12},{12,8},{16,20},{20,16},{24,28},{28,24},{32,36},... | collective-permute-start | bytes 294920 | tf_op jit(solution)/shard_map/ppermute | solution.py:334
  37.0 0.5 collective-permute-start.4
  37.4 0.5 collective-permute-done.3.r1
  37.9 0.4 collective-permute-start.8
  38.3 3.1 %collective-permute-done.4.r2 = bf16[192,256]{1,0:T(8,128)(2,1)S(1)} collective-permute-done((bf16[192,256]{1,0:T(8,128)(2,1)S(1)}, bf16[192,256]{1,0:T(8,128)(2,1)S(1)}, u32[]{:S(2)}, u32[]{:S(2)}) %collective-permute-start.4) | collective-permute-done | bytes 98336 | tf_op jit(solution)/shard_map/ppermute | solution.py:334
  41.3 1.2 %collective-permute-start.5 = (bf16[192,256]{1,0:T(8,128)(2,1)S(1)}, bf16[192,256]{1,0:T(8,128)(2,1)S(1)}, u32[]{:S(2)}, u32[]{:S(2)}) collective-permute-start(bf16[192,256]{1,0:T(8,128)(2,1)S(1)} %get-tuple-element.37), channel_id=1, source_target_pairs={{0,12},{4,8},{8,4},{12,0},{16,28},{20,24},{24,20},{28,16},{32,44},... | collective-permute-start | bytes 294920 | tf_op jit(solution)/shard_map/ppermute | solution.py:334
  42.5 0.7 shard_map.105
  43.3 0.4 shard_map.107
  43.7 2.9 %collective-permute-done.5.r3 = bf16[192,256]{1,0:T(8,128)(2,1)S(1)} collective-permute-done((bf16[192,256]{1,0:T(8,128)(2,1)S(1)}, bf16[192,256]{1,0:T(8,128)(2,1)S(1)}, u32[]{:S(2)}, u32[]{:S(2)}) %collective-permute-start.5) | collective-permute-done | bytes 98336 | tf_op jit(solution)/shard_map/ppermute | solution.py:334
  46.5 0.3 shard_map.102
  46.9 2.0 %collective-permute-start.9 = (bf16[128,256]{1,0:T(8,128)(2,1)S(1)}, bf16[128,256]{1,0:T(8,128)(2,1)S(1)}, u32[]{:S(2)}, u32[]{:S(2)}) collective-permute-start(bf16[128,256]{1,0:T(8,128)(2,1)S(1)} %get-tuple-element.38.own), channel_id=1, source_target_pairs={{0,24},{4,28},{8,16},{12,20},{16,8},{20,12},{24,0},{28,4},{32,56},... | collective-permute-start | bytes 196616 | tf_op jit(solution)/shard_map/ppermute | solution.py:334
  48.9 2.4 %collective-permute-done.9.other = bf16[128,256]{1,0:T(8,128)(2,1)S(1)} collective-permute-done((bf16[128,256]{1,0:T(8,128)(2,1)S(1)}, bf16[128,256]{1,0:T(8,128)(2,1)S(1)}, u32[]{:S(2)}, u32[]{:S(2)}) %collective-permute-start.9) | collective-permute-done | bytes 65568 | tf_op jit(solution)/shard_map/ppermute | solution.py:334
  51.3 2.8 %collective-permute-start.10 = (bf16[256,256]{1,0:T(8,128)(2,1)S(1)}, bf16[256,256]{1,0:T(8,128)(2,1)S(1)}, u32[]{:S(2)}, u32[]{:S(2)}) collective-permute-start(bf16[256,256]{1,0:T(8,128)(2,1)S(1)} %constant_dynamic-update-slice_fusion), channel_id=1, source_target_pairs={{0,32},{4,36},{8,40},{12,44},{16,48},{20,52},{24,56},{28,252},{32,... | collective-permute-start | bytes 393224 | tf_op jit(solution)/shard_map/ppermute | solution.py:334
  54.1 0.0 collective-permute-start.14
  54.1 2.1 %shard_map.112.refs_2_ = f32[1024,256]{1,0:T(8,128)S(1)} custom-call(s32[4,3]{1,0:T(4,128)S(1)} %copy-done.4, s32[4]{0:T(128)S(1)} %copy-done.5, bf16[4096,128]{1,0:T(8,128)(2,1)S(1)} %get-tuple-element.51.left, bf16[128,4096]{1,0:T(8,128)(2,1)S(1)} %get-tuple-element.52.right, bf16[4096,256]{1,0:T(8,128)(2,1)S(1)} %copy-done.2), custom_call_target="tpu_custom_call" | custom-call | flops 1610612736 | bytes 6291456 | tf_op jit(solution)/shard_map/pallas_call | solution.py:425
  56.2 2.9 %collective-permute-start.11 = (bf16[256,256]{1,0:T(8,128)(2,1)S(1)}, bf16[256,256]{1,0:T(8,128)(2,1)S(1)}, u32[]{:S(2)}, u32[]{:S(2)}) collective-permute-start(bf16[256,256]{1,0:T(8,128)(2,1)S(1)} %collective-permute-done.10.s1), channel_id=1, source_target_pairs={{0,32},{4,36},{8,40},{12,44},{16,48},{20,52},{24,56},{28,252},{32,... | collective-permute-start | bytes 393224 | tf_op jit(solution)/shard_map/ppermute | solution.py:334
  59.2 2.1 %shard_map.111.refs_1_ = f32[1024,256]{1,0:T(8,128)S(1)} custom-call(s32[4,3]{1,0:T(4,128)S(1)} %copy-done.4, s32[4]{0:T(128)S(1)} %copy-done.5, bf16[4096,128]{1,0:T(8,128)(2,1)S(1)} %get-tuple-element.51.left, bf16[128,4096]{1,0:T(8,128)(2,1)S(1)} %get-tuple-element.52.right, bf16[4096,256]{1,0:T(8,128)(2,1)S(1)} %copy-done.2), custom_call_target="tpu_custom_call" | custom-call | flops 1610612736 | bytes 6291456 | tf_op jit(solution)/shard_map/pallas_call | solution.py:425
  61.3 4.6 %collective-permute-start.23 = (bf16[64,4096]{1,0:T(8,128)(2,1)S(1)}, bf16[64,4096]{1,0:T(8,128)(2,1)S(1)}, u32[]{:S(2)}, u32[]{:S(2)}) collective-permute-start(bf16[64,4096]{1,0:T(8,128)(2,1)S(1)} %get-tuple-element.50.coords), channel_id=1, source_target_pairs={{0,4},{4,0},{8,12},{12,8},{16,20},{20,16},{24,28},{28,24},{32,36},... | collective-permute-start | bytes 1572872 | tf_op jit(solution)/shard_map/ppermute | solution.py:334
  65.9 1.3 %shard_map.106.field = f32[1024,256]{1,0:T(8,128)S(1)} custom-call(bf16[64,1024]{1,0:T(8,128)(2,1)S(1)} %get-tuple-element.48.coords, bf16[1024,256]{1,0:T(8,128)(2,1)S(1)} %get-tuple-element.49.leaf_skel), custom_call_target="tpu_custom_call" | custom-call | flops 1073741824 | bytes 2097152 | tf_op jit(solution)/shard_map/pallas_call | solution.py:412
  67.2 2.4 %collective-permute-start.12 = (bf16[256,256]{1,0:T(8,128)(2,1)S(1)}, bf16[256,256]{1,0:T(8,128)(2,1)S(1)}, u32[]{:S(2)}, u32[]{:S(2)}) collective-permute-start(bf16[256,256]{1,0:T(8,128)(2,1)S(1)} %collective-permute-done.11.s3), channel_id=1, source_target_pairs={{0,32},{4,36},{8,40},{12,44},{16,48},{20,52},{24,56},{28,252},{32,... | collective-permute-start | bytes 393224 | tf_op jit(solution)/shard_map/ppermute | solution.py:334
  69.6 2.1 %shard_map.108.refs_1_ = f32[1024,256]{1,0:T(8,128)S(1)} custom-call(s32[4,3]{1,0:T(4,128)S(1)} %copy-done.4, s32[4]{0:T(128)S(1)} %copy-done.5, bf16[4096,128]{1,0:T(8,128)(2,1)S(1)} %get-tuple-element.51.left, bf16[128,4096]{1,0:T(8,128)(2,1)S(1)} %get-tuple-element.52.right, bf16[4096,256]{1,0:T(8,128)(2,1)S(1)} %copy-done.2), custom_call_target="tpu_custom_call" | custom-call | flops 1610612736 | bytes 6291456 | tf_op jit(solution)/shard_map/pallas_call | solution.py:425
  71.7 0.8 collective-permute-done.12.s5
  72.5 3.5 %shard_map.109.refs_2_ = f32[1024,256]{1,0:T(8,128)S(1)} custom-call(s32[4,3]{1,0:T(4,128)S(1)} %copy-done.4, s32[4]{0:T(128)S(1)} %copy-done.5, bf16[4096,128]{1,0:T(8,128)(2,1)S(1)} %get-tuple-element.51.left, bf16[128,4096]{1,0:T(8,128)(2,1)S(1)} %get-tuple-element.52.right, bf16[4096,256]{1,0:T(8,128)(2,1)S(1)} %copy-done.2), custom_call_target="tpu_custom_call" | custom-call | flops 1610612736 | bytes 6291456 | tf_op jit(solution)/shard_map/pallas_call | solution.py:425
  76.0 2.9 %collective-permute-done.16.s6 = bf16[256,256]{1,0:T(8,128)(2,1)S(1)} collective-permute-done((bf16[256,256]{1,0:T(8,128)(2,1)S(1)}, bf16[256,256]{1,0:T(8,128)(2,1)S(1)}, u32[]{:S(2)}, u32[]{:S(2)}) %collective-permute-start.16) | collective-permute-done | bytes 131104 | tf_op jit(solution)/shard_map/ppermute | solution.py:334
  78.9 1.2 %collective-permute-start.13 = (bf16[256,256]{1,0:T(8,128)(2,1)S(1)}, bf16[256,256]{1,0:T(8,128)(2,1)S(1)}, u32[]{:S(2)}, u32[]{:S(2)}) collective-permute-start(bf16[256,256]{1,0:T(8,128)(2,1)S(1)} %collective-permute-done.12.s5), channel_id=1, source_target_pairs={{0,32},{4,36},{8,40},{12,44},{16,48},{20,52},{24,56},{28,252},{32,... | collective-permute-start | bytes 393224 | tf_op jit(solution)/shard_map/ppermute | solution.py:334
  80.1 2.2 %shard_map.103 = (f32[64,256]{1,0:T(8,128)S(1)}, f32[256,256]{1,0:T(8,128)S(1)}) custom-call(bf16[128,256]{1,0:T(8,128)(2,1)S(1)} %get-tuple-element.38.own, bf16[128,256]{1,0:T(8,128)(2,1)S(1)} %collective-permute-done.9.other, bf16[256,256]{1,0:T(8,128)(2,1)S(1)} %collective-permute-done.10.s1, bf16[256,256]{1,0:T(8,128)(2,1)S(1)} %collective-permute-done.14.s2, ...), custom_call_target="tpu_custom_call" | custom-call | flops 2147483648 | bytes 2097152 | tf_op jit(solution)/shard_map/pallas_call | solution.py:435
  82.3 0.4 collective-permute-done.13.s7
  82.7 3.7 %collective-permute-start.20 = (bf16[64,4096]{1,0:T(8,128)(2,1)S(1)}, bf16[64,4096]{1,0:T(8,128)(2,1)S(1)}, u32[]{:S(2)}, u32[]{:S(2)}) collective-permute-start(bf16[64,4096]{1,0:T(8,128)(2,1)S(1)} %get-tuple-element.50.coords), channel_id=1, source_target_pairs={{4,8},{12,16},{20,24},{28,32},{36,40},{44,48},{52,56},{60,64},{68,... | collective-permute-start | bytes 1572872 | tf_op jit(solution)/shard_map/ppermute | solution.py:334
  86.4 0.6 shard_map.104
  87.0 0.9 collective-permute-start.17
  87.9 1.7 %collective-permute-start.18 = (bf16[64,256]{1,0:T(8,128)(2,1)S(1)}, bf16[64,256]{1,0:T(8,128)(2,1)S(1)}, u32[]{:S(2)}, u32[]{:S(2)}) collective-permute-start(bf16[64,256]{1,0:T(8,128)(2,1)S(1)} %get-tuple-element.44), channel_id=1, source_target_pairs={{0,8},{4,12},{8,0},{12,4},{16,24},{20,28},{24,16},{28,20},{32,40},... | collective-permute-start | bytes 98312 | tf_op jit(solution)/shard_map/ppermute | solution.py:334
  89.6 2.3 %shard_map.113.refs_3_ = f32[2048,256]{1,0:T(8,128)S(1)} custom-call(s32[4,3]{1,0:T(4,128)S(1)} %copy-done.4, s32[4]{0:T(128)S(1)} %copy-done.5, bf16[4096,128]{1,0:T(8,128)(2,1)S(1)} %get-tuple-element.51.left, bf16[64,4096]{1,0:T(8,128)(2,1)S(1)} %collective-permute-done.23.coords, bf16[4096,256]{1,0:T(8,128)(2,1)S(1)} %collective-permute-done.24.refs_0_, ...), custom_call_target="tpu_custom_call" | custom-call | flops 3221225472 | bytes 12582912 | tf_op jit(solution)/shard_map/pallas_call | solution.py:463
  91.9 2.3 %shard_map.110.refs_2_ = f32[2048,256]{1,0:T(8,128)S(1)} custom-call(s32[4,3]{1,0:T(4,128)S(1)} %copy-done.4, s32[4]{0:T(128)S(1)} %copy-done.5, bf16[4096,128]{1,0:T(8,128)(2,1)S(1)} %get-tuple-element.51.left, bf16[64,4096]{1,0:T(8,128)(2,1)S(1)} %collective-permute-done.23.coords, bf16[4096,256]{1,0:T(8,128)(2,1)S(1)} %collective-permute-done.24.refs_0_, ...), custom_call_target="tpu_custom_call" | custom-call | flops 3221225472 | bytes 12582912 | tf_op jit(solution)/shard_map/pallas_call | solution.py:463
  94.3 1.1 %collective-permute-start.19 = (bf16[64,256]{1,0:T(8,128)(2,1)S(1)}, bf16[64,256]{1,0:T(8,128)(2,1)S(1)}, u32[]{:S(2)}, u32[]{:S(2)}) collective-permute-start(bf16[64,256]{1,0:T(8,128)(2,1)S(1)} %get-tuple-element.45), channel_id=1, source_target_pairs={{0,12},{4,8},{8,4},{12,0},{16,28},{20,24},{24,20},{28,16},{32,44},... | collective-permute-start | bytes 98312 | tf_op jit(solution)/shard_map/ppermute | solution.py:334
  95.4 6.9 %shard_map.114.near = f32[4096,256]{1,0:T(8,128)S(1)} custom-call(s32[4,3]{1,0:T(4,128)S(1)} %copy-done.4, s32[4]{0:T(128)S(1)} %copy-done.5, bf16[4096,128]{1,0:T(8,128)(2,1)S(1)} %get-tuple-element.51.left, bf16[64,4096]{1,0:T(8,128)(2,1)S(1)} %collective-permute-done.20.coords, bf16[4096,256]{1,0:T(8,128)(2,1)S(1)} %collective-permute-done.21.refs_0_, ...), custom_call_target="tpu_custom_call" | custom-call | flops 3221225472 | bytes 12582912 | tf_op jit(solution)/shard_map/pallas_call | solution.py:463
  102.3 3.7 %shard_map.115 = f32[4096,256]{1,0:T(8,128)} custom-call(bf16[64,256]{1,0:T(8,128)(2,1)S(1)} %get-tuple-element.42.t0, bf16[64,256]{1,0:T(8,128)(2,1)S(1)} %collective-permute-done.17.t1, bf16[64,256]{1,0:T(8,128)(2,1)S(1)} %collective-permute-done.18.t2, bf16[64,256]{1,0:T(8,128)(2,1)S(1)} %collective-permute-done.19.t3, ...), custom_call_target="tpu_custom_call" | custom-call | flops 671088640 | bytes 10485760 | tf_op jit(solution)/shard_map/pallas_call | solution.py:479
  (41 shorter events, 0.1 us)
Async XLA Ops:
  0.0 87.9 %collective-permute-start.24 = (bf16[4096,256]{1,0:T(8,128)(2,1)}, bf16[4096,256]{1,0:T(8,128)(2,1)S(1)}, u32[]{:S(2)}, u32[]{:S(2)}) collective-permute-start(bf16[4096,256]{1,0:T(8,128)(2,1)} %weights.9), channel_id=1, source_target_pairs={{0,4},{4,0},{8,12},{12,8},{16,20},{20,16},{24,28},{28,24},{32,36},... | collective-permute-start | bytes 6291464 | tf_op jit(solution)/shard_map/ppermute | solution.py:334
  0.7 12.4 %copy-start.2 = (bf16[4096,256]{1,0:T(8,128)(2,1)S(1)}, bf16[4096,256]{1,0:T(8,128)(2,1)}, u32[]{:S(2)}) copy-start(bf16[4096,256]{1,0:T(8,128)(2,1)} %weights.9) | copy-start | bytes 6291460
  0.7 13.4 %copy-start.3 = (bf16[64,1024]{1,0:T(8,128)(2,1)S(1)}, bf16[64,1024]{1,0:T(8,128)(2,1)}, u32[]{:S(2)}) copy-start(bf16[64,1024]{1,0:T(8,128)(2,1)} %g0.1) | copy-start | bytes 393220
  0.7 14.8 %copy-start.7 = (s32[16,256]{1,0:T(8,128)S(1)}, s32[16,256]{1,0:T(8,128)}, u32[]{:S(2)}) copy-start(s32[16,256]{1,0:T(8,128)} %param.17) | copy-start | bytes 49156
  0.7 14.8 %copy-start.8 = (s32[4,256]{1,0:T(4,128)S(1)}, s32[4,256]{1,0:T(4,128)}, u32[]{:S(2)}) copy-start(s32[4,256]{1,0:T(4,128)} %param.15) | copy-start | bytes 12292
  0.7 14.8 %copy-start.9 = (s32[1,256]{1,0:T(1,128)S(1)}, s32[1,256]{1,0:T(1,128)}, u32[]{:S(2)}) copy-start(s32[1,256]{1,0:T(1,128)} %param.16) | copy-start | bytes 3076
  0.7 14.8 %copy-start.6 = (bf16[4096,16]{0,1:T(8,128)(2,1)S(1)}, bf16[4096,16]{0,1:T(8,128)(2,1)}, u32[]{:S(2)}) copy-start(bf16[4096,16]{0,1:T(8,128)(2,1)} %param.10) | copy-start | bytes 393220
  0.7 12.4 %collective-permute-start = (bf16[16,4096]{1,0:T(8,128)(2,1)}, bf16[16,4096]{1,0:T(8,128)(2,1)S(1)}, u32[]{:S(2)}, u32[]{:S(2)}) collective-permute-start(bf16[16,4096]{1,0:T(8,128)(2,1)} %bitcast.1), channel_id=1, source_target_pairs={{0,1},{1,2},{2,3},{3,0},{4,5},{5,6},{6,7},{7,4},{8,9},{9,10},{10,1... | collective-permute-start | bytes 393224 | tf_op jit(solution)/shard_map/ppermute | solution.py:334
  2.0 12.1 %collective-permute-start.1 = (bf16[16,4096]{1,0:T(8,128)(2,1)}, bf16[16,4096]{1,0:T(8,128)(2,1)S(1)}, u32[]{:S(2)}, u32[]{:S(2)}) collective-permute-start(bf16[16,4096]{1,0:T(8,128)(2,1)} %bitcast.2), channel_id=1, source_target_pairs={{0,2},{1,3},{2,0},{3,1},{4,6},{5,7},{6,4},{7,5},{8,10},{9,11},{10,... | collective-permute-start | bytes 393224 | tf_op jit(solution)/shard_map/ppermute | solution.py:334
  4.4 11.0 %collective-permute-start.2 = (bf16[16,4096]{1,0:T(8,128)(2,1)}, bf16[16,4096]{1,0:T(8,128)(2,1)S(1)}, u32[]{:S(2)}, u32[]{:S(2)}) collective-permute-start(bf16[16,4096]{1,0:T(8,128)(2,1)} %bitcast.3), channel_id=1, source_target_pairs={{0,3},{1,0},{2,1},{3,2},{4,7},{5,4},{6,5},{7,6},{8,11},{9,8},{10,9... | collective-permute-start | bytes 393224 | tf_op jit(solution)/shard_map/ppermute | solution.py:334
  5.6 89.8 %collective-permute-start.21 = (bf16[4096,256]{1,0:T(8,128)(2,1)}, bf16[4096,256]{1,0:T(8,128)(2,1)S(1)}, u32[]{:S(2)}, u32[]{:S(2)}) collective-permute-start(bf16[4096,256]{1,0:T(8,128)(2,1)} %weights.9), channel_id=1, source_target_pairs={{4,8},{12,16},{20,24},{36,40},{44,48},{52,56},{68,72},{76,80},{84,... | collective-permute-start | bytes 6291464 | tf_op jit(solution)/shard_map/ppermute | solution.py:334
  9.5 33.0 %copy-start.1 = (bf16[256,1024]{1,0:T(8,128)(2,1)S(1)}, bf16[256,1024]{1,0:T(8,128)(2,1)}, u32[]{:S(2)}) copy-start(bf16[256,1024]{1,0:T(8,128)(2,1)} %transfer.3) | copy-start | bytes 1572868
  13.1 29.4 %copy-start = (bf16[1024,1024]{1,0:T(8,128)(2,1)S(1)}, bf16[1024,1024]{1,0:T(8,128)(2,1)}, u32[]{:S(2)}) copy-start(bf16[1024,1024]{1,0:T(8,128)(2,1)} %basis.3) | copy-start | bytes 6291460
  13.1 82.2 %collective-permute-start.22 = (bf16[4096,256]{1,0:T(8,128)(2,1)S(1)}, bf16[4096,256]{1,0:T(8,128)(2,1)S(1)}, u32[]{:S(2)}, u32[]{:S(2)}) collective-permute-start(bf16[4096,256]{1,0:T(8,128)(2,1)S(1)} %copy-done.2), channel_id=1, source_target_pairs={{28,32},{60,64},{92,96},{124,128},{156,160},{188,192},{220,224},{3... | collective-permute-start | bytes 6291464 | tf_op jit(solution)/shard_map/ppermute | solution.py:334
  14.1 21.4 %collective-permute-start.7 = (bf16[64,1024]{1,0:T(8,128)(2,1)S(1)}, bf16[64,1024]{1,0:T(8,128)(2,1)S(1)}, u32[]{:S(2)}, u32[]{:S(2)}) collective-permute-start(bf16[64,1024]{1,0:T(8,128)(2,1)S(1)} %copy-done.3), channel_id=1, source_target_pairs={{0,8},{4,12},{8,0},{12,4},{16,24},{20,28},{24,16},{28,20},{32,40},... | collective-permute-start | bytes 393224 | tf_op jit(solution)/shard_map/ppermute | solution.py:334
  15.5 21.5 %collective-permute-start.6 = (bf16[64,1024]{1,0:T(8,128)(2,1)S(1)}, bf16[64,1024]{1,0:T(8,128)(2,1)S(1)}, u32[]{:S(2)}, u32[]{:S(2)}) collective-permute-start(bf16[64,1024]{1,0:T(8,128)(2,1)S(1)} %copy-done.3), channel_id=1, source_target_pairs={{0,4},{4,0},{8,12},{12,8},{16,20},{20,16},{24,28},{28,24},{32,36},... | collective-permute-start | bytes 393224 | tf_op jit(solution)/shard_map/ppermute | solution.py:334
  35.5 2.4 %collective-permute-start.3 = (bf16[192,256]{1,0:T(8,128)(2,1)S(1)}, bf16[192,256]{1,0:T(8,128)(2,1)S(1)}, u32[]{:S(2)}, u32[]{:S(2)}) collective-permute-start(bf16[192,256]{1,0:T(8,128)(2,1)S(1)} %get-tuple-element.35), channel_id=1, source_target_pairs={{0,4},{4,0},{8,12},{12,8},{16,20},{20,16},{24,28},{28,24},{32,36},... | collective-permute-start | bytes 294920 | tf_op jit(solution)/shard_map/ppermute | solution.py:334
  37.0 4.3 %collective-permute-start.4 = (bf16[192,256]{1,0:T(8,128)(2,1)S(1)}, bf16[192,256]{1,0:T(8,128)(2,1)S(1)}, u32[]{:S(2)}, u32[]{:S(2)}) collective-permute-start(bf16[192,256]{1,0:T(8,128)(2,1)S(1)} %get-tuple-element.36), channel_id=1, source_target_pairs={{0,8},{4,12},{8,0},{12,4},{16,24},{20,28},{24,16},{28,20},{32,40},... | collective-permute-start | bytes 294920 | tf_op jit(solution)/shard_map/ppermute | solution.py:334
  37.9 8.6 %collective-permute-start.8 = (bf16[64,1024]{1,0:T(8,128)(2,1)S(1)}, bf16[64,1024]{1,0:T(8,128)(2,1)S(1)}, u32[]{:S(2)}, u32[]{:S(2)}) collective-permute-start(bf16[64,1024]{1,0:T(8,128)(2,1)S(1)} %collective-permute-done.7.g2), channel_id=1, source_target_pairs={{0,4},{4,0},{8,12},{12,8},{16,20},{20,16},{24,28},{28,24},{32,36},... | collective-permute-start | bytes 393224 | tf_op jit(solution)/shard_map/ppermute | solution.py:334
  41.3 12.8 %copy-start.4 = (s32[4,3]{1,0:T(4,128)S(1)}, s32[4,3]{1,0:T(4,128)}, u32[]{:S(2)}) copy-start(s32[4,3]{1,0:T(4,128)} %near_list.13) | copy-start | bytes 148
  41.3 12.8 %copy-start.5 = (s32[4]{0:T(128)S(1)}, s32[4]{0:T(128)}, u32[]{:S(2)}) copy-start(s32[4]{0:T(128)} %near_count.13) | copy-start | bytes 52
  41.3 5.2 %collective-permute-start.5 = (bf16[192,256]{1,0:T(8,128)(2,1)S(1)}, bf16[192,256]{1,0:T(8,128)(2,1)S(1)}, u32[]{:S(2)}, u32[]{:S(2)}) collective-permute-start(bf16[192,256]{1,0:T(8,128)(2,1)S(1)} %get-tuple-element.37), channel_id=1, source_target_pairs={{0,12},{4,8},{8,4},{12,0},{16,28},{20,24},{24,20},{28,16},{32,44},... | collective-permute-start | bytes 294920 | tf_op jit(solution)/shard_map/ppermute | solution.py:334
  46.9 4.4 %collective-permute-start.9 = (bf16[128,256]{1,0:T(8,128)(2,1)S(1)}, bf16[128,256]{1,0:T(8,128)(2,1)S(1)}, u32[]{:S(2)}, u32[]{:S(2)}) collective-permute-start(bf16[128,256]{1,0:T(8,128)(2,1)S(1)} %get-tuple-element.38.own), channel_id=1, source_target_pairs={{0,24},{4,28},{8,16},{12,20},{16,8},{20,12},{24,0},{28,4},{32,56},... | collective-permute-start | bytes 196616 | tf_op jit(solution)/shard_map/ppermute | solution.py:334
  51.3 4.9 %collective-permute-start.10 = (bf16[256,256]{1,0:T(8,128)(2,1)S(1)}, bf16[256,256]{1,0:T(8,128)(2,1)S(1)}, u32[]{:S(2)}, u32[]{:S(2)}) collective-permute-start(bf16[256,256]{1,0:T(8,128)(2,1)S(1)} %constant_dynamic-update-slice_fusion), channel_id=1, source_target_pairs={{0,32},{4,36},{8,40},{12,44},{16,48},{20,52},{24,56},{28,252},{32,... | collective-permute-start | bytes 393224 | tf_op jit(solution)/shard_map/ppermute | solution.py:334
  54.1 5.0 %collective-permute-start.14 = (bf16[256,256]{1,0:T(8,128)(2,1)S(1)}, bf16[256,256]{1,0:T(8,128)(2,1)S(1)}, u32[]{:S(2)}, u32[]{:S(2)}) collective-permute-start(bf16[256,256]{1,0:T(8,128)(2,1)S(1)} %constant_dynamic-update-slice_fusion), channel_id=1, source_target_pairs={{0,224},{4,228},{8,232},{12,236},{16,240},{20,244},{24,248},{28,60... | collective-permute-start | bytes 393224 | tf_op jit(solution)/shard_map/ppermute | solution.py:334
  56.2 5.0 %collective-permute-start.11 = (bf16[256,256]{1,0:T(8,128)(2,1)S(1)}, bf16[256,256]{1,0:T(8,128)(2,1)S(1)}, u32[]{:S(2)}, u32[]{:S(2)}) collective-permute-start(bf16[256,256]{1,0:T(8,128)(2,1)S(1)} %collective-permute-done.10.s1), channel_id=1, source_target_pairs={{0,32},{4,36},{8,40},{12,44},{16,48},{20,52},{24,56},{28,252},{32,... | collective-permute-start | bytes 393224 | tf_op jit(solution)/shard_map/ppermute | solution.py:334
  59.2 8.1 %collective-permute-start.15 = (bf16[256,256]{1,0:T(8,128)(2,1)S(1)}, bf16[256,256]{1,0:T(8,128)(2,1)S(1)}, u32[]{:S(2)}, u32[]{:S(2)}) collective-permute-start(bf16[256,256]{1,0:T(8,128)(2,1)S(1)} %collective-permute-done.14.s2), channel_id=1, source_target_pairs={{0,224},{4,228},{8,232},{12,236},{16,240},{20,244},{24,248},{28,60... | collective-permute-start | bytes 393224 | tf_op jit(solution)/shard_map/ppermute | solution.py:334
  61.3 25.7 %collective-permute-start.23 = (bf16[64,4096]{1,0:T(8,128)(2,1)S(1)}, bf16[64,4096]{1,0:T(8,128)(2,1)S(1)}, u32[]{:S(2)}, u32[]{:S(2)}) collective-permute-start(bf16[64,4096]{1,0:T(8,128)(2,1)S(1)} %get-tuple-element.50.coords), channel_id=1, source_target_pairs={{0,4},{4,0},{8,12},{12,8},{16,20},{20,16},{24,28},{28,24},{32,36},... | collective-permute-start | bytes 1572872 | tf_op jit(solution)/shard_map/ppermute | solution.py:334
  67.2 5.2 %collective-permute-start.12 = (bf16[256,256]{1,0:T(8,128)(2,1)S(1)}, bf16[256,256]{1,0:T(8,128)(2,1)S(1)}, u32[]{:S(2)}, u32[]{:S(2)}) collective-permute-start(bf16[256,256]{1,0:T(8,128)(2,1)S(1)} %collective-permute-done.11.s3), channel_id=1, source_target_pairs={{0,32},{4,36},{8,40},{12,44},{16,48},{20,52},{24,56},{28,252},{32,... | collective-permute-start | bytes 393224 | tf_op jit(solution)/shard_map/ppermute | solution.py:334
  72.5 6.4 %collective-permute-start.16 = (bf16[256,256]{1,0:T(8,128)(2,1)S(1)}, bf16[256,256]{1,0:T(8,128)(2,1)S(1)}, u32[]{:S(2)}, u32[]{:S(2)}) collective-permute-start(bf16[256,256]{1,0:T(8,128)(2,1)S(1)} %collective-permute-done.15.s4), channel_id=1, source_target_pairs={{0,224},{4,228},{8,232},{12,236},{16,240},{20,244},{24,248},{28,60... | collective-permute-start | bytes 393224 | tf_op jit(solution)/shard_map/ppermute | solution.py:334
  78.9 3.8 %collective-permute-start.13 = (bf16[256,256]{1,0:T(8,128)(2,1)S(1)}, bf16[256,256]{1,0:T(8,128)(2,1)S(1)}, u32[]{:S(2)}, u32[]{:S(2)}) collective-permute-start(bf16[256,256]{1,0:T(8,128)(2,1)S(1)} %collective-permute-done.12.s5), channel_id=1, source_target_pairs={{0,32},{4,36},{8,40},{12,44},{16,48},{20,52},{24,56},{28,252},{32,... | collective-permute-start | bytes 393224 | tf_op jit(solution)/shard_map/ppermute | solution.py:334
  82.7 11.6 %collective-permute-start.20 = (bf16[64,4096]{1,0:T(8,128)(2,1)S(1)}, bf16[64,4096]{1,0:T(8,128)(2,1)S(1)}, u32[]{:S(2)}, u32[]{:S(2)}) collective-permute-start(bf16[64,4096]{1,0:T(8,128)(2,1)S(1)} %get-tuple-element.50.coords), channel_id=1, source_target_pairs={{4,8},{12,16},{20,24},{28,32},{36,40},{44,48},{52,56},{60,64},{68,... | collective-permute-start | bytes 1572872 | tf_op jit(solution)/shard_map/ppermute | solution.py:334
  87.0 15.2 %collective-permute-start.17 = (bf16[64,256]{1,0:T(8,128)(2,1)S(1)}, bf16[64,256]{1,0:T(8,128)(2,1)S(1)}, u32[]{:S(2)}, u32[]{:S(2)}) collective-permute-start(bf16[64,256]{1,0:T(8,128)(2,1)S(1)} %get-tuple-element.43), channel_id=1, source_target_pairs={{0,4},{4,0},{8,12},{12,8},{16,20},{20,16},{24,28},{28,24},{32,36},... | collective-permute-start | bytes 98312 | tf_op jit(solution)/shard_map/ppermute | solution.py:334
  87.9 14.4 %collective-permute-start.18 = (bf16[64,256]{1,0:T(8,128)(2,1)S(1)}, bf16[64,256]{1,0:T(8,128)(2,1)S(1)}, u32[]{:S(2)}, u32[]{:S(2)}) collective-permute-start(bf16[64,256]{1,0:T(8,128)(2,1)S(1)} %get-tuple-element.44), channel_id=1, source_target_pairs={{0,8},{4,12},{8,0},{12,4},{16,24},{20,28},{24,16},{28,20},{32,40},... | collective-permute-start | bytes 98312 | tf_op jit(solution)/shard_map/ppermute | solution.py:334
  94.3 8.0 %collective-permute-start.19 = (bf16[64,256]{1,0:T(8,128)(2,1)S(1)}, bf16[64,256]{1,0:T(8,128)(2,1)S(1)}, u32[]{:S(2)}, u32[]{:S(2)}) collective-permute-start(bf16[64,256]{1,0:T(8,128)(2,1)S(1)} %get-tuple-element.45), channel_id=1, source_target_pairs={{0,12},{4,8},{8,4},{12,0},{16,28},{20,24},{24,20},{28,16},{32,44},... | collective-permute-start | bytes 98312 | tf_op jit(solution)/shard_map/ppermute | solution.py:334
